TPU v7x, 256 devices: a whole 4x4x8 slice. The times are simulated.
256 devices in a mesh: seq: 32 (over x, z), tp: 8 (over y, core).
Axes of the slice: x: 4, y: 4, z: 8, core: 2. Of those that a mesh axis runs over, the one named last changes fastest.
Arguments:
- tokens: bfloat16 [16384, 5376], P('seq'), may hold values from -6 to 6
- query_weight: bfloat16 [5376, 2048], P(None, 'tp')
- key_weight: bfloat16 [5376, 1024], P(None, 'tp')
- value_weight: bfloat16 [5376, 1024], P(None, 'tp'), may hold values from -0.078125 to 0.078125
- query_norm_gain: float32 [128], replicated, as said below
- key_norm_gain: float32 [128], replicated, as said below
- adapter_down_weight: bfloat16 [32, 5376, 64], P('seq', 'tp'), may hold values from -0.078125 to 0.078125
- adapter_up_weight: bfloat16 [32, 64, 2048], P('seq', None, 'tp'), may hold values from -0.75 to 0.75
- token_adapter_index: int32 [16384, 1], P('seq'), may hold values from 0 to 31; in each aligned block of 512 rows (0 to 511, 512 to 1023, ...) at most 32 rows name the same one
- packed_prompt_length: int32 [16], replicated, may hold values from 1 to 2048, 16384 in all
Outputs:
- attended: bfloat16 [16384, 2048], P('seq', 'tp')
Inputs may be any that keep to these rules, and one draw needn't show every extreme that they name: `token_adapter_index`: in each aligned block of 512 rows (the rows of one index of seq) no adapter is named by more than 32 rows, a bound that some block reaches. `packed_prompt_length`: they sum to 16384; the largest is exactly 2048. `query_norm_gain`: positive gains. `key_norm_gain`: positive gains.
All inputs are finite; a program needn't handle non-finite values.
Results may differ from a plain program's by a relative error of at most 0.02.
Values may be sent and summed in bfloat16 or wider, within the bound.
No kernel may reach another device: no remote copies, remote signals or barrier semaphores. Data moves between devices by JAX's collectives and lax.ppermute only.
A program may use at most 64 MiB of HBM per device.

v0:
```python
import functools
import jax
import jax.numpy as jnp
from jax import lax
from jax.experimental import pallas as pl
from jax.experimental.pallas import tpu as pltpu
from jax.sharding import Mesh, PartitionSpec as P

WINDOW = 1024
QUERY_SCALE = 0.07715167498104596
X, Z, T = 4, 8, 8
ROWS, WIDTH, HEAD, RANK, CAP = 512, 5376, 128, 64, 32
SLICE = WIDTH // T
PAD = 768
STEP = 768
STEPS = WIDTH // STEP
UP = 256
SLOTS = X * T * CAP
NEAR = (0, 1, Z - 1, 2)


def dot(a, b, ca=1, cb=0):
    return lax.dot_general(a, b, (((ca,), (cb,)), ((), ())), preferred_element_type=jnp.float32)


def pack_kernel(idx_ref, x_ref, out0, out1, out2, out3, target_ref, pick, held, sems):
    copies = [
        pltpu.make_async_copy(x_ref.at[:, pl.ds(j * STEP, STEP)], held.at[j], sems.at[j])
        for j in range(STEPS)
    ]
    for copy in copies:
        copy.start()
    x, t = lax.axis_index("x"), lax.axis_index("tp")
    idx = idx_ref[...]
    named = lax.broadcasted_iota(jnp.int32, (X * T, ROWS), 0) == idx
    earlier = lax.broadcasted_iota(jnp.int32, (ROWS, ROWS), 0) < lax.broadcasted_iota(
        jnp.int32, (ROWS, ROWS), 1
    )
    before = dot(named.astype(jnp.float32).astype(jnp.bfloat16),
                 earlier.astype(jnp.float32).astype(jnp.bfloat16))
    rank = jnp.sum(jnp.where(named, before, 0.0), axis=0, keepdims=True).astype(jnp.int32)
    target = idx * CAP + rank
    target_ref[...] = target
    slot = lax.broadcasted_iota(jnp.int32, (CAP, ROWS), 0)
    for d in range(X):
        adapter = lax.rem(x + d, X) * T + t
        pick[d * CAP:(d + 1) * CAP, :] = (
            (slot + adapter * CAP == target).astype(jnp.float32).astype(jnp.bfloat16)
        )
    for j in range(STEPS):
        copies[j].wait()
        packed = dot(pick[...], held[j]).astype(jnp.bfloat16)
        for d, out in enumerate((out0, out1, out2, out3)):
            out[:, j * STEP:(j + 1) * STEP] = packed[d * CAP:(d + 1) * CAP, :]


def pack(idx, tokens):
    row = jax.ShapeDtypeStruct((CAP, WIDTH), jnp.bfloat16)
    return pl.pallas_call(
        pack_kernel,
        in_specs=[pl.BlockSpec(memory_space=pltpu.VMEM), pl.BlockSpec(memory_space=pl.ANY)],
        out_specs=[pl.BlockSpec(memory_space=pltpu.VMEM)] * (X + 1),
        out_shape=[row] * X + [jax.ShapeDtypeStruct((1, ROWS), jnp.int32)],
        scratch_shapes=[
            pltpu.VMEM((X * CAP, ROWS), jnp.bfloat16),
            pltpu.VMEM((STEPS, ROWS, STEP), jnp.bfloat16),
            pltpu.SemaphoreType.DMA((STEPS,)),
        ],
        cost_estimate=pl.CostEstimate(
            flops=2 * X * CAP * ROWS * WIDTH, bytes_accessed=7_000_000, transcendentals=0
        ),
        name="pack",
    )(idx, tokens)


def unit(field, gain):
    return field / jnp.sqrt(jnp.mean(field * field, axis=-1, keepdims=True) + 1e-06) * gain


def turn(field, cosine, sine):
    return field * cosine + pltpu.roll(field, HEAD // 2, 1) * sine


def project_kernel(
    lens_ref, x_ref, wq_ref, wk_ref, wv_ref, cos_ref, sin_ref, gain_ref, target_ref,
    q_ref, kv_ref, lower_ref, column_ref, x_held, q_held, kv_held, acc, sems,
):
    copies = []
    for j in range(STEPS):
        part = pl.ds(j * STEP, STEP)
        pairs = (
            (x_ref.at[:, part], x_held.at[j]),
            (wk_ref.at[part, :], kv_held.at[j, :, pl.ds(0, HEAD)]),
            (wv_ref.at[part, :], kv_held.at[j, :, pl.ds(HEAD, HEAD)]),
            (wq_ref.at[part, :], q_held.at[j]),
        )
        copies.append([
            pltpu.make_async_copy(source, target, sems.at[j, n])
            for n, (source, target) in enumerate(pairs)
        ])
    for group in copies:
        for copy in group:
            copy.start()
    begin = (lax.axis_index("x") * Z + lax.axis_index("z")) * ROWS
    place = begin + lax.broadcasted_iota(jnp.int32, (ROWS, HEAD), 0)
    start = jnp.zeros((ROWS, HEAD), jnp.int32)
    at = jnp.int32(0)
    for i in range(lens_ref.shape[0]):
        start = jnp.where(place >= at, at, start)
        at = at + lens_ref[i]
    lower_ref[...] = jnp.maximum(start, place - (WINDOW - 1)) - (begin - WINDOW)
    wide = jnp.broadcast_to(target_ref[...].astype(jnp.float32), (HEAD, ROWS))
    column_ref[...] = jnp.transpose(wide).astype(jnp.int32)
    for j in range(STEPS):
        for copy in copies[j]:
            copy.wait()
        q = dot(x_held[j], q_held[j])
        kv = dot(x_held[j], kv_held[j])
        if j == 0:
            q_ref[...] = q
            acc[...] = kv
        else:
            q_ref[...] += q
            acc[...] += kv
    key = turn(unit(acc[:, :HEAD], gain_ref[...]), cos_ref[...], sin_ref[...])
    kv_ref[:, :HEAD] = key.astype(jnp.bfloat16)
    kv_ref[:, HEAD:] = acc[:, HEAD:].astype(jnp.bfloat16)


def project(lens, tokens, wq, wk, wv, cosine, sine, gain, target):
    near, far = pl.BlockSpec(memory_space=pltpu.VMEM), pl.BlockSpec(memory_space=pl.ANY)
    return pl.pallas_call(
        project_kernel,
        in_specs=[pl.BlockSpec(memory_space=pltpu.SMEM)] + [far] * 4 + [near] * 4,
        out_specs=[near] * 4,
        out_shape=[
            jax.ShapeDtypeStruct((ROWS, 2 * HEAD), jnp.float32),
            jax.ShapeDtypeStruct((ROWS, 2 * HEAD), jnp.bfloat16),
            jax.ShapeDtypeStruct((ROWS, HEAD), jnp.int32),
            jax.ShapeDtypeStruct((ROWS, HEAD), jnp.int32),
        ],
        scratch_shapes=[
            pltpu.VMEM((STEPS, ROWS, STEP), jnp.bfloat16),
            pltpu.VMEM((STEPS, STEP, 2 * HEAD), jnp.bfloat16),
            pltpu.VMEM((STEPS, STEP, 2 * HEAD), jnp.bfloat16),
            pltpu.VMEM((ROWS, 2 * HEAD), jnp.float32),
            pltpu.SemaphoreType.DMA((STEPS, 4)),
        ],
        cost_estimate=pl.CostEstimate(
            flops=2 * ROWS * WIDTH * 512, bytes_accessed=12_500_000, transcendentals=0
        ),
        name="project",
    )(lens, tokens, wq, wk, wv, cosine, sine, gain, target)


def adapt_kernel(*refs):
    rows, weights, out, held = refs[:X], refs[X:X + 4], refs[X + 4], refs[X + 5]
    x, z = lax.axis_index("x"), lax.axis_index("z")
    for d in range(4):
        for n in range(2):
            held[lax.rem(z + NEAR[d] + 4 * n, T)] = weights[d][n * RANK:(n + 1) * RANK, :]
    packed = jnp.concatenate([r[...] for r in rows], axis=0)
    low = jnp.zeros((X * CAP, RANK), jnp.float32)
    for w in range(T):
        first = w * SLICE // 128 * 128
        low += dot(packed[:, first:first + PAD], held[w, :, :PAD], 1, 1)
    low = low.astype(jnp.bfloat16)
    for w in range(T):
        delta = dot(low, held[w, :, PAD:]).astype(jnp.bfloat16)
        for d in range(X):
            out[lax.rem(x - d + X, X), w] = delta[d * CAP:(d + 1) * CAP, :]


def adapt(rows, weights):
    return pl.pallas_call(
        adapt_kernel,
        in_specs=[pl.BlockSpec(memory_space=pltpu.VMEM)] * (X + 4),
        out_specs=pl.BlockSpec(memory_space=pltpu.VMEM),
        out_shape=jax.ShapeDtypeStruct((X, T, CAP, UP), jnp.bfloat16),
        scratch_shapes=[
            pltpu.VMEM((T, RANK, PAD + UP), jnp.bfloat16),
        ],
        cost_estimate=pl.CostEstimate(
            flops=2 * 128 * RANK * (WIDTH + 2048), bytes_accessed=3_000_000, transcendentals=0
        ),
        name="adapt",
    )(*rows, *weights)


def attend_kernel(delta_ref, q_ref, kv0, kv1, kv2, cos_ref, sin_ref, gain_ref, lower_ref, column_ref,
                  out_ref):
    half = ROWS // 2
    slot = lax.broadcasted_iota(jnp.int32, (ROWS, HEAD), 1)
    column = column_ref[...]
    chosen = jnp.concatenate(
        [(column == slot + c * HEAD).astype(jnp.float32).astype(jnp.bfloat16)
         for c in range(SLOTS // HEAD)], axis=1)
    query = q_ref[...] + dot(chosen, delta_ref[...])
    turned = [
        (turn(unit(query[:, h * HEAD:(h + 1) * HEAD], gain_ref[...]), cos_ref[...], sin_ref[...])
         ).astype(jnp.bfloat16)
        for h in range(2)
    ]
    for tile in range(2):
        here = slice(tile * half, (tile + 1) * half)
        q = jnp.concatenate([turned[0][here], turned[1][here]], axis=0)
        pieces = ((kv0, tile * half, ROWS), (kv1, 0, ROWS), (kv2, 0, (tile + 1) * half))
        low = lower_ref[here, :1]
        high = WINDOW + tile * half + lax.broadcasted_iota(jnp.int32, (half, 1), 0)
        scores = []
        for n, (ref, a, b) in enumerate(pieces):
            s = dot(q, ref[a:b, :HEAD], 1, 1) * QUERY_SCALE
            at = n * ROWS + a + lax.broadcasted_iota(jnp.int32, (half, b - a), 1)
            allowed = at >= low
            if n == 2:
                allowed = allowed & (at <= high)
            scores.append(jnp.where(jnp.concatenate([allowed, allowed], axis=0), s, -1e30))
        peak = functools.reduce(
            jnp.maximum, [jnp.max(s, axis=-1, keepdims=True) for s in scores])
        weights = [jnp.exp(s - peak) for s in scores]
        total = sum(jnp.sum(w, axis=-1, keepdims=True) for w in weights)
        mixed = sum(
            dot(w.astype(jnp.bfloat16), ref[a:b, HEAD:])
            for w, (ref, a, b) in zip(weights, pieces))
        mixed = (mixed / total).astype(jnp.bfloat16)
        out_ref[here, :HEAD] = mixed[:half]
        out_ref[here, HEAD:] = mixed[half:]


def attend(*args):
    return pl.pallas_call(
        attend_kernel,
        in_specs=[pl.BlockSpec(memory_space=pltpu.VMEM)] * 10,
        out_specs=pl.BlockSpec(memory_space=pltpu.VMEM),
        out_shape=jax.ShapeDtypeStruct((ROWS, 2 * HEAD), jnp.bfloat16),
        cost_estimate=pl.CostEstimate(
            flops=4 * 1024 * 1280 * HEAD, bytes_accessed=4_000_000, transcendentals=1024 * 1280
        ),
        name="attend",
    )(*args)


def layer(
    tokens, query_weight, key_weight, value_weight, query_norm_gain, key_norm_gain,
    adapter_down_weight, adapter_up_weight, token_adapter_index, packed_prompt_length,
):
    x, z, t = lax.axis_index("x"), lax.axis_index("z"), lax.axis_index("tp")
    down = jnp.swapaxes(adapter_down_weight[0], 0, 1)
    shift = lax.rem(t * SLICE, 128)
    down = functools.reduce(
        lambda other, at: jnp.where(
            shift == at, jnp.pad(down, ((0, 0), (at, PAD - SLICE - at))), other),
        (32, 64, 96), jnp.pad(down, ((0, 0), (0, PAD - SLICE))))
    carried = jnp.concatenate([down, adapter_up_weight[0]], axis=1)
    weights = [
        lax.ppermute(
            carried, ("z", "tp"),
            [(a * T + w, (w + d) % Z * T + a) for a in range(Z) for w in range(T)])
        for d in (0, 4)
    ]
    weights = jnp.concatenate(weights, axis=0)
    weights = [weights] + [
        lax.ppermute(
            weights, "z", [((i + d) % Z, i) for i in range(Z)])
        for d in NEAR[1:]
    ]
    *rows, target = pack(token_adapter_index.reshape(1, ROWS), tokens)
    rows = [rows[0]] + [
        lax.ppermute(
            rows[d], "x", [(i, (i + d) % X) for i in range(X)])
        for d in range(1, X)
    ]
    place = ((x * Z + z) * ROWS + jnp.arange(ROWS, dtype=jnp.int32)).astype(jnp.float32)
    half = HEAD // 2
    freq = jnp.exp(
        -(2.0 * jnp.arange(half, dtype=jnp.float32) / HEAD) * jnp.log(jnp.float32(10000.0)))
    angle = place[:, None] * freq[None, :]
    cosine, sine = jnp.cos(angle), jnp.sin(angle)
    cosine = jnp.concatenate([cosine, cosine], axis=1)
    sine = jnp.concatenate([-sine, sine], axis=1)
    query, kv, lower, column = project(
        packed_prompt_length, tokens, query_weight, key_weight, value_weight,
        cosine, sine, key_norm_gain.reshape(1, HEAD), target)
    onward = [(i, i + 1) for i in range(X * Z - 1)]
    kv1 = lax.ppermute(kv, ("x", "z"), onward)
    kv0 = lax.ppermute(kv1, ("x", "z"), onward)
    delta = adapt(rows, weights)
    delta = lax.all_to_all(
        delta.reshape(X * T, CAP, UP), ("x", "tp"), 0, 0)
    return attend(
        delta.reshape(SLOTS, UP), query, kv0, kv1, kv, cosine, sine,
        query_norm_gain.reshape(1, HEAD), lower, column)


def solution(mesh):
    mesh = Mesh(mesh.devices.reshape(X, Z, T), ("x", "z", "tp"))
    seq = ("x", "z")
    in_specs = (
        P(seq, None), P(None, "tp"), P(None, "tp"), P(None, "tp"), P(), P(),
        P(seq, "tp", None), P(seq, None, "tp"), P(seq, None), P(),
    )
    return jax.shard_map(
        layer, mesh=mesh, in_specs=in_specs, out_specs=P(seq, "tp"), check_vma=False)
```

profile of v0, /device:TPU:1, one launch (start us, length us, event | category | flops | bytes accessed | tf_op | source)
XLA Modules:
  0.0 81.1 jit_solution(12831350487706496565)
XLA Ops:
  0.0 1.2 %select_select_fusion = bf16[64,768]{1,0:T(8,128)(2,1)S(1)} fusion(bf16[64,672]{1,0:T(8,128)(2,1)} %bitcast.11, pred[]{:T(512)S(6)} %eq.11, pred[]{:T(512)S(6)} %eq.10, pred[]{:T(512)S(6)} %eq.9), kind=kLoop, calls=%fused_computation.5 | loop fusion | flops 147456 | bytes 184323 | tf_op jit(solution)/shard_map/jit(_where)/select_n | solution.py:251
  1.2 0.8 pad_maximum_fusion.2
  2.0 4.9 %collective-permute-start.3 = (bf16[64,1024]{1,0:T(8,128)(2,1)S(1)}, bf16[64,1024]{1,0:T(8,128)(2,1)S(1)}, u32[]{:S(2)}, u32[]{:S(2)}) collective-permute-start(bf16[64,1024]{1,0:T(8,128)(2,1)S(1)} %pad_maximum_fusion.2), channel_id=1, source_target_pairs={{0,0},{1,8},{2,16},{3,24},{4,32},{5,40},{6,48},{7,56},{8,1},{9,9},... | collective-permute-start | bytes 393224 | tf_op jit(solution)/shard_map/ppermute | solution.py:256
  6.9 5.3 %collective-permute-start.4 = (bf16[64,1024]{1,0:T(8,128)(2,1)S(1)}, bf16[64,1024]{1,0:T(8,128)(2,1)S(1)}, u32[]{:S(2)}, u32[]{:S(2)}) collective-permute-start(bf16[64,1024]{1,0:T(8,128)(2,1)S(1)} %pad_maximum_fusion.2), channel_id=1, source_target_pairs={{0,32},{1,40},{2,48},{3,56},{4,0},{5,8},{6,16},{7,24},{8,33},{9,41... | collective-permute-start | bytes 393224 | tf_op jit(solution)/shard_map/ppermute | solution.py:256
  12.2 5.1 %pack.1 = (bf16[32,5376]{1,0:T(8,128)(2,1)}, bf16[32,5376]{1,0:T(8,128)(2,1)}, bf16[32,5376]{1,0:T(8,128)(2,1)}, bf16[32,5376]{1,0:T(8,128)(2,1)}, s32[1,512]{1,0:T(1,128)}) custom-call(s32[1,512]{1,0:T(1,128)} %bitcast.13, bf16[512,5376]{1,0:T(8,128)(2,1)} %x_ref.3), custom_call_target="tpu_custom_call" | custom-call | flops 704643072 | bytes 7000000 | tf_op jit(solution)/shard_map/pack/pallas_call | solution.py:59
  17.3 1.3 %collective-permute-start = (bf16[32,5376]{1,0:T(8,128)(2,1)}, bf16[32,5376]{1,0:T(8,128)(2,1)S(1)}, u32[]{:S(2)}, u32[]{:S(2)}) collective-permute-start(bf16[32,5376]{1,0:T(8,128)(2,1)} %get-tuple-element.15), channel_id=1, source_target_pairs={{0,64},{64,128},{128,192},{192,0},{1,65},{65,129},{129,193},{193,1... | collective-permute-start | bytes 1032200 | tf_op jit(solution)/shard_map/ppermute | solution.py:269
  18.6 2.4 %collective-permute-start.1 = (bf16[32,5376]{1,0:T(8,128)(2,1)}, bf16[32,5376]{1,0:T(8,128)(2,1)S(1)}, u32[]{:S(2)}, u32[]{:S(2)}) collective-permute-start(bf16[32,5376]{1,0:T(8,128)(2,1)} %get-tuple-element.16), channel_id=1, source_target_pairs={{0,128},{64,192},{128,0},{192,64},{1,129},{65,193},{129,1},{193,65... | collective-permute-start | bytes 1032200 | tf_op jit(solution)/shard_map/ppermute | solution.py:269
  21.0 1.2 %collective-permute-start.2 = (bf16[32,5376]{1,0:T(8,128)(2,1)}, bf16[32,5376]{1,0:T(8,128)(2,1)S(1)}, u32[]{:S(2)}, u32[]{:S(2)}) collective-permute-start(bf16[32,5376]{1,0:T(8,128)(2,1)} %get-tuple-element.17), channel_id=1, source_target_pairs={{0,192},{64,0},{128,64},{192,128},{1,193},{65,1},{129,65},{193,129... | collective-permute-start | bytes 1032200 | tf_op jit(solution)/shard_map/ppermute | solution.py:269
  22.2 1.0 %fusion = (f32[512,64]{1,0:T(8,128)S(1)}, f32[512,64]{1,0:T(8,128)S(1)}, f32[512,64]{1,0:T(8,128)S(1)}) fusion(f32[64]{0:T(128)S(1)} %multiply_exponential_fusion, f32[512]{0:T(512)S(1)} %add_convert_fusion), kind=kLoop, calls=%fused_computation.6 | loop fusion | flops 65536 | bytes 395520 | tf_op jit(solution)/shard_map/neg | solution.py:280
  23.2 1.0 %pad_maximum_fusion = (f32[512,128]{1,0:T(8,128)}, f32[512,128]{1,0:T(8,128)}) fusion(f32[512,64]{1,0:T(8,128)S(1)} %get-tuple-element.25, f32[512,64]{1,0:T(8,128)S(1)} %get-tuple-element.24, f32[512,64]{1,0:T(8,128)S(1)} %get-tuple-element.23), kind=kLoop, calls=%fused_computation.2 | loop fusion | flops 131072 | bytes 917504 | tf_op jit(solution)/shard_map/concatenate | solution.py:279
  24.2 0.0 collective-permute-done.3
  24.2 0.0 collective-permute-done.4
  24.3 0.0 copy-start.1
  24.3 3.3 %collective-permute-start.5 = (bf16[128,1024]{1,0:T(8,128)(2,1)S(1)}, bf16[128,1024]{1,0:T(8,128)(2,1)S(1)}, u32[]{:S(2)}, u32[]{:S(2)}) collective-permute-start(bf16[128,1024]{1,0:T(8,128)(2,1)S(1)} %constant_dynamic-update-slice_fusion.refs_4_), channel_id=1, source_target_pairs={{8,0},{16,8},{24,16},{32,24},{40,32},{48,40},{56,48},{0,56},{9,1},... | collective-permute-start | bytes 786440 | tf_op jit(solution)/shard_map/ppermute | solution.py:263
  27.5 0.0 collective-permute-start.6
  27.6 0.0 collective-permute-done.refs_1_
  27.6 2.0 %collective-permute-start.7 = (bf16[128,1024]{1,0:T(8,128)(2,1)S(1)}, bf16[128,1024]{1,0:T(8,128)(2,1)S(1)}, u32[]{:S(2)}, u32[]{:S(2)}) collective-permute-start(bf16[128,1024]{1,0:T(8,128)(2,1)S(1)} %constant_dynamic-update-slice_fusion.refs_4_), channel_id=1, source_target_pairs={{16,0},{24,8},{32,16},{40,24},{48,32},{56,40},{0,48},{8,56},{17,1}... | collective-permute-start | bytes 786440 | tf_op jit(solution)/shard_map/ppermute | solution.py:263
  29.6 7.4 %project.1 = (f32[512,256]{1,0:T(8,128)}, bf16[512,256]{1,0:T(8,128)(2,1)}, s32[512,128]{1,0:T(8,128)}, s32[512,128]{1,0:T(8,128)}) custom-call(s32[16]{0:T(128)} %lens_ref.1, bf16[512,5376]{1,0:T(8,128)(2,1)} %x_ref.3, bf16[5376,256]{1,0:T(8,128)(2,1)} %wq_ref.1, bf16[5376,128]{1,0:T(8,128)(2,1)} %wk_ref.1, bf16[5376,128]{1,0:T(8,128)(2,1)} %wv_ref.1, ...), custom_call_target="tpu_custom_call" | custom-call | flops 2818572288 | bytes 12500000 | tf_op jit(solution)/shard_map/project/pallas_call | solution.py:132
  37.0 0.0 collective-permute-done.1.refs_2_
  37.0 3.9 %collective-permute-start.8 = (bf16[512,256]{1,0:T(8,128)(2,1)}, bf16[512,256]{1,0:T(8,128)(2,1)S(1)}, u32[]{:S(2)}, u32[]{:S(2)}) collective-permute-start(bf16[512,256]{1,0:T(8,128)(2,1)} %get-tuple-element.20.kv2), channel_id=1, source_target_pairs={{0,8},{8,16},{16,24},{24,32},{32,40},{40,48},{48,56},{56,64},{64,7... | collective-permute-start | bytes 786440 | tf_op jit(solution)/shard_map/ppermute | solution.py:285
  40.9 0.0 collective-permute-done.2.refs_3_
  40.9 0.0 collective-permute-done.6.refs_6_
  41.0 3.6 %collective-permute-done.7.refs_7_ = bf16[128,1024]{1,0:T(8,128)(2,1)S(1)} collective-permute-done((bf16[128,1024]{1,0:T(8,128)(2,1)S(1)}, bf16[128,1024]{1,0:T(8,128)(2,1)S(1)}, u32[]{:S(2)}, u32[]{:S(2)}) %collective-permute-start.7) | collective-permute-done | bytes 262176 | tf_op jit(solution)/shard_map/ppermute | solution.py:263
  44.6 0.7 copy-done.7
  45.2 3.5 %adapt.1 = bf16[4,8,32,256]{3,2,1,0:T(8,128)(2,1)} custom-call(bf16[32,5376]{1,0:T(8,128)(2,1)} %get-tuple-element.14.refs_0_, bf16[32,5376]{1,0:T(8,128)(2,1)} %copy-done.2, bf16[32,5376]{1,0:T(8,128)(2,1)} %copy-done.3, bf16[32,5376]{1,0:T(8,128)(2,1)} %copy-done.4, bf16[128,1024]{1,0:T(8,128)(2,1)} %copy-done.1, bf16[128,1024]{1,0:T(8,128)(2,1)} %copy-done.5, ...), custom_call_target="tpu_custom_call" | custom-call | flops 121634816 | bytes 3000000 | tf_op jit(solution)/shard_map/adapt/pallas_call | solution.py:175
  48.8 7.1 %all-to-all-start = ((bf16[32,32,256]{2,1,0:T(8,128)(2,1)}), bf16[32,32,256]{2,1,0:T(8,128)(2,1)S(1)}, u32[]{:S(2)}, u32[]{:S(2)}) async-start(bf16[32,32,256]{2,1,0:T(8,128)(2,1)} %bitcast.10), calls=%async_computation | async-start | bytes 1048576 | tf_op jit(solution)/shard_map/all_to_all | solution.py:288
  55.9 0.0 collective-permute-done.8.kv1
  55.9 2.0 %collective-permute-start.9 = (bf16[512,256]{1,0:T(8,128)(2,1)S(1)}, bf16[512,256]{1,0:T(8,128)(2,1)S(1)}, u32[]{:S(2)}, u32[]{:S(2)}) collective-permute-start(bf16[512,256]{1,0:T(8,128)(2,1)S(1)} %collective-permute-done.8.kv1), channel_id=1, source_target_pairs={{0,8},{8,16},{16,24},{24,32},{32,40},{40,48},{48,56},{56,64},{64,7... | collective-permute-start | bytes 786440 | tf_op jit(solution)/shard_map/ppermute | solution.py:286
  57.9 5.2 %collective-permute-done.9.kv0 = bf16[512,256]{1,0:T(8,128)(2,1)S(1)} collective-permute-done((bf16[512,256]{1,0:T(8,128)(2,1)S(1)}, bf16[512,256]{1,0:T(8,128)(2,1)S(1)}, u32[]{:S(2)}, u32[]{:S(2)}) %collective-permute-start.9) | collective-permute-done | bytes 262176 | tf_op jit(solution)/shard_map/ppermute | solution.py:286
  63.1 10.0 %all-to-all-done = bf16[32,32,256]{2,1,0:T(8,128)(2,1)S(1)} async-done(((bf16[32,32,256]{2,1,0:T(8,128)(2,1)}), bf16[32,32,256]{2,1,0:T(8,128)(2,1)S(1)}, u32[]{:S(2)}, u32[]{:S(2)}) %all-to-all-start) | async-done | bytes 524320 | tf_op jit(solution)/shard_map/all_to_all | solution.py:288
  73.1 0.8 copy-done
  73.9 7.2 %attend.1 = bf16[512,256]{1,0:T(8,128)(2,1)} custom-call(bf16[1024,256]{1,0:T(8,128)(2,1)} %bitcast.9, f32[512,256]{1,0:T(8,128)} %get-tuple-element.19.q_ref, bf16[512,256]{1,0:T(8,128)(2,1)} %copy-done.9, bf16[512,256]{1,0:T(8,128)(2,1)} %copy-done.8, bf16[512,256]{1,0:T(8,128)(2,1)} %get-tuple-element.20.kv2, f32[512,128]{1,0:T(8,128)} %get-tuple-element.26.cos_ref, ...), custom_call_target="tpu_custom_call" | custom-call | flops 671088640 | bytes 4000000 | tf_op jit(solution)/shard_map/attend/pallas_call | solution.py:231
  (22 shorter events, 0.1 us)
Async XLA Ops:
  2.0 22.2 %collective-permute-start.3 = (bf16[64,1024]{1,0:T(8,128)(2,1)S(1)}, bf16[64,1024]{1,0:T(8,128)(2,1)S(1)}, u32[]{:S(2)}, u32[]{:S(2)}) collective-permute-start(bf16[64,1024]{1,0:T(8,128)(2,1)S(1)} %pad_maximum_fusion.2), channel_id=1, source_target_pairs={{0,0},{1,8},{2,16},{3,24},{4,32},{5,40},{6,48},{7,56},{8,1},{9,9},... | collective-permute-start | bytes 393224 | tf_op jit(solution)/shard_map/ppermute | solution.py:256
  6.9 17.3 %collective-permute-start.4 = (bf16[64,1024]{1,0:T(8,128)(2,1)S(1)}, bf16[64,1024]{1,0:T(8,128)(2,1)S(1)}, u32[]{:S(2)}, u32[]{:S(2)}) collective-permute-start(bf16[64,1024]{1,0:T(8,128)(2,1)S(1)} %pad_maximum_fusion.2), channel_id=1, source_target_pairs={{0,32},{1,40},{2,48},{3,56},{4,0},{5,8},{6,16},{7,24},{8,33},{9,41... | collective-permute-start | bytes 393224 | tf_op jit(solution)/shard_map/ppermute | solution.py:256
  17.3 10.3 %collective-permute-start = (bf16[32,5376]{1,0:T(8,128)(2,1)}, bf16[32,5376]{1,0:T(8,128)(2,1)S(1)}, u32[]{:S(2)}, u32[]{:S(2)}) collective-permute-start(bf16[32,5376]{1,0:T(8,128)(2,1)} %get-tuple-element.15), channel_id=1, source_target_pairs={{0,64},{64,128},{128,192},{192,0},{1,65},{65,129},{129,193},{193,1... | collective-permute-start | bytes 1032200 | tf_op jit(solution)/shard_map/ppermute | solution.py:269
  18.6 18.4 %collective-permute-start.1 = (bf16[32,5376]{1,0:T(8,128)(2,1)}, bf16[32,5376]{1,0:T(8,128)(2,1)S(1)}, u32[]{:S(2)}, u32[]{:S(2)}) collective-permute-start(bf16[32,5376]{1,0:T(8,128)(2,1)} %get-tuple-element.16), channel_id=1, source_target_pairs={{0,128},{64,192},{128,0},{192,64},{1,129},{65,193},{129,1},{193,65... | collective-permute-start | bytes 1032200 | tf_op jit(solution)/shard_map/ppermute | solution.py:269
  21.0 19.9 %collective-permute-start.2 = (bf16[32,5376]{1,0:T(8,128)(2,1)}, bf16[32,5376]{1,0:T(8,128)(2,1)S(1)}, u32[]{:S(2)}, u32[]{:S(2)}) collective-permute-start(bf16[32,5376]{1,0:T(8,128)(2,1)} %get-tuple-element.17), channel_id=1, source_target_pairs={{0,192},{64,0},{128,64},{192,128},{1,193},{65,1},{129,65},{193,129... | collective-permute-start | bytes 1032200 | tf_op jit(solution)/shard_map/ppermute | solution.py:269
  24.3 12.7 %copy-start.1 = (bf16[128,1024]{1,0:T(8,128)(2,1)}, bf16[128,1024]{1,0:T(8,128)(2,1)S(1)}, u32[]{:S(2)}) copy-start(bf16[128,1024]{1,0:T(8,128)(2,1)S(1)} %constant_dynamic-update-slice_fusion.refs_4_) | copy-start | bytes 786436
  24.3 16.6 %collective-permute-start.5 = (bf16[128,1024]{1,0:T(8,128)(2,1)S(1)}, bf16[128,1024]{1,0:T(8,128)(2,1)S(1)}, u32[]{:S(2)}, u32[]{:S(2)}) collective-permute-start(bf16[128,1024]{1,0:T(8,128)(2,1)S(1)} %constant_dynamic-update-slice_fusion.refs_4_), channel_id=1, source_target_pairs={{8,0},{16,8},{24,16},{32,24},{40,32},{48,40},{56,48},{0,56},{9,1},... | collective-permute-start | bytes 786440 | tf_op jit(solution)/shard_map/ppermute | solution.py:263
  27.5 13.4 %collective-permute-start.6 = (bf16[128,1024]{1,0:T(8,128)(2,1)S(1)}, bf16[128,1024]{1,0:T(8,128)(2,1)S(1)}, u32[]{:S(2)}, u32[]{:S(2)}) collective-permute-start(bf16[128,1024]{1,0:T(8,128)(2,1)S(1)} %constant_dynamic-update-slice_fusion.refs_4_), channel_id=1, source_target_pairs={{56,0},{0,8},{8,16},{16,24},{24,32},{32,40},{40,48},{48,56},{57,1}... | collective-permute-start | bytes 786440 | tf_op jit(solution)/shard_map/ppermute | solution.py:263
  27.6 9.4 %copy-start.2 = (bf16[32,5376]{1,0:T(8,128)(2,1)}, bf16[32,5376]{1,0:T(8,128)(2,1)S(1)}, u32[]{:S(2)}) copy-start(bf16[32,5376]{1,0:T(8,128)(2,1)S(1)} %collective-permute-done.refs_1_) | copy-start | bytes 1032196
  27.6 17.0 %collective-permute-start.7 = (bf16[128,1024]{1,0:T(8,128)(2,1)S(1)}, bf16[128,1024]{1,0:T(8,128)(2,1)S(1)}, u32[]{:S(2)}, u32[]{:S(2)}) collective-permute-start(bf16[128,1024]{1,0:T(8,128)(2,1)S(1)} %constant_dynamic-update-slice_fusion.refs_4_), channel_id=1, source_target_pairs={{16,0},{24,8},{32,16},{40,24},{48,32},{56,40},{0,48},{8,56},{17,1}... | collective-permute-start | bytes 786440 | tf_op jit(solution)/shard_map/ppermute | solution.py:263
  37.0 7.5 %copy-start.3 = (bf16[32,5376]{1,0:T(8,128)(2,1)}, bf16[32,5376]{1,0:T(8,128)(2,1)S(1)}, u32[]{:S(2)}) copy-start(bf16[32,5376]{1,0:T(8,128)(2,1)S(1)} %collective-permute-done.1.refs_2_) | copy-start | bytes 1032196
  37.0 18.9 %collective-permute-start.8 = (bf16[512,256]{1,0:T(8,128)(2,1)}, bf16[512,256]{1,0:T(8,128)(2,1)S(1)}, u32[]{:S(2)}, u32[]{:S(2)}) collective-permute-start(bf16[512,256]{1,0:T(8,128)(2,1)} %get-tuple-element.20.kv2), channel_id=1, source_target_pairs={{0,8},{8,16},{16,24},{24,32},{32,40},{40,48},{48,56},{56,64},{64,7... | collective-permute-start | bytes 786440 | tf_op jit(solution)/shard_map/ppermute | solution.py:285
  40.9 3.6 %copy-start.4 = (bf16[32,5376]{1,0:T(8,128)(2,1)}, bf16[32,5376]{1,0:T(8,128)(2,1)S(1)}, u32[]{:S(2)}) copy-start(bf16[32,5376]{1,0:T(8,128)(2,1)S(1)} %collective-permute-done.2.refs_3_) | copy-start | bytes 1032196
  40.9 3.6 %copy-start.5 = (bf16[128,1024]{1,0:T(8,128)(2,1)}, bf16[128,1024]{1,0:T(8,128)(2,1)S(1)}, u32[]{:S(2)}) copy-start(bf16[128,1024]{1,0:T(8,128)(2,1)S(1)} %collective-permute-done.5.refs_5_) | copy-start | bytes 786436
  40.9 3.6 %copy-start.6 = (bf16[128,1024]{1,0:T(8,128)(2,1)}, bf16[128,1024]{1,0:T(8,128)(2,1)S(1)}, u32[]{:S(2)}) copy-start(bf16[128,1024]{1,0:T(8,128)(2,1)S(1)} %collective-permute-done.6.refs_6_) | copy-start | bytes 786436
  44.5 0.7 copy-start.7
  48.8 24.3 %all-to-all-start = ((bf16[32,32,256]{2,1,0:T(8,128)(2,1)}), bf16[32,32,256]{2,1,0:T(8,128)(2,1)S(1)}, u32[]{:S(2)}, u32[]{:S(2)}) async-start(bf16[32,32,256]{2,1,0:T(8,128)(2,1)} %bitcast.10), calls=%async_computation | async-start | bytes 1048576 | tf_op jit(solution)/shard_map/all_to_all | solution.py:288
  55.9 17.2 %copy-start.8 = (bf16[512,256]{1,0:T(8,128)(2,1)}, bf16[512,256]{1,0:T(8,128)(2,1)S(1)}, u32[]{:S(2)}) copy-start(bf16[512,256]{1,0:T(8,128)(2,1)S(1)} %collective-permute-done.8.kv1) | copy-start | bytes 786436
  55.9 7.2 %collective-permute-start.9 = (bf16[512,256]{1,0:T(8,128)(2,1)S(1)}, bf16[512,256]{1,0:T(8,128)(2,1)S(1)}, u32[]{:S(2)}, u32[]{:S(2)}) collective-permute-start(bf16[512,256]{1,0:T(8,128)(2,1)S(1)} %collective-permute-done.8.kv1), channel_id=1, source_target_pairs={{0,8},{8,16},{16,24},{24,32},{32,40},{40,48},{48,56},{56,64},{64,7... | collective-permute-start | bytes 786440 | tf_op jit(solution)/shard_map/ppermute | solution.py:286
  63.1 10.0 %copy-start.9 = (bf16[512,256]{1,0:T(8,128)(2,1)}, bf16[512,256]{1,0:T(8,128)(2,1)S(1)}, u32[]{:S(2)}) copy-start(bf16[512,256]{1,0:T(8,128)(2,1)S(1)} %collective-permute-done.9.kv0) | copy-start | bytes 786436
  73.1 0.8 copy-start
where the time goes:
time: 81.6 us; the launch traced here: 81.1 us
  starting transfers between devices  33.3 us (41%)
  Pallas kernels  23.2 us (28%)
  waiting for transfers between devices  18.8 us (23%)
  other arithmetic  4.03 us (5%)
  local copies, waits for them, and re-layouts  1.53 us (2%)
    ppermute x2, starting transfers between devices, layer(): lax.ppermute(carried, ('z', 'tp'), [(a * T + w, (w + d) % Z * T + a) for...  10.2 us
    all_to_all x1, waiting for transfers between devices, layer(): delta = lax.all_to_all(delta.reshape(X * T, CAP, UP), ('x', 'tp'), 0, 0)  10 us
    pallas_call x1, Pallas kernels, project(): pl.pallas_call(project_kernel, in_specs=[pl.BlockSpec(memory_space=pltpu....  7.4 us
    pallas_call x1, Pallas kernels, attend(): pl.pallas_call(attend_kernel, in_specs=[pl.BlockSpec(memory_space=pltpu.V...  7.2 us
    all_to_all x1, starting transfers between devices, layer(): delta = lax.all_to_all(delta.reshape(X * T, CAP, UP), ('x', 'tp'), 0, 0)  7.11 us
    ppermute x3, starting transfers between devices, layer(): lax.ppermute(weights, 'z', [((i + d) % Z, i) for i in range(Z)])  5.29 us
    ppermute x1, waiting for transfers between devices, layer(): kv0 = lax.ppermute(kv1, ('x', 'z'), onward)  5.22 us
    pallas_call x1, Pallas kernels, pack(): pl.pallas_call(pack_kernel, in_specs=[pl.BlockSpec(memory_space=pltpu.VME...  5.08 us
  transfers between devices with their start and end apart: 11, of which 3 were waited for; matrix products, arithmetic and copies ran while one was open for 3% of the time, Pallas kernels for 20%

commit v1 on v0

--- a/solution.py
+++ b/solution.py
@@ -8,6 +8,7 @@
 
 WINDOW = 1024
 QUERY_SCALE = 0.07715167498104596
+LOG2E = 1.4426950408889634
 X, Z, T = 4, 8, 8
 ROWS, WIDTH, HEAD, RANK, CAP = 512, 5376, 128, 64, 32
 SLICE = WIDTH // T
@@ -82,8 +83,8 @@
 
 
 def project_kernel(
-    lens_ref, x_ref, wq_ref, wk_ref, wv_ref, cos_ref, sin_ref, gain_ref, target_ref,
-    q_ref, kv_ref, lower_ref, column_ref, x_held, q_held, kv_held, acc, sems,
+    lens_ref, x_ref, wq_ref, wk_ref, wv_ref, gain_ref, target_ref,
+    q_ref, kv_ref, lower_ref, column_ref, cos_ref, sin_ref, x_held, q_held, kv_held, acc, sems,
 ):
     copies = []
     for j in range(STEPS):
@@ -111,6 +112,12 @@
     lower_ref[...] = jnp.maximum(start, place - (WINDOW - 1)) - (begin - WINDOW)
     wide = jnp.broadcast_to(target_ref[...].astype(jnp.float32), (HEAD, ROWS))
     column_ref[...] = jnp.transpose(wide).astype(jnp.int32)
+    lane = lax.broadcasted_iota(jnp.int32, (ROWS, HEAD), 1)
+    pair = jnp.bitwise_and(lane, HEAD // 2 - 1).astype(jnp.float32)
+    angle = place.astype(jnp.float32) * jnp.exp(-(2.0 * pair / HEAD) * jnp.log(jnp.float32(10000.0)))
+    cos_ref[...] = jnp.cos(angle)
+    sine = jnp.sin(angle)
+    sin_ref[...] = jnp.where(lane < HEAD // 2, -sine, sine)
     for j in range(STEPS):
         for copy in copies[j]:
             copy.wait()
@@ -127,17 +134,19 @@
     kv_ref[:, HEAD:] = acc[:, HEAD:].astype(jnp.bfloat16)
 
 
-def project(lens, tokens, wq, wk, wv, cosine, sine, gain, target):
+def project(lens, tokens, wq, wk, wv, gain, target):
     near, far = pl.BlockSpec(memory_space=pltpu.VMEM), pl.BlockSpec(memory_space=pl.ANY)
     return pl.pallas_call(
         project_kernel,
-        in_specs=[pl.BlockSpec(memory_space=pltpu.SMEM)] + [far] * 4 + [near] * 4,
-        out_specs=[near] * 4,
+        in_specs=[pl.BlockSpec(memory_space=pltpu.SMEM)] + [far] * 4 + [near] * 2,
+        out_specs=[near] * 6,
         out_shape=[
             jax.ShapeDtypeStruct((ROWS, 2 * HEAD), jnp.float32),
             jax.ShapeDtypeStruct((ROWS, 2 * HEAD), jnp.bfloat16),
             jax.ShapeDtypeStruct((ROWS, HEAD), jnp.int32),
             jax.ShapeDtypeStruct((ROWS, HEAD), jnp.int32),
+            jax.ShapeDtypeStruct((ROWS, HEAD), jnp.float32),
+            jax.ShapeDtypeStruct((ROWS, HEAD), jnp.float32),
         ],
         scratch_shapes=[
             pltpu.VMEM((STEPS, ROWS, STEP), jnp.bfloat16),
@@ -150,16 +159,26 @@
             flops=2 * ROWS * WIDTH * 512, bytes_accessed=12_500_000, transcendentals=0
         ),
         name="project",
-    )(lens, tokens, wq, wk, wv, cosine, sine, gain, target)
+    )(lens, tokens, wq, wk, wv, gain, target)
 
 
 def adapt_kernel(*refs):
-    rows, weights, out, held = refs[:X], refs[X:X + 4], refs[X + 4], refs[X + 5]
+    rows, weights, out = refs[:X], refs[X:X + 4], refs[X + 4]
+    packed, held, sems = refs[X + 5:]
     x, z = lax.axis_index("x"), lax.axis_index("z")
-    for d in range(4):
-        for n in range(2):
-            held[lax.rem(z + NEAR[d] + 4 * n, T)] = weights[d][n * RANK:(n + 1) * RANK, :]
-    packed = jnp.concatenate([r[...] for r in rows], axis=0)
+    copies = [
+        pltpu.make_async_copy(
+            weights[d].at[pl.ds(n * RANK, RANK), :],
+            held.at[lax.rem(z + NEAR[d] + 4 * n, T)], sems.at[X + 2 * d + n])
+        for d in range(4) for n in range(2)
+    ] + [
+        pltpu.make_async_copy(rows[d], packed.at[pl.ds(d * CAP, CAP), :], sems.at[d])
+        for d in range(X)
+    ]
+    for copy in copies:
+        copy.start()
+    for copy in copies:
+        copy.wait()
     low = jnp.zeros((X * CAP, RANK), jnp.float32)
     for w in range(T):
         first = w * SLICE // 128 * 128
@@ -174,12 +193,15 @@
 def adapt(rows, weights):
     return pl.pallas_call(
         adapt_kernel,
-        in_specs=[pl.BlockSpec(memory_space=pltpu.VMEM)] * (X + 4),
+        in_specs=[pl.BlockSpec(memory_space=pl.ANY)] * (X + 4),
         out_specs=pl.BlockSpec(memory_space=pltpu.VMEM),
         out_shape=jax.ShapeDtypeStruct((X, T, CAP, UP), jnp.bfloat16),
         scratch_shapes=[
+            pltpu.VMEM((X * CAP, WIDTH), jnp.bfloat16),
             pltpu.VMEM((T, RANK, PAD + UP), jnp.bfloat16),
-        ],
+            pltpu.SemaphoreType.DMA((X + T,)),
+        ],
+        compiler_params=pltpu.CompilerParams(vmem_limit_bytes=12 << 20),
         cost_estimate=pl.CostEstimate(
             flops=2 * 128 * RANK * (WIDTH + 2048), bytes_accessed=3_000_000, transcendentals=0
         ),
@@ -187,52 +209,79 @@
     )(*rows, *weights)
 
 
-def attend_kernel(delta_ref, q_ref, kv0, kv1, kv2, cos_ref, sin_ref, gain_ref, lower_ref, column_ref,
-                  out_ref):
+def attend_kernel(delta_hbm, column_hbm, q_hbm, cos_hbm, sin_hbm, lower_hbm, kv0_hbm, kv1_hbm, kv2_hbm,
+                  gain_ref, out_ref, delta_ref, column_ref, q_ref, cos_ref, sin_ref, lower_ref,
+                  kv_ref, sems):
     half = ROWS // 2
+    pairs = [
+        (column_hbm, column_ref), (delta_hbm, delta_ref), (q_hbm, q_ref), (cos_hbm, cos_ref),
+        (sin_hbm, sin_ref), (lower_hbm, lower_ref),
+    ] + [
+        (source.at[:, pl.ds(n * HEAD, HEAD)], kv_ref.at[pl.ds(b * ROWS, ROWS), pl.ds(n * HEAD, HEAD)])
+        for b, source in enumerate((kv0_hbm, kv1_hbm, kv2_hbm)) for n in range(2)
+    ]
+    copies = [
+        pltpu.make_async_copy(source, target, sems.at[n])
+        for n, (source, target) in enumerate(pairs)
+    ]
+    for copy in copies:
+        copy.start()
+    kv_ref[:, 2 * HEAD:] = jnp.ones((3 * ROWS, HEAD), jnp.bfloat16)
     slot = lax.broadcasted_iota(jnp.int32, (ROWS, HEAD), 1)
+    copies[0].wait()
     column = column_ref[...]
     chosen = jnp.concatenate(
         [(column == slot + c * HEAD).astype(jnp.float32).astype(jnp.bfloat16)
          for c in range(SLOTS // HEAD)], axis=1)
-    query = q_ref[...] + dot(chosen, delta_ref[...])
+    copies[1].wait()
+    delta = dot(chosen, delta_ref[...])
+    for copy in copies[2:5]:
+        copy.wait()
+    query = q_ref[...] + delta
+    gain = gain_ref[...] * (QUERY_SCALE * LOG2E)
     turned = [
-        (turn(unit(query[:, h * HEAD:(h + 1) * HEAD], gain_ref[...]), cos_ref[...], sin_ref[...])
-         ).astype(jnp.bfloat16)
+        turn(unit(query[:, h * HEAD:(h + 1) * HEAD], gain), cos_ref[...], sin_ref[...]
+             ).astype(jnp.bfloat16)
         for h in range(2)
     ]
+    for copy in copies[5:]:
+        copy.wait()
     for tile in range(2):
         here = slice(tile * half, (tile + 1) * half)
+        first, past = tile * half, tile * half + WINDOW + half
         q = jnp.concatenate([turned[0][here], turned[1][here]], axis=0)
-        pieces = ((kv0, tile * half, ROWS), (kv1, 0, ROWS), (kv2, 0, (tile + 1) * half))
-        low = lower_ref[here, :1]
-        high = WINDOW + tile * half + lax.broadcasted_iota(jnp.int32, (half, 1), 0)
-        scores = []
-        for n, (ref, a, b) in enumerate(pieces):
-            s = dot(q, ref[a:b, :HEAD], 1, 1) * QUERY_SCALE
-            at = n * ROWS + a + lax.broadcasted_iota(jnp.int32, (half, b - a), 1)
-            allowed = at >= low
-            if n == 2:
-                allowed = allowed & (at <= high)
-            scores.append(jnp.where(jnp.concatenate([allowed, allowed], axis=0), s, -1e30))
-        peak = functools.reduce(
-            jnp.maximum, [jnp.max(s, axis=-1, keepdims=True) for s in scores])
-        weights = [jnp.exp(s - peak) for s in scores]
-        total = sum(jnp.sum(w, axis=-1, keepdims=True) for w in weights)
-        mixed = sum(
-            dot(w.astype(jnp.bfloat16), ref[a:b, HEAD:])
-            for w, (ref, a, b) in zip(weights, pieces))
-        mixed = (mixed / total).astype(jnp.bfloat16)
+        s = dot(q, kv_ref[first:past, :HEAD], 1, 1)
+        low = lower_ref[here, :1] - first
+        at = lax.broadcasted_iota(jnp.int32, (half, WINDOW + half), 1)
+        high = WINDOW + lax.broadcasted_iota(jnp.int32, (half, 1), 0)
+        allowed = (at >= low) & (at <= high)
+        s = jnp.where(jnp.concatenate([allowed, allowed], axis=0), s, -1e30)
+        peak = jnp.max(s, axis=-1, keepdims=True)
+        weights = jnp.exp2(s - peak).astype(jnp.bfloat16)
+        mixed = dot(weights, kv_ref[first:past, HEAD:])
+        mixed = (mixed[:, :HEAD] / mixed[:, HEAD:]).astype(jnp.bfloat16)
         out_ref[here, :HEAD] = mixed[:half]
         out_ref[here, HEAD:] = mixed[half:]
 
 
 def attend(*args):
+    near, far = pl.BlockSpec(memory_space=pltpu.VMEM), pl.BlockSpec(memory_space=pl.ANY)
     return pl.pallas_call(
         attend_kernel,
-        in_specs=[pl.BlockSpec(memory_space=pltpu.VMEM)] * 10,
-        out_specs=pl.BlockSpec(memory_space=pltpu.VMEM),
+        in_specs=[far] * 9 + [near],
+        out_specs=near,
         out_shape=jax.ShapeDtypeStruct((ROWS, 2 * HEAD), jnp.bfloat16),
+        scratch_shapes=[
+            pltpu.VMEM((SLOTS, UP), jnp.bfloat16),
+            pltpu.VMEM((ROWS, HEAD), jnp.int32),
+            pltpu.VMEM((ROWS, 2 * HEAD), jnp.float32),
+            pltpu.VMEM((ROWS, HEAD), jnp.float32),
+            pltpu.VMEM((ROWS, HEAD), jnp.float32),
+            pltpu.VMEM((ROWS, HEAD), jnp.int32),
+            pltpu.VMEM((3 * ROWS, 3 * HEAD), jnp.bfloat16),
+            pltpu.SemaphoreType.DMA((12,)),
+        ],
+        compiler_params=pltpu.CompilerParams(vmem_limit_bytes=24 << 20),
         cost_estimate=pl.CostEstimate(
             flops=4 * 1024 * 1280 * HEAD, bytes_accessed=4_000_000, transcendentals=1024 * 1280
         ),
@@ -244,14 +293,16 @@
     tokens, query_weight, key_weight, value_weight, query_norm_gain, key_norm_gain,
     adapter_down_weight, adapter_up_weight, token_adapter_index, packed_prompt_length,
 ):
-    x, z, t = lax.axis_index("x"), lax.axis_index("z"), lax.axis_index("tp")
+    t = lax.axis_index("tp")
     down = jnp.swapaxes(adapter_down_weight[0], 0, 1)
     shift = lax.rem(t * SLICE, 128)
-    down = functools.reduce(
+    carried = functools.reduce(
         lambda other, at: jnp.where(
-            shift == at, jnp.pad(down, ((0, 0), (at, PAD - SLICE - at))), other),
-        (32, 64, 96), jnp.pad(down, ((0, 0), (0, PAD - SLICE))))
-    carried = jnp.concatenate([down, adapter_up_weight[0]], axis=1)
+            shift == at, jnp.pad(down, ((0, 0), (at, PAD + UP - SLICE - at))), other),
+        (32, 64, 96), jnp.pad(down, ((0, 0), (0, PAD + UP - SLICE))))
+    carried = jnp.where(
+        jnp.arange(PAD + UP)[None, :] < PAD, carried,
+        jnp.pad(adapter_up_weight[0], ((0, 0), (PAD, 0))))
     weights = [
         lax.ppermute(
             carried, ("z", "tp"),
@@ -270,26 +321,20 @@
             rows[d], "x", [(i, (i + d) % X) for i in range(X)])
         for d in range(1, X)
     ]
-    place = ((x * Z + z) * ROWS + jnp.arange(ROWS, dtype=jnp.int32)).astype(jnp.float32)
-    half = HEAD // 2
-    freq = jnp.exp(
-        -(2.0 * jnp.arange(half, dtype=jnp.float32) / HEAD) * jnp.log(jnp.float32(10000.0)))
-    angle = place[:, None] * freq[None, :]
-    cosine, sine = jnp.cos(angle), jnp.sin(angle)
-    cosine = jnp.concatenate([cosine, cosine], axis=1)
-    sine = jnp.concatenate([-sine, sine], axis=1)
-    query, kv, lower, column = project(
+    query, kv, lower, column, cosine, sine = project(
         packed_prompt_length, tokens, query_weight, key_weight, value_weight,
-        cosine, sine, key_norm_gain.reshape(1, HEAD), target)
-    onward = [(i, i + 1) for i in range(X * Z - 1)]
-    kv1 = lax.ppermute(kv, ("x", "z"), onward)
-    kv0 = lax.ppermute(kv1, ("x", "z"), onward)
+        key_norm_gain.reshape(1, HEAD), target)
+    kv1, kv0 = [
+        lax.ppermute(
+            kv, ("x", "z"), [(i, i + d) for i in range(X * Z - d)])
+        for d in (1, 2)
+    ]
     delta = adapt(rows, weights)
     delta = lax.all_to_all(
         delta.reshape(X * T, CAP, UP), ("x", "tp"), 0, 0)
     return attend(
-        delta.reshape(SLOTS, UP), query, kv0, kv1, kv, cosine, sine,
-        query_norm_gain.reshape(1, HEAD), lower, column)
+        delta.reshape(SLOTS, UP), column, query, cosine, sine, lower,
+        kv0, kv1, kv, query_norm_gain.reshape(1, HEAD))
 
 
 def solution(mesh):

time: 81.6 us -> 103 us (1.26)
  the two profiles are of different devices: /device:TPU:1 before, /device:TPU:6 now
where the time goes in v1:
time: 103 us; the launch traced here: 102 us
  starting transfers between devices  41.6 us (40%)
  waiting for transfers between devices  31.5 us (31%)
  Pallas kernels  21.1 us (20%)
  local copies, waits for them, and re-layouts  6.79 us (7%)
  other arithmetic  1.29 us (1%)
    ppermute x2, waiting for transfers between devices, layer(): lax.ppermute(kv, ('x', 'z'), [(i, i + d) for i in range(X * Z - d)])  18.8 us
    ppermute x3, starting transfers between devices, layer(): lax.ppermute(weights, 'z', [((i + d) % Z, i) for i in range(Z)])  13.5 us
    all_to_all x1, starting transfers between devices, layer(): delta = lax.all_to_all(delta.reshape(X * T, CAP, UP), ('x', 'tp'), 0, 0)  9.59 us
    ppermute x3, waiting for transfers between devices, layer(): lax.ppermute(weights, 'z', [((i + d) % Z, i) for i in range(Z)])  8.89 us
    ppermute x2, starting transfers between devices, layer(): lax.ppermute(carried, ('z', 'tp'), [(a * T + w, (w + d) % Z * T + a) for...  8.76 us
    pallas_call x1, Pallas kernels, project(): pl.pallas_call(project_kernel, in_specs=[pl.BlockSpec(memory_space=pltpu....  7.01 us
    unnamed x17, local copies, waits for them, and re-layouts  6.78 us
    pallas_call x1, Pallas kernels, attend(): pl.pallas_call(attend_kernel, in_specs=[far] * 9 + [near], out_specs=near...  5.19 us
  transfers between devices with their start and end apart: 11, of which 6 were waited for; matrix products, arithmetic and copies ran while one was open for 0% of the time, Pallas kernels for 12%

profile of v1, /device:TPU:6, one launch (start us, length us, event | category | flops | bytes accessed | tf_op | source)
XLA Modules:
  0.0 102.5 jit_solution(15916808308281543727)
XLA Ops:
  0.0 1.3 %pad_select_fusion = bf16[64,1024]{1,0:T(8,128)(2,1)S(1)} fusion(bf16[64,256]{1,0:T(8,128)(2,1)} %bitcast.12, bf16[64,672]{1,0:T(8,128)(2,1)} %bitcast.11, pred[]{:T(512)S(6)} %eq.11, pred[]{:T(512)S(6)} %eq.10, pred[]{:T(512)S(6)} %eq.9, pred[1024]{0:T(1024)(128)(4,1)S(1)} %iota_compare_fusion), kind=kLoop, calls=%fused_computation | loop fusion | flops 262144 | bytes 250883 | tf_op jit(solution)/shard_map/jit(_where)/select_n | solution.py:303
  1.3 0.7 collective-permute-start.3
  2.0 5.1 %pack.1 = (bf16[32,5376]{1,0:T(8,128)(2,1)}, bf16[32,5376]{1,0:T(8,128)(2,1)}, bf16[32,5376]{1,0:T(8,128)(2,1)}, bf16[32,5376]{1,0:T(8,128)(2,1)}, s32[1,512]{1,0:T(1,128)}) custom-call(s32[1,512]{1,0:T(1,128)} %bitcast.13, bf16[512,5376]{1,0:T(8,128)(2,1)} %x_ref.3), custom_call_target="tpu_custom_call" | custom-call | flops 704643072 | bytes 7000000 | tf_op jit(solution)/shard_map/pack/pallas_call | solution.py:60
  7.0 2.3 %collective-permute-start = (bf16[32,5376]{1,0:T(8,128)(2,1)}, bf16[32,5376]{1,0:T(8,128)(2,1)S(1)}, u32[]{:S(2)}, u32[]{:S(2)}) collective-permute-start(bf16[32,5376]{1,0:T(8,128)(2,1)} %get-tuple-element.17), channel_id=1, source_target_pairs={{0,64},{64,128},{128,192},{192,0},{1,65},{65,129},{129,193},{193,1... | collective-permute-start | bytes 1032200 | tf_op jit(solution)/shard_map/ppermute | solution.py:320
  9.3 8.1 %collective-permute-start.4 = (bf16[64,1024]{1,0:T(8,128)(2,1)S(1)}, bf16[64,1024]{1,0:T(8,128)(2,1)S(1)}, u32[]{:S(2)}, u32[]{:S(2)}) collective-permute-start(bf16[64,1024]{1,0:T(8,128)(2,1)S(1)} %pad_select_fusion), channel_id=1, source_target_pairs={{0,32},{1,40},{2,48},{3,56},{4,0},{5,8},{6,16},{7,24},{8,33},{9,41... | collective-permute-start | bytes 393224 | tf_op jit(solution)/shard_map/ppermute | solution.py:307
  17.4 2.4 %collective-permute-start.1 = (bf16[32,5376]{1,0:T(8,128)(2,1)}, bf16[32,5376]{1,0:T(8,128)(2,1)S(1)}, u32[]{:S(2)}, u32[]{:S(2)}) collective-permute-start(bf16[32,5376]{1,0:T(8,128)(2,1)} %get-tuple-element.18), channel_id=1, source_target_pairs={{0,128},{64,192},{128,0},{192,64},{1,129},{65,193},{129,1},{193,65... | collective-permute-start | bytes 1032200 | tf_op jit(solution)/shard_map/ppermute | solution.py:320
  19.8 0.0 collective-permute-start.2
  19.8 3.8 %collective-permute-done.4 = bf16[64,1024]{1,0:T(8,128)(2,1)S(1)} collective-permute-done((bf16[64,1024]{1,0:T(8,128)(2,1)S(1)}, bf16[64,1024]{1,0:T(8,128)(2,1)S(1)}, u32[]{:S(2)}, u32[]{:S(2)}) %collective-permute-start.4) | collective-permute-done | bytes 131104 | tf_op jit(solution)/shard_map/ppermute | solution.py:307
  23.7 10.2 %collective-permute-start.7 = (bf16[128,1024]{1,0:T(8,128)(2,1)S(1)}, bf16[128,1024]{1,0:T(8,128)(2,1)S(1)}, u32[]{:S(2)}, u32[]{:S(2)}) collective-permute-start(bf16[128,1024]{1,0:T(8,128)(2,1)S(1)} %constant_dynamic-update-slice_fusion.refs_4_), channel_id=1, source_target_pairs={{16,0},{24,8},{32,16},{40,24},{48,32},{56,40},{0,48},{8,56},{17,1}... | collective-permute-start | bytes 786440 | tf_op jit(solution)/shard_map/ppermute | solution.py:314
  33.9 0.0 collective-permute-start.6
  33.9 0.0 collective-permute-done.refs_1_
  33.9 3.2 %collective-permute-start.5 = (bf16[128,1024]{1,0:T(8,128)(2,1)S(1)}, bf16[128,1024]{1,0:T(8,128)(2,1)S(1)}, u32[]{:S(2)}, u32[]{:S(2)}) collective-permute-start(bf16[128,1024]{1,0:T(8,128)(2,1)S(1)} %constant_dynamic-update-slice_fusion.refs_4_), channel_id=1, source_target_pairs={{8,0},{16,8},{24,16},{32,24},{40,32},{48,40},{56,48},{0,56},{9,1},... | collective-permute-start | bytes 786440 | tf_op jit(solution)/shard_map/ppermute | solution.py:314
  37.1 3.8 %collective-permute-done.7.refs_7_ = bf16[128,1024]{1,0:T(8,128)(2,1)S(1)} collective-permute-done((bf16[128,1024]{1,0:T(8,128)(2,1)S(1)}, bf16[128,1024]{1,0:T(8,128)(2,1)S(1)}, u32[]{:S(2)}, u32[]{:S(2)}) %collective-permute-start.7) | collective-permute-done | bytes 262176 | tf_op jit(solution)/shard_map/ppermute | solution.py:314
  41.0 1.8 %collective-permute-done.6.refs_6_ = bf16[128,1024]{1,0:T(8,128)(2,1)S(1)} collective-permute-done((bf16[128,1024]{1,0:T(8,128)(2,1)S(1)}, bf16[128,1024]{1,0:T(8,128)(2,1)S(1)}, u32[]{:S(2)}, u32[]{:S(2)}) %collective-permute-start.6) | collective-permute-done | bytes 262176 | tf_op jit(solution)/shard_map/ppermute | solution.py:314
  42.8 3.3 %collective-permute-done.5.refs_5_ = bf16[128,1024]{1,0:T(8,128)(2,1)S(1)} collective-permute-done((bf16[128,1024]{1,0:T(8,128)(2,1)S(1)}, bf16[128,1024]{1,0:T(8,128)(2,1)S(1)}, u32[]{:S(2)}, u32[]{:S(2)}) %collective-permute-start.5) | collective-permute-done | bytes 262176 | tf_op jit(solution)/shard_map/ppermute | solution.py:314
  46.0 1.0 copy-done.1
  47.0 3.8 %adapt.1 = bf16[4,8,32,256]{3,2,1,0:T(8,128)(2,1)} custom-call(bf16[32,5376]{1,0:T(8,128)(2,1)S(1)} %copy-done.1, bf16[32,5376]{1,0:T(8,128)(2,1)S(1)} %collective-permute-done.refs_1_, bf16[32,5376]{1,0:T(8,128)(2,1)S(1)} %collective-permute-done.1.refs_2_, bf16[32,5376]{1,0:T(8,128)(2,1)S(1)} %collective-permute-done.2.refs_3_, ...), custom_call_target="tpu_custom_call" | custom-call | flops 121634816 | bytes 3000000 | tf_op jit(solution)/shard_map/adapt/pallas_call | solution.py:194
  50.8 9.6 %all-to-all-start = ((bf16[32,32,256]{2,1,0:T(8,128)(2,1)}), bf16[32,32,256]{2,1,0:T(8,128)(2,1)S(1)}, u32[]{:S(2)}, u32[]{:S(2)}) async-start(bf16[32,32,256]{2,1,0:T(8,128)(2,1)} %bitcast.5), calls=%async_computation | async-start | bytes 1048576 | tf_op jit(solution)/shard_map/all_to_all | solution.py:333
  60.4 0.0 copy-start.7
  60.4 7.0 %project.1 = (f32[512,256]{1,0:T(8,128)}, bf16[512,256]{1,0:T(8,128)(2,1)}, s32[512,128]{1,0:T(8,128)}, s32[512,128]{1,0:T(8,128)}, f32[512,128]{1,0:T(8,128)}, /*index=5*/f32[512,128]{1,0:T(8,128)}) custom-call(s32[16]{0:T(128)} %lens_ref.1, bf16[512,5376]{1,0:T(8,128)(2,1)} %x_ref.3, bf16[5376,256]{1,0:T(8,128)(2,1)} %wq_ref.1, bf16[5376,128]{1,0:T(8,128)(2,1)} %wk_ref.1, ...), custom_call_target="tpu_custom_call" | custom-call | flops 2818572288 | bytes 12500000 | tf_op jit(solution)/shard_map/project/pallas_call | solution.py:139
  67.4 3.0 %collective-permute-start.9 = (bf16[512,256]{1,0:T(8,128)(2,1)}, bf16[512,256]{1,0:T(8,128)(2,1)S(1)}, u32[]{:S(2)}, u32[]{:S(2)}) collective-permute-start(bf16[512,256]{1,0:T(8,128)(2,1)} %get-tuple-element.26.kv2_hbm), channel_id=1, source_target_pairs={{0,8},{8,16},{16,24},{24,32},{32,40},{40,48},{48,56},{56,64},{64,7... | collective-permute-start | bytes 786440 | tf_op jit(solution)/shard_map/ppermute | solution.py:328
  70.4 2.1 %collective-permute-start.8 = (bf16[512,256]{1,0:T(8,128)(2,1)}, bf16[512,256]{1,0:T(8,128)(2,1)S(1)}, u32[]{:S(2)}, u32[]{:S(2)}) collective-permute-start(bf16[512,256]{1,0:T(8,128)(2,1)} %get-tuple-element.26.kv2_hbm), channel_id=1, source_target_pairs={{0,16},{8,24},{16,32},{24,40},{32,48},{40,56},{48,64},{56,72},{64,... | collective-permute-start | bytes 786440 | tf_op jit(solution)/shard_map/ppermute | solution.py:328
  72.5 8.5 %collective-permute-done.9.kv1_hbm = bf16[512,256]{1,0:T(8,128)(2,1)S(1)} collective-permute-done((bf16[512,256]{1,0:T(8,128)(2,1)}, bf16[512,256]{1,0:T(8,128)(2,1)S(1)}, u32[]{:S(2)}, u32[]{:S(2)}) %collective-permute-start.9) | collective-permute-done | bytes 262176 | tf_op jit(solution)/shard_map/ppermute | solution.py:328
  81.0 10.4 %collective-permute-done.8.kv0_hbm = bf16[512,256]{1,0:T(8,128)(2,1)S(1)} collective-permute-done((bf16[512,256]{1,0:T(8,128)(2,1)}, bf16[512,256]{1,0:T(8,128)(2,1)S(1)}, u32[]{:S(2)}, u32[]{:S(2)}) %collective-permute-start.8) | collective-permute-done | bytes 262176 | tf_op jit(solution)/shard_map/ppermute | solution.py:328
  91.3 0.0 all-to-all-done
  91.4 1.0 %copy-done = f32[512,256]{1,0:T(8,128)S(1)} copy-done((f32[512,256]{1,0:T(8,128)S(1)}, f32[512,256]{1,0:T(8,128)}, u32[]{:S(2)}) %copy-start) | copy-done | bytes 524312
  92.4 0.9 copy-done.2
  93.3 0.9 copy-done.3
  94.3 0.9 copy-done.4
  95.2 0.9 copy-done.5
  96.2 0.9 copy-done.6
  97.1 5.2 %attend.1 = bf16[512,256]{1,0:T(8,128)(2,1)} custom-call(bf16[1024,256]{1,0:T(8,128)(2,1)S(1)} %bitcast.9, s32[512,128]{1,0:T(8,128)S(1)} %copy-done.4, f32[512,256]{1,0:T(8,128)S(1)} %copy-done, f32[512,128]{1,0:T(8,128)S(1)} %copy-done.5, f32[512,128]{1,0:T(8,128)S(1)} %copy-done.6, s32[512,128]{1,0:T(8,128)S(1)} %copy-done.3, ...), custom_call_target="tpu_custom_call" | custom-call | flops 671088640 | bytes 4000000 | tf_op jit(solution)/shard_map/attend/pallas_call | solution.py:269
  (14 shorter events, 0.0 us)
Async XLA Ops:
  1.3 18.5 %collective-permute-start.3 = (bf16[64,1024]{1,0:T(8,128)(2,1)S(1)}, bf16[64,1024]{1,0:T(8,128)(2,1)S(1)}, u32[]{:S(2)}, u32[]{:S(2)}) collective-permute-start(bf16[64,1024]{1,0:T(8,128)(2,1)S(1)} %pad_select_fusion), channel_id=1, source_target_pairs={{0,0},{1,8},{2,16},{3,24},{4,32},{5,40},{6,48},{7,56},{8,1},{9,9},... | collective-permute-start | bytes 393224 | tf_op jit(solution)/shard_map/ppermute | solution.py:307
  7.0 26.8 %collective-permute-start = (bf16[32,5376]{1,0:T(8,128)(2,1)}, bf16[32,5376]{1,0:T(8,128)(2,1)S(1)}, u32[]{:S(2)}, u32[]{:S(2)}) collective-permute-start(bf16[32,5376]{1,0:T(8,128)(2,1)} %get-tuple-element.17), channel_id=1, source_target_pairs={{0,64},{64,128},{128,192},{192,0},{1,65},{65,129},{129,193},{193,1... | collective-permute-start | bytes 1032200 | tf_op jit(solution)/shard_map/ppermute | solution.py:320
  9.3 14.3 %collective-permute-start.4 = (bf16[64,1024]{1,0:T(8,128)(2,1)S(1)}, bf16[64,1024]{1,0:T(8,128)(2,1)S(1)}, u32[]{:S(2)}, u32[]{:S(2)}) collective-permute-start(bf16[64,1024]{1,0:T(8,128)(2,1)S(1)} %pad_select_fusion), channel_id=1, source_target_pairs={{0,32},{1,40},{2,48},{3,56},{4,0},{5,8},{6,16},{7,24},{8,33},{9,41... | collective-permute-start | bytes 393224 | tf_op jit(solution)/shard_map/ppermute | solution.py:307
  17.4 19.7 %collective-permute-start.1 = (bf16[32,5376]{1,0:T(8,128)(2,1)}, bf16[32,5376]{1,0:T(8,128)(2,1)S(1)}, u32[]{:S(2)}, u32[]{:S(2)}) collective-permute-start(bf16[32,5376]{1,0:T(8,128)(2,1)} %get-tuple-element.18), channel_id=1, source_target_pairs={{0,128},{64,192},{128,0},{192,64},{1,129},{65,193},{129,1},{193,65... | collective-permute-start | bytes 1032200 | tf_op jit(solution)/shard_map/ppermute | solution.py:320
  19.8 17.3 %collective-permute-start.2 = (bf16[32,5376]{1,0:T(8,128)(2,1)}, bf16[32,5376]{1,0:T(8,128)(2,1)S(1)}, u32[]{:S(2)}, u32[]{:S(2)}) collective-permute-start(bf16[32,5376]{1,0:T(8,128)(2,1)} %get-tuple-element.19), channel_id=1, source_target_pairs={{0,192},{64,0},{128,64},{192,128},{1,193},{65,1},{129,65},{193,129... | collective-permute-start | bytes 1032200 | tf_op jit(solution)/shard_map/ppermute | solution.py:320
  23.7 17.3 %collective-permute-start.7 = (bf16[128,1024]{1,0:T(8,128)(2,1)S(1)}, bf16[128,1024]{1,0:T(8,128)(2,1)S(1)}, u32[]{:S(2)}, u32[]{:S(2)}) collective-permute-start(bf16[128,1024]{1,0:T(8,128)(2,1)S(1)} %constant_dynamic-update-slice_fusion.refs_4_), channel_id=1, source_target_pairs={{16,0},{24,8},{32,16},{40,24},{48,32},{56,40},{0,48},{8,56},{17,1}... | collective-permute-start | bytes 786440 | tf_op jit(solution)/shard_map/ppermute | solution.py:314
  33.9 8.9 %collective-permute-start.6 = (bf16[128,1024]{1,0:T(8,128)(2,1)S(1)}, bf16[128,1024]{1,0:T(8,128)(2,1)S(1)}, u32[]{:S(2)}, u32[]{:S(2)}) collective-permute-start(bf16[128,1024]{1,0:T(8,128)(2,1)S(1)} %constant_dynamic-update-slice_fusion.refs_4_), channel_id=1, source_target_pairs={{56,0},{0,8},{8,16},{16,24},{24,32},{32,40},{40,48},{48,56},{57,1}... | collective-permute-start | bytes 786440 | tf_op jit(solution)/shard_map/ppermute | solution.py:314
  33.9 12.1 %collective-permute-start.5 = (bf16[128,1024]{1,0:T(8,128)(2,1)S(1)}, bf16[128,1024]{1,0:T(8,128)(2,1)S(1)}, u32[]{:S(2)}, u32[]{:S(2)}) collective-permute-start(bf16[128,1024]{1,0:T(8,128)(2,1)S(1)} %constant_dynamic-update-slice_fusion.refs_4_), channel_id=1, source_target_pairs={{8,0},{16,8},{24,16},{32,24},{40,32},{48,40},{56,48},{0,56},{9,1},... | collective-permute-start | bytes 786440 | tf_op jit(solution)/shard_map/ppermute | solution.py:314
  46.0 1.0 copy-start.1
  50.8 40.5 %all-to-all-start = ((bf16[32,32,256]{2,1,0:T(8,128)(2,1)}), bf16[32,32,256]{2,1,0:T(8,128)(2,1)S(1)}, u32[]{:S(2)}, u32[]{:S(2)}) async-start(bf16[32,32,256]{2,1,0:T(8,128)(2,1)} %bitcast.5), calls=%async_computation | async-start | bytes 1048576 | tf_op jit(solution)/shard_map/all_to_all | solution.py:333
  60.4 30.9 %copy-start.7 = (f32[128]{0:T(128)S(1)}, f32[128]{0:T(128)}, u32[]{:S(2)}) copy-start(f32[128]{0:T(128)} %param.14) | copy-start | bytes 1540
  67.4 13.6 %collective-permute-start.9 = (bf16[512,256]{1,0:T(8,128)(2,1)}, bf16[512,256]{1,0:T(8,128)(2,1)S(1)}, u32[]{:S(2)}, u32[]{:S(2)}) collective-permute-start(bf16[512,256]{1,0:T(8,128)(2,1)} %get-tuple-element.26.kv2_hbm), channel_id=1, source_target_pairs={{0,8},{8,16},{16,24},{24,32},{32,40},{40,48},{48,56},{56,64},{64,7... | collective-permute-start | bytes 786440 | tf_op jit(solution)/shard_map/ppermute | solution.py:328
  70.4 20.9 %collective-permute-start.8 = (bf16[512,256]{1,0:T(8,128)(2,1)}, bf16[512,256]{1,0:T(8,128)(2,1)S(1)}, u32[]{:S(2)}, u32[]{:S(2)}) collective-permute-start(bf16[512,256]{1,0:T(8,128)(2,1)} %get-tuple-element.26.kv2_hbm), channel_id=1, source_target_pairs={{0,16},{8,24},{16,32},{24,40},{32,48},{40,56},{48,64},{56,72},{64,... | collective-permute-start | bytes 786440 | tf_op jit(solution)/shard_map/ppermute | solution.py:328
  91.3 1.0 %copy-start = (f32[512,256]{1,0:T(8,128)S(1)}, f32[512,256]{1,0:T(8,128)}, u32[]{:S(2)}) copy-start(f32[512,256]{1,0:T(8,128)} %get-tuple-element.22.q_hbm) | copy-start | bytes 1572868
  92.4 0.9 copy-start.2
  93.3 0.9 copy-start.3
  94.3 0.9 copy-start.4
  95.2 0.9 copy-start.5
  96.2 0.9 copy-start.6

commit v2 on v1

--- a/solution.py
+++ b/solution.py
@@ -17,7 +17,10 @@
 STEPS = WIDTH // STEP
 UP = 256
 SLOTS = X * T * CAP
-NEAR = (0, 1, Z - 1, 2)
+COS, SIN, AUX, SIDE = 2 * HEAD, 3 * HEAD, 4 * HEAD, 5 * HEAD
+NEAR = (0, 1, Z - 1, 2, Z - 2)
+SPLIT = (2, 2, 2, 1, 1)
+PARTS = len(NEAR)
 
 
 def dot(a, b, ca=1, cb=0):
@@ -59,7 +62,7 @@
     row = jax.ShapeDtypeStruct((CAP, WIDTH), jnp.bfloat16)
     return pl.pallas_call(
         pack_kernel,
-        in_specs=[pl.BlockSpec(memory_space=pltpu.VMEM), pl.BlockSpec(memory_space=pl.ANY)],
+        in_specs=[pl.BlockSpec(memory_space=pltpu.VMEM), pl.BlockSpec(memory_space=pltpu.HBM)],
         out_specs=[pl.BlockSpec(memory_space=pltpu.VMEM)] * (X + 1),
         out_shape=[row] * X + [jax.ShapeDtypeStruct((1, ROWS), jnp.int32)],
         scratch_shapes=[
@@ -70,6 +73,7 @@
         cost_estimate=pl.CostEstimate(
             flops=2 * X * CAP * ROWS * WIDTH, bytes_accessed=7_000_000, transcendentals=0
         ),
+        compiler_params=pltpu.CompilerParams(vmem_limit_bytes=12 << 20),
         name="pack",
     )(idx, tokens)
 
@@ -84,7 +88,7 @@
 
 def project_kernel(
     lens_ref, x_ref, wq_ref, wk_ref, wv_ref, gain_ref, target_ref,
-    q_ref, kv_ref, lower_ref, column_ref, cos_ref, sin_ref, x_held, q_held, kv_held, acc, sems,
+    side_ref, kv_ref, x_held, q_held, kv_held, acc, sems,
 ):
     copies = []
     for j in range(STEPS):
@@ -109,44 +113,42 @@
     for i in range(lens_ref.shape[0]):
         start = jnp.where(place >= at, at, start)
         at = at + lens_ref[i]
-    lower_ref[...] = jnp.maximum(start, place - (WINDOW - 1)) - (begin - WINDOW)
+    lower = jnp.maximum(start, place - (WINDOW - 1)) - (begin - WINDOW)
     wide = jnp.broadcast_to(target_ref[...].astype(jnp.float32), (HEAD, ROWS))
-    column_ref[...] = jnp.transpose(wide).astype(jnp.int32)
     lane = lax.broadcasted_iota(jnp.int32, (ROWS, HEAD), 1)
+    side_ref[:, AUX:] = jnp.where(lane < HEAD // 2, lower.astype(jnp.float32), jnp.transpose(wide))
     pair = jnp.bitwise_and(lane, HEAD // 2 - 1).astype(jnp.float32)
     angle = place.astype(jnp.float32) * jnp.exp(-(2.0 * pair / HEAD) * jnp.log(jnp.float32(10000.0)))
-    cos_ref[...] = jnp.cos(angle)
+    cosine = jnp.cos(angle)
     sine = jnp.sin(angle)
-    sin_ref[...] = jnp.where(lane < HEAD // 2, -sine, sine)
+    sine = jnp.where(lane < HEAD // 2, -sine, sine)
+    side_ref[:, COS:SIN] = cosine
+    side_ref[:, SIN:AUX] = sine
     for j in range(STEPS):
         for copy in copies[j]:
             copy.wait()
         q = dot(x_held[j], q_held[j])
         kv = dot(x_held[j], kv_held[j])
         if j == 0:
-            q_ref[...] = q
+            side_ref[:, :COS] = q
             acc[...] = kv
         else:
-            q_ref[...] += q
+            side_ref[:, :COS] += q
             acc[...] += kv
-    key = turn(unit(acc[:, :HEAD], gain_ref[...]), cos_ref[...], sin_ref[...])
+    key = turn(unit(acc[:, :HEAD], gain_ref[...]), side_ref[:, COS:SIN], side_ref[:, SIN:AUX])
     kv_ref[:, :HEAD] = key.astype(jnp.bfloat16)
     kv_ref[:, HEAD:] = acc[:, HEAD:].astype(jnp.bfloat16)
 
 
 def project(lens, tokens, wq, wk, wv, gain, target):
-    near, far = pl.BlockSpec(memory_space=pltpu.VMEM), pl.BlockSpec(memory_space=pl.ANY)
+    near, far = pl.BlockSpec(memory_space=pltpu.VMEM), pl.BlockSpec(memory_space=pltpu.HBM)
     return pl.pallas_call(
         project_kernel,
         in_specs=[pl.BlockSpec(memory_space=pltpu.SMEM)] + [far] * 4 + [near] * 2,
-        out_specs=[near] * 6,
+        out_specs=[near] * 2,
         out_shape=[
-            jax.ShapeDtypeStruct((ROWS, 2 * HEAD), jnp.float32),
+            jax.ShapeDtypeStruct((ROWS, SIDE), jnp.float32),
             jax.ShapeDtypeStruct((ROWS, 2 * HEAD), jnp.bfloat16),
-            jax.ShapeDtypeStruct((ROWS, HEAD), jnp.int32),
-            jax.ShapeDtypeStruct((ROWS, HEAD), jnp.int32),
-            jax.ShapeDtypeStruct((ROWS, HEAD), jnp.float32),
-            jax.ShapeDtypeStruct((ROWS, HEAD), jnp.float32),
         ],
         scratch_shapes=[
             pltpu.VMEM((STEPS, ROWS, STEP), jnp.bfloat16),
@@ -158,19 +160,20 @@
         cost_estimate=pl.CostEstimate(
             flops=2 * ROWS * WIDTH * 512, bytes_accessed=12_500_000, transcendentals=0
         ),
+        compiler_params=pltpu.CompilerParams(vmem_limit_bytes=20 << 20),
         name="project",
     )(lens, tokens, wq, wk, wv, gain, target)
 
 
 def adapt_kernel(*refs):
-    rows, weights, out = refs[:X], refs[X:X + 4], refs[X + 4]
-    packed, held, sems = refs[X + 5:]
-    x, z = lax.axis_index("x"), lax.axis_index("z")
+    rows, weights, out = refs[:X], refs[X:X + PARTS], refs[X + PARTS]
+    packed, held, sems = refs[X + PARTS + 1:]
+    x, z, t = lax.axis_index("x"), lax.axis_index("z"), lax.axis_index("tp")
     copies = [
         pltpu.make_async_copy(
             weights[d].at[pl.ds(n * RANK, RANK), :],
-            held.at[lax.rem(z + NEAR[d] + 4 * n, T)], sems.at[X + 2 * d + n])
-        for d in range(4) for n in range(2)
+            held.at[lax.rem(z - t + T + NEAR[d] + 4 * n, T)], sems.at[X + sum(SPLIT[:d]) + n])
+        for d in range(PARTS) for n in range(SPLIT[d])
     ] + [
         pltpu.make_async_copy(rows[d], packed.at[pl.ds(d * CAP, CAP), :], sems.at[d])
         for d in range(X)
@@ -193,7 +196,7 @@
 def adapt(rows, weights):
     return pl.pallas_call(
         adapt_kernel,
-        in_specs=[pl.BlockSpec(memory_space=pl.ANY)] * (X + 4),
+        in_specs=[pl.BlockSpec(memory_space=pl.ANY)] * (X + PARTS),
         out_specs=pl.BlockSpec(memory_space=pltpu.VMEM),
         out_shape=jax.ShapeDtypeStruct((X, T, CAP, UP), jnp.bfloat16),
         scratch_shapes=[
@@ -209,13 +212,13 @@
     )(*rows, *weights)
 
 
-def attend_kernel(delta_hbm, column_hbm, q_hbm, cos_hbm, sin_hbm, lower_hbm, kv0_hbm, kv1_hbm, kv2_hbm,
-                  gain_ref, out_ref, delta_ref, column_ref, q_ref, cos_ref, sin_ref, lower_ref,
-                  kv_ref, sems):
+def attend_kernel(delta_hbm, side_hbm, kv0_hbm, kv1_hbm, kv2_hbm, gain_ref, out_ref,
+                  delta_ref, side_ref, kv_ref, sems):
     half = ROWS // 2
     pairs = [
-        (column_hbm, column_ref), (delta_hbm, delta_ref), (q_hbm, q_ref), (cos_hbm, cos_ref),
-        (sin_hbm, sin_ref), (lower_hbm, lower_ref),
+        (side_hbm.at[:, pl.ds(AUX, HEAD)], side_ref.at[:, pl.ds(AUX, HEAD)]),
+        (delta_hbm, delta_ref),
+        (side_hbm.at[:, pl.ds(0, AUX)], side_ref.at[:, pl.ds(0, AUX)]),
     ] + [
         (source.at[:, pl.ds(n * HEAD, HEAD)], kv_ref.at[pl.ds(b * ROWS, ROWS), pl.ds(n * HEAD, HEAD)])
         for b, source in enumerate((kv0_hbm, kv1_hbm, kv2_hbm)) for n in range(2)
@@ -229,29 +232,28 @@
     kv_ref[:, 2 * HEAD:] = jnp.ones((3 * ROWS, HEAD), jnp.bfloat16)
     slot = lax.broadcasted_iota(jnp.int32, (ROWS, HEAD), 1)
     copies[0].wait()
-    column = column_ref[...]
+    column = jnp.broadcast_to(side_ref[:, SIDE - 1:].astype(jnp.int32), (ROWS, HEAD))
     chosen = jnp.concatenate(
         [(column == slot + c * HEAD).astype(jnp.float32).astype(jnp.bfloat16)
          for c in range(SLOTS // HEAD)], axis=1)
     copies[1].wait()
     delta = dot(chosen, delta_ref[...])
-    for copy in copies[2:5]:
-        copy.wait()
-    query = q_ref[...] + delta
+    copies[2].wait()
+    query = side_ref[:, :COS] + delta
     gain = gain_ref[...] * (QUERY_SCALE * LOG2E)
     turned = [
-        turn(unit(query[:, h * HEAD:(h + 1) * HEAD], gain), cos_ref[...], sin_ref[...]
-             ).astype(jnp.bfloat16)
+        turn(unit(query[:, h * HEAD:(h + 1) * HEAD], gain), side_ref[:, COS:SIN],
+             side_ref[:, SIN:AUX]).astype(jnp.bfloat16)
         for h in range(2)
     ]
-    for copy in copies[5:]:
+    for copy in copies[3:]:
         copy.wait()
     for tile in range(2):
         here = slice(tile * half, (tile + 1) * half)
         first, past = tile * half, tile * half + WINDOW + half
         q = jnp.concatenate([turned[0][here], turned[1][here]], axis=0)
         s = dot(q, kv_ref[first:past, :HEAD], 1, 1)
-        low = lower_ref[here, :1] - first
+        low = side_ref[here, AUX:AUX + 1].astype(jnp.int32) - first
         at = lax.broadcasted_iota(jnp.int32, (half, WINDOW + half), 1)
         high = WINDOW + lax.broadcasted_iota(jnp.int32, (half, 1), 0)
         allowed = (at >= low) & (at <= high)
@@ -268,18 +270,14 @@
     near, far = pl.BlockSpec(memory_space=pltpu.VMEM), pl.BlockSpec(memory_space=pl.ANY)
     return pl.pallas_call(
         attend_kernel,
-        in_specs=[far] * 9 + [near],
+        in_specs=[far] * 5 + [near],
         out_specs=near,
         out_shape=jax.ShapeDtypeStruct((ROWS, 2 * HEAD), jnp.bfloat16),
         scratch_shapes=[
             pltpu.VMEM((SLOTS, UP), jnp.bfloat16),
-            pltpu.VMEM((ROWS, HEAD), jnp.int32),
-            pltpu.VMEM((ROWS, 2 * HEAD), jnp.float32),
-            pltpu.VMEM((ROWS, HEAD), jnp.float32),
-            pltpu.VMEM((ROWS, HEAD), jnp.float32),
-            pltpu.VMEM((ROWS, HEAD), jnp.int32),
+            pltpu.VMEM((ROWS, SIDE), jnp.float32),
             pltpu.VMEM((3 * ROWS, 3 * HEAD), jnp.bfloat16),
-            pltpu.SemaphoreType.DMA((12,)),
+            pltpu.SemaphoreType.DMA((9,)),
         ],
         compiler_params=pltpu.CompilerParams(vmem_limit_bytes=24 << 20),
         cost_estimate=pl.CostEstimate(
@@ -293,6 +291,10 @@
     tokens, query_weight, key_weight, value_weight, query_norm_gain, key_norm_gain,
     adapter_down_weight, adapter_up_weight, token_adapter_index, packed_prompt_length,
 ):
+    tokens, query_weight, key_weight, value_weight = [
+        pltpu.with_memory_space_constraint(v, pltpu.HBM)
+        for v in (tokens, query_weight, key_weight, value_weight)
+    ]
     t = lax.axis_index("tp")
     down = jnp.swapaxes(adapter_down_weight[0], 0, 1)
     shift = lax.rem(t * SLICE, 128)
@@ -303,16 +305,16 @@
     carried = jnp.where(
         jnp.arange(PAD + UP)[None, :] < PAD, carried,
         jnp.pad(adapter_up_weight[0], ((0, 0), (PAD, 0))))
-    weights = [
+    single, other = [
         lax.ppermute(
             carried, ("z", "tp"),
-            [(a * T + w, (w + d) % Z * T + a) for a in range(Z) for w in range(T)])
+            [(a * T + w, (a + w + d) % Z * T + a) for a in range(Z) for w in range(T)])
         for d in (0, 4)
     ]
-    weights = jnp.concatenate(weights, axis=0)
-    weights = [weights] + [
+    double = jnp.concatenate([single, other], axis=0)
+    weights = [double] + [
         lax.ppermute(
-            weights, "z", [((i + d) % Z, i) for i in range(Z)])
+            double if d in (1, Z - 1) else single, "z", [((i + d) % Z, i) for i in range(Z)])
         for d in NEAR[1:]
     ]
     *rows, target = pack(token_adapter_index.reshape(1, ROWS), tokens)
@@ -321,7 +323,7 @@
             rows[d], "x", [(i, (i + d) % X) for i in range(X)])
         for d in range(1, X)
     ]
-    query, kv, lower, column, cosine, sine = project(
+    side, kv = project(
         packed_prompt_length, tokens, query_weight, key_weight, value_weight,
         key_norm_gain.reshape(1, HEAD), target)
     kv1, kv0 = [
@@ -333,8 +335,7 @@
     delta = lax.all_to_all(
         delta.reshape(X * T, CAP, UP), ("x", "tp"), 0, 0)
     return attend(
-        delta.reshape(SLOTS, UP), column, query, cosine, sine, lower,
-        kv0, kv1, kv, query_norm_gain.reshape(1, HEAD))
+        delta.reshape(SLOTS, UP), side, kv0, kv1, kv, query_norm_gain.reshape(1, HEAD))
 
 
 def solution(mesh):

time: 103 us -> 87.3 us (0.85)
  local copies, waits for them, and re-layouts: 6.79 us -> 0.71 us
  waiting for transfers between devices: 31.5 us -> 26.6 us
  Pallas kernels: 21.1 us -> 18.3 us
  starting transfers between devices: 41.6 us -> 39.8 us
    unnamed x17 -> x9, local copies, waits for them, and re-layouts: 6.78 us -> 0.7 us
    ppermute x5 -> x6, waiting for transfers between devices: 12.7 us -> 7.27 us  [the longest x4 7.27 us: layer(): lax.ppermute(double if d in (1, Z - 1) else single, 'z', [((i + d) % Z, i...]
    ppermute x2, starting transfers between devices: 5.08 us -> 9.08 us  [layer(): lax.ppermute(kv, ('x', 'z'), [(i, i + d) for i in range(X * Z - d)])]
    ppermute x3, waiting for transfers between devices: 0.01 us -> 3.6 us  [layer(): lax.ppermute(rows[d], 'x', [(i, (i + d) % X) for i in range(X)])]
    all_to_all x1, starting transfers between devices: 9.59 us -> 6.15 us  [layer(): delta = lax.all_to_all(delta.reshape(X * T, CAP, UP), ('x', 'tp'), 0, 0)]
    ppermute x2, waiting for transfers between devices: 18.8 us -> 15.7 us  [layer(): lax.ppermute(kv, ('x', 'z'), [(i, i + d) for i in range(X * Z - d)])]
    pallas_call x1, Pallas kernels: 5.07 us -> 3.31 us  [pack(): pl.pallas_call(pack_kernel, in_specs=[pl.BlockSpec(memory_space=pltpu.VME...]
    ppermute x3, starting transfers between devices: 4.68 us -> 3.06 us  [layer(): lax.ppermute(rows[d], 'x', [(i, (i + d) % X) for i in range(X)])]
  transfers between devices with their start and end apart: 11 -> 12, of which waited for: 6 -> 7; matrix products, arithmetic and copies ran while one was open for 0% -> 0% of each run, Pallas kernels for 12% -> 11%
where the time goes in v2:
time: 87.3 us; the launch traced here: 87 us
  starting transfers between devices  39.8 us (46%)
  waiting for transfers between devices  26.6 us (30%)
  Pallas kernels  18.3 us (21%)
  other arithmetic  1.29 us (1%)
    ppermute x2, waiting for transfers between devices, layer(): lax.ppermute(kv, ('x', 'z'), [(i, i + d) for i in range(X * Z - d)])  15.7 us
    ppermute x2, starting transfers between devices, layer(): lax.ppermute(carried, ('z', 'tp'), [(a * T + w, (a + w + d) % Z * T + a)...  14.2 us
    ppermute x2, starting transfers between devices, layer(): lax.ppermute(kv, ('x', 'z'), [(i, i + d) for i in range(X * Z - d)])  9.08 us
    ppermute x4, waiting for transfers between devices, layer(): lax.ppermute(double if d in (1, Z - 1) else single, 'z', [((i + d) % Z, i...  7.27 us
    ppermute x4, starting transfers between devices, layer(): lax.ppermute(double if d in (1, Z - 1) else single, 'z', [((i + d) % Z, i...  7.26 us
    all_to_all x1, starting transfers between devices, layer(): delta = lax.all_to_all(delta.reshape(X * T, CAP, UP), ('x', 'tp'), 0, 0)  6.15 us
    pallas_call x1, Pallas kernels, project(): pl.pallas_call(project_kernel, in_specs=[pl.BlockSpec(memory_space=pltpu....  5.97 us
    pallas_call x1, Pallas kernels, attend(): pl.pallas_call(attend_kernel, in_specs=[far] * 5 + [near], out_specs=near...  5.18 us
  transfers between devices with their start and end apart: 12, of which 7 were waited for; matrix products, arithmetic and copies ran while one was open for 0% of the time, Pallas kernels for 11%

profile of v2, /device:TPU:6, one launch (start us, length us, event | category | flops | bytes accessed | tf_op | source)
XLA Modules:
  0.0 87.0 jit_solution(4799472886807525436)
XLA Ops:
  0.0 1.3 %pad_select_fusion = bf16[64,1024]{1,0:T(8,128)(2,1)S(1)} fusion(bf16[64,256]{1,0:T(8,128)(2,1)} %bitcast.14, bf16[64,672]{1,0:T(8,128)(2,1)} %bitcast.13, pred[]{:T(512)S(6)} %eq.11, pred[]{:T(512)S(6)} %eq.10, pred[]{:T(512)S(6)} %eq.9, pred[1024]{0:T(1024)(128)(4,1)S(1)} %iota_compare_fusion), kind=kLoop, calls=%fused_computation | loop fusion | flops 262144 | bytes 250883 | tf_op jit(solution)/shard_map/jit(_where)/select_n | solution.py:305
  1.3 0.7 collective-permute-start.3
  2.0 13.5 %collective-permute-start.4 = (bf16[64,1024]{1,0:T(8,128)(2,1)S(1)}, bf16[64,1024]{1,0:T(8,128)(2,1)S(1)}, u32[]{:S(2)}, u32[]{:S(2)}) collective-permute-start(bf16[64,1024]{1,0:T(8,128)(2,1)S(1)} %pad_select_fusion), channel_id=1, source_target_pairs={{0,32},{1,40},{2,48},{3,56},{4,0},{5,8},{6,16},{7,24},{8,41},{9,49... | collective-permute-start | bytes 393224 | tf_op jit(solution)/shard_map/ppermute | solution.py:309
  15.5 0.0 copy-start
  15.5 0.7 copy-done
  16.2 3.3 %pack.1 = (bf16[32,5376]{1,0:T(8,128)(2,1)S(1)}, bf16[32,5376]{1,0:T(8,128)(2,1)S(1)}, bf16[32,5376]{1,0:T(8,128)(2,1)S(1)}, bf16[32,5376]{1,0:T(8,128)(2,1)S(1)}, s32[1,512]{1,0:T(1,128)S(1)}) custom-call(s32[1,512]{1,0:T(1,128)S(1)} %bitcast.10, bf16[512,5376]{1,0:T(8,128)(2,1)} %x_ref.3), custom_call_target="tpu_custom_call" | custom-call | flops 704643072 | bytes 7000000 | tf_op jit(solution)/shard_map/pack/pallas_call | solution.py:63
  19.5 0.6 collective-permute-start
  20.1 2.4 %collective-permute-start.1 = (bf16[32,5376]{1,0:T(8,128)(2,1)S(1)}, bf16[32,5376]{1,0:T(8,128)(2,1)S(1)}, u32[]{:S(2)}, u32[]{:S(2)}) collective-permute-start(bf16[32,5376]{1,0:T(8,128)(2,1)S(1)} %get-tuple-element.14), channel_id=1, source_target_pairs={{0,128},{64,192},{128,0},{192,64},{1,129},{65,193},{129,1},{193,65... | collective-permute-start | bytes 1032200 | tf_op jit(solution)/shard_map/ppermute | solution.py:322
  22.5 0.0 collective-permute-done.3
  22.5 0.0 collective-permute-start.8
  22.5 4.1 %collective-permute-start.7 = (bf16[64,1024]{1,0:T(8,128)(2,1)S(1)}, bf16[64,1024]{1,0:T(8,128)(2,1)S(1)}, u32[]{:S(2)}, u32[]{:S(2)}) collective-permute-start(bf16[64,1024]{1,0:T(8,128)(2,1)S(1)} %collective-permute-done.3), channel_id=1, source_target_pairs={{16,0},{24,8},{32,16},{40,24},{48,32},{56,40},{0,48},{8,56},{17,1}... | collective-permute-start | bytes 393224 | tf_op jit(solution)/shard_map/ppermute | solution.py:316
  26.6 0.0 collective-permute-done.4
  26.6 0.1 collective-permute-start.2
  26.8 4.1 %collective-permute-done.8.refs_8_ = bf16[64,1024]{1,0:T(8,128)(2,1)S(1)} collective-permute-done((bf16[64,1024]{1,0:T(8,128)(2,1)S(1)}, bf16[64,1024]{1,0:T(8,128)(2,1)S(1)}, u32[]{:S(2)}, u32[]{:S(2)}) %collective-permute-start.8) | collective-permute-done | bytes 131104 | tf_op jit(solution)/shard_map/ppermute | solution.py:316
  30.9 1.9 %collective-permute-start.6 = (bf16[128,1024]{1,0:T(8,128)(2,1)S(1)}, bf16[128,1024]{1,0:T(8,128)(2,1)S(1)}, u32[]{:S(2)}, u32[]{:S(2)}) collective-permute-start(bf16[128,1024]{1,0:T(8,128)(2,1)S(1)} %constant_dynamic-update-slice_fusion.refs_4_), channel_id=1, source_target_pairs={{56,0},{0,8},{8,16},{16,24},{24,32},{32,40},{40,48},{48,56},{57,1}... | collective-permute-start | bytes 786440 | tf_op jit(solution)/shard_map/ppermute | solution.py:316
  32.8 0.1 collective-permute-done.7.refs_7_
  32.9 1.2 %collective-permute-start.5 = (bf16[128,1024]{1,0:T(8,128)(2,1)S(1)}, bf16[128,1024]{1,0:T(8,128)(2,1)S(1)}, u32[]{:S(2)}, u32[]{:S(2)}) collective-permute-start(bf16[128,1024]{1,0:T(8,128)(2,1)S(1)} %constant_dynamic-update-slice_fusion.refs_4_), channel_id=1, source_target_pairs={{8,0},{16,8},{24,16},{32,24},{40,32},{48,40},{56,48},{0,56},{9,1},... | collective-permute-start | bytes 786440 | tf_op jit(solution)/shard_map/ppermute | solution.py:316
  34.1 0.0 collective-permute-done.refs_1_
  34.1 0.0 collective-permute-done.1.refs_2_
  34.1 3.6 %collective-permute-done.2.refs_3_ = bf16[32,5376]{1,0:T(8,128)(2,1)S(1)} collective-permute-done((bf16[32,5376]{1,0:T(8,128)(2,1)S(1)}, bf16[32,5376]{1,0:T(8,128)(2,1)S(1)}, u32[]{:S(2)}, u32[]{:S(2)}) %collective-permute-start.2) | collective-permute-done | bytes 344096 | tf_op jit(solution)/shard_map/ppermute | solution.py:322
  37.7 1.0 %collective-permute-done.6.refs_6_ = bf16[128,1024]{1,0:T(8,128)(2,1)S(1)} collective-permute-done((bf16[128,1024]{1,0:T(8,128)(2,1)S(1)}, bf16[128,1024]{1,0:T(8,128)(2,1)S(1)}, u32[]{:S(2)}, u32[]{:S(2)}) %collective-permute-start.6) | collective-permute-done | bytes 262176 | tf_op jit(solution)/shard_map/ppermute | solution.py:316
  38.7 2.1 %collective-permute-done.5.refs_5_ = bf16[128,1024]{1,0:T(8,128)(2,1)S(1)} collective-permute-done((bf16[128,1024]{1,0:T(8,128)(2,1)S(1)}, bf16[128,1024]{1,0:T(8,128)(2,1)S(1)}, u32[]{:S(2)}, u32[]{:S(2)}) %collective-permute-start.5) | collective-permute-done | bytes 262176 | tf_op jit(solution)/shard_map/ppermute | solution.py:316
  40.8 3.9 %adapt.1 = bf16[4,8,32,256]{3,2,1,0:T(8,128)(2,1)} custom-call(bf16[32,5376]{1,0:T(8,128)(2,1)S(1)} %get-tuple-element.12.refs_0_, bf16[32,5376]{1,0:T(8,128)(2,1)S(1)} %collective-permute-done.refs_1_, bf16[32,5376]{1,0:T(8,128)(2,1)S(1)} %collective-permute-done.1.refs_2_, bf16[32,5376]{1,0:T(8,128)(2,1)S(1)} %collective-permute-done.2.refs_3_, ...), custom_call_target="tpu_custom_call" | custom-call | flops 121634816 | bytes 3000000 | tf_op jit(solution)/shard_map/adapt/pallas_call | solution.py:197
  44.6 6.2 %all-to-all-start = ((bf16[32,32,256]{2,1,0:T(8,128)(2,1)}), bf16[32,32,256]{2,1,0:T(8,128)(2,1)S(1)}, u32[]{:S(2)}, u32[]{:S(2)}) async-start(bf16[32,32,256]{2,1,0:T(8,128)(2,1)} %bitcast.5), calls=%async_computation | async-start | bytes 1048576 | tf_op jit(solution)/shard_map/all_to_all | solution.py:335
  50.8 0.0 copy-start.3
  50.8 6.0 %project.1 = (f32[512,640]{1,0:T(8,128)S(1)}, bf16[512,256]{1,0:T(8,128)(2,1)S(1)}) custom-call(s32[16]{0:T(128)S(1)} %copy-done.1, bf16[512,5376]{1,0:T(8,128)(2,1)} %x_ref.3, bf16[5376,256]{1,0:T(8,128)(2,1)} %wq_ref.1, bf16[5376,128]{1,0:T(8,128)(2,1)} %wk_ref.1, bf16[5376,128]{1,0:T(8,128)(2,1)} %wv_ref.1, f32[1,128]{1,0:T(1,128)S(1)} %bitcast.11, ...), custom_call_target="tpu_custom_call" | custom-call | flops 2818572288 | bytes 12500000 | tf_op jit(solution)/shard_map/project/pallas_call | solution.py:145
  56.8 2.5 %collective-permute-start.10 = (bf16[512,256]{1,0:T(8,128)(2,1)S(1)}, bf16[512,256]{1,0:T(8,128)(2,1)S(1)}, u32[]{:S(2)}, u32[]{:S(2)}) collective-permute-start(bf16[512,256]{1,0:T(8,128)(2,1)S(1)} %get-tuple-element.18.kv2_hbm), channel_id=1, source_target_pairs={{0,8},{8,16},{16,24},{24,32},{32,40},{40,48},{48,56},{56,64},{64,7... | collective-permute-start | bytes 786440 | tf_op jit(solution)/shard_map/ppermute | solution.py:330
  59.3 6.5 %collective-permute-start.9 = (bf16[512,256]{1,0:T(8,128)(2,1)S(1)}, bf16[512,256]{1,0:T(8,128)(2,1)S(1)}, u32[]{:S(2)}, u32[]{:S(2)}) collective-permute-start(bf16[512,256]{1,0:T(8,128)(2,1)S(1)} %get-tuple-element.18.kv2_hbm), channel_id=1, source_target_pairs={{0,16},{8,24},{16,32},{24,40},{32,48},{40,56},{48,64},{56,72},{64,... | collective-permute-start | bytes 786440 | tf_op jit(solution)/shard_map/ppermute | solution.py:330
  65.9 4.1 %collective-permute-done.10.kv1_hbm = bf16[512,256]{1,0:T(8,128)(2,1)S(1)} collective-permute-done((bf16[512,256]{1,0:T(8,128)(2,1)S(1)}, bf16[512,256]{1,0:T(8,128)(2,1)S(1)}, u32[]{:S(2)}, u32[]{:S(2)}) %collective-permute-start.10) | collective-permute-done | bytes 262176 | tf_op jit(solution)/shard_map/ppermute | solution.py:330
  70.0 11.7 %collective-permute-done.9.kv0_hbm = bf16[512,256]{1,0:T(8,128)(2,1)S(1)} collective-permute-done((bf16[512,256]{1,0:T(8,128)(2,1)S(1)}, bf16[512,256]{1,0:T(8,128)(2,1)S(1)}, u32[]{:S(2)}, u32[]{:S(2)}) %collective-permute-start.9) | collective-permute-done | bytes 262176 | tf_op jit(solution)/shard_map/ppermute | solution.py:330
  81.6 0.0 all-to-all-done
  81.6 5.2 %attend.1 = bf16[512,256]{1,0:T(8,128)(2,1)} custom-call(bf16[1024,256]{1,0:T(8,128)(2,1)S(1)} %bitcast.9, f32[512,640]{1,0:T(8,128)S(1)} %get-tuple-element.17.side_hbm, bf16[512,256]{1,0:T(8,128)(2,1)S(1)} %collective-permute-done.9.kv0_hbm, bf16[512,256]{1,0:T(8,128)(2,1)S(1)} %collective-permute-done.10.kv1_hbm, ...), custom_call_target="tpu_custom_call" | custom-call | flops 671088640 | bytes 4000000 | tf_op jit(solution)/shard_map/attend/pallas_call | solution.py:271
  (8 shorter events, 0.0 us)
Async XLA Ops:
  1.3 21.2 %collective-permute-start.3 = (bf16[64,1024]{1,0:T(8,128)(2,1)S(1)}, bf16[64,1024]{1,0:T(8,128)(2,1)S(1)}, u32[]{:S(2)}, u32[]{:S(2)}) collective-permute-start(bf16[64,1024]{1,0:T(8,128)(2,1)S(1)} %pad_select_fusion), channel_id=1, source_target_pairs={{0,0},{1,8},{2,16},{3,24},{4,32},{5,40},{6,48},{7,56},{8,9},{9,17}... | collective-permute-start | bytes 393224 | tf_op jit(solution)/shard_map/ppermute | solution.py:309
  2.0 24.7 %collective-permute-start.4 = (bf16[64,1024]{1,0:T(8,128)(2,1)S(1)}, bf16[64,1024]{1,0:T(8,128)(2,1)S(1)}, u32[]{:S(2)}, u32[]{:S(2)}) collective-permute-start(bf16[64,1024]{1,0:T(8,128)(2,1)S(1)} %pad_select_fusion), channel_id=1, source_target_pairs={{0,32},{1,40},{2,48},{3,56},{4,0},{5,8},{6,16},{7,24},{8,41},{9,49... | collective-permute-start | bytes 393224 | tf_op jit(solution)/shard_map/ppermute | solution.py:309
  15.5 0.7 copy-start
  19.5 14.6 %collective-permute-start = (bf16[32,5376]{1,0:T(8,128)(2,1)S(1)}, bf16[32,5376]{1,0:T(8,128)(2,1)S(1)}, u32[]{:S(2)}, u32[]{:S(2)}) collective-permute-start(bf16[32,5376]{1,0:T(8,128)(2,1)S(1)} %get-tuple-element.13), channel_id=1, source_target_pairs={{0,64},{64,128},{128,192},{192,0},{1,65},{65,129},{129,193},{193,1... | collective-permute-start | bytes 1032200 | tf_op jit(solution)/shard_map/ppermute | solution.py:322
  20.1 14.1 %collective-permute-start.1 = (bf16[32,5376]{1,0:T(8,128)(2,1)S(1)}, bf16[32,5376]{1,0:T(8,128)(2,1)S(1)}, u32[]{:S(2)}, u32[]{:S(2)}) collective-permute-start(bf16[32,5376]{1,0:T(8,128)(2,1)S(1)} %get-tuple-element.14), channel_id=1, source_target_pairs={{0,128},{64,192},{128,0},{192,64},{1,129},{65,193},{129,1},{193,65... | collective-permute-start | bytes 1032200 | tf_op jit(solution)/shard_map/ppermute | solution.py:322
  22.5 8.4 %collective-permute-start.8 = (bf16[64,1024]{1,0:T(8,128)(2,1)S(1)}, bf16[64,1024]{1,0:T(8,128)(2,1)S(1)}, u32[]{:S(2)}, u32[]{:S(2)}) collective-permute-start(bf16[64,1024]{1,0:T(8,128)(2,1)S(1)} %collective-permute-done.3), channel_id=1, source_target_pairs={{48,0},{56,8},{0,16},{8,24},{16,32},{24,40},{32,48},{40,56},{49,1}... | collective-permute-start | bytes 393224 | tf_op jit(solution)/shard_map/ppermute | solution.py:316
  22.5 10.4 %collective-permute-start.7 = (bf16[64,1024]{1,0:T(8,128)(2,1)S(1)}, bf16[64,1024]{1,0:T(8,128)(2,1)S(1)}, u32[]{:S(2)}, u32[]{:S(2)}) collective-permute-start(bf16[64,1024]{1,0:T(8,128)(2,1)S(1)} %collective-permute-done.3), channel_id=1, source_target_pairs={{16,0},{24,8},{32,16},{40,24},{48,32},{56,40},{0,48},{8,56},{17,1}... | collective-permute-start | bytes 393224 | tf_op jit(solution)/shard_map/ppermute | solution.py:316
  26.6 11.1 %collective-permute-start.2 = (bf16[32,5376]{1,0:T(8,128)(2,1)S(1)}, bf16[32,5376]{1,0:T(8,128)(2,1)S(1)}, u32[]{:S(2)}, u32[]{:S(2)}) collective-permute-start(bf16[32,5376]{1,0:T(8,128)(2,1)S(1)} %get-tuple-element.15), channel_id=1, source_target_pairs={{0,192},{64,0},{128,64},{192,128},{1,193},{65,1},{129,65},{193,129... | collective-permute-start | bytes 1032200 | tf_op jit(solution)/shard_map/ppermute | solution.py:322
  30.9 7.8 %collective-permute-start.6 = (bf16[128,1024]{1,0:T(8,128)(2,1)S(1)}, bf16[128,1024]{1,0:T(8,128)(2,1)S(1)}, u32[]{:S(2)}, u32[]{:S(2)}) collective-permute-start(bf16[128,1024]{1,0:T(8,128)(2,1)S(1)} %constant_dynamic-update-slice_fusion.refs_4_), channel_id=1, source_target_pairs={{56,0},{0,8},{8,16},{16,24},{24,32},{32,40},{40,48},{48,56},{57,1}... | collective-permute-start | bytes 786440 | tf_op jit(solution)/shard_map/ppermute | solution.py:316
  32.9 7.8 %collective-permute-start.5 = (bf16[128,1024]{1,0:T(8,128)(2,1)S(1)}, bf16[128,1024]{1,0:T(8,128)(2,1)S(1)}, u32[]{:S(2)}, u32[]{:S(2)}) collective-permute-start(bf16[128,1024]{1,0:T(8,128)(2,1)S(1)} %constant_dynamic-update-slice_fusion.refs_4_), channel_id=1, source_target_pairs={{8,0},{16,8},{24,16},{32,24},{40,32},{48,40},{56,48},{0,56},{9,1},... | collective-permute-start | bytes 786440 | tf_op jit(solution)/shard_map/ppermute | solution.py:316
  40.8 10.0 %copy-start.1 = (s32[16]{0:T(128)S(1)}, s32[16]{0:T(128)}, u32[]{:S(2)}) copy-start(s32[16]{0:T(128)} %lens_ref.1) | copy-start | bytes 196
  40.8 10.0 %copy-start.2 = (f32[128]{0:T(128)S(1)}, f32[128]{0:T(128)}, u32[]{:S(2)}) copy-start(f32[128]{0:T(128)} %param.15) | copy-start | bytes 1540
  44.6 37.0 %all-to-all-start = ((bf16[32,32,256]{2,1,0:T(8,128)(2,1)}), bf16[32,32,256]{2,1,0:T(8,128)(2,1)S(1)}, u32[]{:S(2)}, u32[]{:S(2)}) async-start(bf16[32,32,256]{2,1,0:T(8,128)(2,1)} %bitcast.5), calls=%async_computation | async-start | bytes 1048576 | tf_op jit(solution)/shard_map/all_to_all | solution.py:335
  50.8 30.8 %copy-start.3 = (f32[128]{0:T(128)S(1)}, f32[128]{0:T(128)}, u32[]{:S(2)}) copy-start(f32[128]{0:T(128)} %param.14) | copy-start | bytes 1540
  56.8 13.2 %collective-permute-start.10 = (bf16[512,256]{1,0:T(8,128)(2,1)S(1)}, bf16[512,256]{1,0:T(8,128)(2,1)S(1)}, u32[]{:S(2)}, u32[]{:S(2)}) collective-permute-start(bf16[512,256]{1,0:T(8,128)(2,1)S(1)} %get-tuple-element.18.kv2_hbm), channel_id=1, source_target_pairs={{0,8},{8,16},{16,24},{24,32},{32,40},{40,48},{48,56},{56,64},{64,7... | collective-permute-start | bytes 786440 | tf_op jit(solution)/shard_map/ppermute | solution.py:330
  59.3 22.3 %collective-permute-start.9 = (bf16[512,256]{1,0:T(8,128)(2,1)S(1)}, bf16[512,256]{1,0:T(8,128)(2,1)S(1)}, u32[]{:S(2)}, u32[]{:S(2)}) collective-permute-start(bf16[512,256]{1,0:T(8,128)(2,1)S(1)} %get-tuple-element.18.kv2_hbm), channel_id=1, source_target_pairs={{0,16},{8,24},{16,32},{24,40},{32,48},{40,56},{48,64},{56,72},{64,... | collective-permute-start | bytes 786440 | tf_op jit(solution)/shard_map/ppermute | solution.py:330

commit v3 on v2

--- a/solution.py
+++ b/solution.py
@@ -1,4 +1,3 @@
-import functools
 import jax
 import jax.numpy as jnp
 from jax import lax
@@ -17,7 +16,7 @@
 STEPS = WIDTH // STEP
 UP = 256
 SLOTS = X * T * CAP
-COS, SIN, AUX, SIDE = 2 * HEAD, 3 * HEAD, 4 * HEAD, 5 * HEAD
+COS, SIN, AUX, SIDE = 0, HEAD, 2 * HEAD, 3 * HEAD
 NEAR = (0, 1, Z - 1, 2, Z - 2)
 SPLIT = (2, 2, 2, 1, 1)
 PARTS = len(NEAR)
@@ -27,7 +26,16 @@
     return lax.dot_general(a, b, (((ca,), (cb,)), ((), ())), preferred_element_type=jnp.float32)
 
 
-def pack_kernel(idx_ref, x_ref, out0, out1, out2, out3, target_ref, pick, held, sems):
+def pack_kernel(idx_hbm, down_hbm, up_hbm, x_ref, out0, out1, out2, out3, target_ref, carried_ref,
+                pick, wide, idx_ref, down_ref, held, sems, small_sems):
+    small = [
+        pltpu.make_async_copy(source, target, small_sems.at[n])
+        for n, (source, target) in enumerate((
+            (idx_hbm, idx_ref), (down_hbm, down_ref),
+            (up_hbm, carried_ref.at[:, pl.ds(PAD, UP)])))
+    ]
+    for copy in small:
+        copy.start()
     copies = [
         pltpu.make_async_copy(x_ref.at[:, pl.ds(j * STEP, STEP)], held.at[j], sems.at[j])
         for j in range(STEPS)
@@ -35,6 +43,7 @@
     for copy in copies:
         copy.start()
     x, t = lax.axis_index("x"), lax.axis_index("tp")
+    small[0].wait()
     idx = idx_ref[...]
     named = lax.broadcasted_iota(jnp.int32, (X * T, ROWS), 0) == idx
     earlier = lax.broadcasted_iota(jnp.int32, (ROWS, ROWS), 0) < lax.broadcasted_iota(
@@ -51,6 +60,11 @@
         pick[d * CAP:(d + 1) * CAP, :] = (
             (slot + adapter * CAP == target).astype(jnp.float32).astype(jnp.bfloat16)
         )
+    small[1].wait()
+    wide[:, PAD - 128:] = jnp.zeros((RANK, 128), jnp.float32)
+    wide[:, :SLICE] = down_ref[...].astype(jnp.float32)
+    carried_ref[:, :PAD] = pltpu.roll(wide[...], lax.rem(t * SLICE, 128), 1).astype(jnp.bfloat16)
+    small[2].wait()
     for j in range(STEPS):
         copies[j].wait()
         packed = dot(pick[...], held[j]).astype(jnp.bfloat16)
@@ -58,24 +72,31 @@
             out[:, j * STEP:(j + 1) * STEP] = packed[d * CAP:(d + 1) * CAP, :]
 
 
-def pack(idx, tokens):
+def pack(idx, down, up, tokens):
     row = jax.ShapeDtypeStruct((CAP, WIDTH), jnp.bfloat16)
     return pl.pallas_call(
         pack_kernel,
-        in_specs=[pl.BlockSpec(memory_space=pltpu.VMEM), pl.BlockSpec(memory_space=pltpu.HBM)],
-        out_specs=[pl.BlockSpec(memory_space=pltpu.VMEM)] * (X + 1),
-        out_shape=[row] * X + [jax.ShapeDtypeStruct((1, ROWS), jnp.int32)],
+        in_specs=[pl.BlockSpec(memory_space=pltpu.HBM)] * 4,
+        out_specs=[pl.BlockSpec(memory_space=pltpu.VMEM)] * (X + 2),
+        out_shape=[row] * X + [
+            jax.ShapeDtypeStruct((1, ROWS), jnp.int32),
+            jax.ShapeDtypeStruct((RANK, PAD + UP), jnp.bfloat16),
+        ],
         scratch_shapes=[
             pltpu.VMEM((X * CAP, ROWS), jnp.bfloat16),
+            pltpu.VMEM((RANK, PAD), jnp.float32),
+            pltpu.VMEM((1, ROWS), jnp.int32),
+            pltpu.VMEM((RANK, SLICE), jnp.bfloat16),
             pltpu.VMEM((STEPS, ROWS, STEP), jnp.bfloat16),
             pltpu.SemaphoreType.DMA((STEPS,)),
+            pltpu.SemaphoreType.DMA((3,)),
         ],
         cost_estimate=pl.CostEstimate(
             flops=2 * X * CAP * ROWS * WIDTH, bytes_accessed=7_000_000, transcendentals=0
         ),
         compiler_params=pltpu.CompilerParams(vmem_limit_bytes=12 << 20),
         name="pack",
-    )(idx, tokens)
+    )(idx, down, up, tokens)
 
 
 def unit(field, gain):
@@ -86,26 +107,29 @@
     return field * cosine + pltpu.roll(field, HEAD // 2, 1) * sine
 
 
-def project_kernel(
-    lens_ref, x_ref, wq_ref, wk_ref, wv_ref, gain_ref, target_ref,
-    side_ref, kv_ref, x_held, q_held, kv_held, acc, sems,
-):
-    copies = []
-    for j in range(STEPS):
-        part = pl.ds(j * STEP, STEP)
-        pairs = (
-            (x_ref.at[:, part], x_held.at[j]),
-            (wk_ref.at[part, :], kv_held.at[j, :, pl.ds(0, HEAD)]),
-            (wv_ref.at[part, :], kv_held.at[j, :, pl.ds(HEAD, HEAD)]),
-            (wq_ref.at[part, :], q_held.at[j]),
-        )
-        copies.append([
-            pltpu.make_async_copy(source, target, sems.at[j, n])
-            for n, (source, target) in enumerate(pairs)
-        ])
+def fetch(pairs, sems):
+    copies = [
+        [pltpu.make_async_copy(source, target, sems.at[j, n])
+         for n, (source, target) in enumerate(group)]
+        for j, group in enumerate(pairs)
+    ]
     for group in copies:
         for copy in group:
             copy.start()
+    return copies
+
+
+def keys_kernel(
+    lens_ref, x_ref, wk_ref, wv_ref, gain_ref, target_ref, side_ref, kv_ref, x_held, kv_held, acc,
+    sems,
+):
+    part = [pl.ds(j * STEP, STEP) for j in range(STEPS)]
+    copies = fetch([
+        ((x_ref.at[:, part[j]], x_held.at[j]),
+         (wk_ref.at[part[j], :], kv_held.at[j, :, pl.ds(0, HEAD)]),
+         (wv_ref.at[part[j], :], kv_held.at[j, :, pl.ds(HEAD, HEAD)]))
+        for j in range(STEPS)
+    ], sems)
     begin = (lax.axis_index("x") * Z + lax.axis_index("z")) * ROWS
     place = begin + lax.broadcasted_iota(jnp.int32, (ROWS, HEAD), 0)
     start = jnp.zeros((ROWS, HEAD), jnp.int32)
@@ -119,50 +143,80 @@
     side_ref[:, AUX:] = jnp.where(lane < HEAD // 2, lower.astype(jnp.float32), jnp.transpose(wide))
     pair = jnp.bitwise_and(lane, HEAD // 2 - 1).astype(jnp.float32)
     angle = place.astype(jnp.float32) * jnp.exp(-(2.0 * pair / HEAD) * jnp.log(jnp.float32(10000.0)))
-    cosine = jnp.cos(angle)
     sine = jnp.sin(angle)
-    sine = jnp.where(lane < HEAD // 2, -sine, sine)
-    side_ref[:, COS:SIN] = cosine
-    side_ref[:, SIN:AUX] = sine
+    side_ref[:, COS:SIN] = jnp.cos(angle)
+    side_ref[:, SIN:AUX] = jnp.where(lane < HEAD // 2, -sine, sine)
+    for j in range(STEPS):
+        for copy in copies[j]:
+            copy.wait()
+        kv = dot(x_held[j], kv_held[j])
+        if j == 0:
+            acc[...] = kv
+        else:
+            acc[...] += kv
+    key = turn(unit(acc[:, :HEAD], gain_ref[...]), side_ref[:, COS:SIN], side_ref[:, SIN:AUX])
+    kv_ref[:, :HEAD] = key.astype(jnp.bfloat16)
+    kv_ref[:, HEAD:] = acc[:, HEAD:].astype(jnp.bfloat16)
+
+
+def project_keys(lens, tokens, wk, wv, gain, target):
+    near, far = pl.BlockSpec(memory_space=pltpu.VMEM), pl.BlockSpec(memory_space=pltpu.HBM)
+    return pl.pallas_call(
+        keys_kernel,
+        in_specs=[pl.BlockSpec(memory_space=pltpu.SMEM)] + [far] * 3 + [near] * 2,
+        out_specs=[near] * 2,
+        out_shape=[
+            jax.ShapeDtypeStruct((ROWS, SIDE), jnp.float32),
+            jax.ShapeDtypeStruct((ROWS, 2 * HEAD), jnp.bfloat16),
+        ],
+        scratch_shapes=[
+            pltpu.VMEM((STEPS, ROWS, STEP), jnp.bfloat16),
+            pltpu.VMEM((STEPS, STEP, 2 * HEAD), jnp.bfloat16),
+            pltpu.VMEM((ROWS, 2 * HEAD), jnp.float32),
+            pltpu.SemaphoreType.DMA((STEPS, 3)),
+        ],
+        compiler_params=pltpu.CompilerParams(vmem_limit_bytes=16 << 20),
+        cost_estimate=pl.CostEstimate(
+            flops=2 * ROWS * WIDTH * 256, bytes_accessed=9_500_000, transcendentals=0
+        ),
+        name="project_keys",
+    )(lens, tokens, wk, wv, gain, target)
+
+
+def queries_kernel(x_ref, wq_ref, q_ref, x_held, q_held, sems):
+    part = [pl.ds(j * STEP, STEP) for j in range(STEPS)]
+    copies = fetch([
+        ((x_ref.at[:, part[j]], x_held.at[j]), (wq_ref.at[part[j], :], q_held.at[j]))
+        for j in range(STEPS)
+    ], sems)
     for j in range(STEPS):
         for copy in copies[j]:
             copy.wait()
         q = dot(x_held[j], q_held[j])
-        kv = dot(x_held[j], kv_held[j])
         if j == 0:
-            side_ref[:, :COS] = q
-            acc[...] = kv
+            q_ref[...] = q
         else:
-            side_ref[:, :COS] += q
-            acc[...] += kv
-    key = turn(unit(acc[:, :HEAD], gain_ref[...]), side_ref[:, COS:SIN], side_ref[:, SIN:AUX])
-    kv_ref[:, :HEAD] = key.astype(jnp.bfloat16)
-    kv_ref[:, HEAD:] = acc[:, HEAD:].astype(jnp.bfloat16)
-
-
-def project(lens, tokens, wq, wk, wv, gain, target):
+            q_ref[...] += q
+
+
+def project_queries(tokens, wq):
     near, far = pl.BlockSpec(memory_space=pltpu.VMEM), pl.BlockSpec(memory_space=pltpu.HBM)
     return pl.pallas_call(
-        project_kernel,
-        in_specs=[pl.BlockSpec(memory_space=pltpu.SMEM)] + [far] * 4 + [near] * 2,
-        out_specs=[near] * 2,
-        out_shape=[
-            jax.ShapeDtypeStruct((ROWS, SIDE), jnp.float32),
-            jax.ShapeDtypeStruct((ROWS, 2 * HEAD), jnp.bfloat16),
-        ],
+        queries_kernel,
+        in_specs=[far] * 2,
+        out_specs=near,
+        out_shape=jax.ShapeDtypeStruct((ROWS, 2 * HEAD), jnp.float32),
         scratch_shapes=[
             pltpu.VMEM((STEPS, ROWS, STEP), jnp.bfloat16),
             pltpu.VMEM((STEPS, STEP, 2 * HEAD), jnp.bfloat16),
-            pltpu.VMEM((STEPS, STEP, 2 * HEAD), jnp.bfloat16),
-            pltpu.VMEM((ROWS, 2 * HEAD), jnp.float32),
-            pltpu.SemaphoreType.DMA((STEPS, 4)),
-        ],
+            pltpu.SemaphoreType.DMA((STEPS, 2)),
+        ],
+        compiler_params=pltpu.CompilerParams(vmem_limit_bytes=16 << 20),
         cost_estimate=pl.CostEstimate(
-            flops=2 * ROWS * WIDTH * 512, bytes_accessed=12_500_000, transcendentals=0
+            flops=2 * ROWS * WIDTH * 256, bytes_accessed=8_800_000, transcendentals=0
         ),
-        compiler_params=pltpu.CompilerParams(vmem_limit_bytes=20 << 20),
-        name="project",
-    )(lens, tokens, wq, wk, wv, gain, target)
+        name="project_queries",
+    )(tokens, wq)
 
 
 def adapt_kernel(*refs):
@@ -182,10 +236,17 @@
         copy.start()
     for copy in copies:
         copy.wait()
-    low = jnp.zeros((X * CAP, RANK), jnp.float32)
-    for w in range(T):
-        first = w * SLICE // 128 * 128
-        low += dot(packed[:, first:first + PAD], held[w, :, :PAD], 1, 1)
+    chunks = [(w, n * 256) for w in range(T) for n in range(PAD // 256)]
+    groups = len(chunks) // 4
+    left, right = [], []
+    for j in range(4):
+        mine = chunks[j * groups:(j + 1) * groups]
+        firsts = [w * SLICE // 128 * 128 + n for w, n in mine]
+        left.append(jnp.concatenate([packed[:, at:at + 256] for at in firsts], axis=1))
+        right.append(jnp.concatenate([held[w, :, n:n + 256] for w, n in mine], axis=1))
+    low = dot(jnp.concatenate(left, axis=0), jnp.concatenate(right, axis=0), 1, 1)
+    low = sum(
+        low[j * X * CAP:(j + 1) * X * CAP, j * RANK:(j + 1) * RANK] for j in range(4))
     low = low.astype(jnp.bfloat16)
     for w in range(T):
         delta = dot(low, held[w, :, PAD:]).astype(jnp.bfloat16)
@@ -212,12 +273,13 @@
     )(*rows, *weights)
 
 
-def attend_kernel(delta_hbm, side_hbm, kv0_hbm, kv1_hbm, kv2_hbm, gain_ref, out_ref,
-                  delta_ref, side_ref, kv_ref, sems):
+def attend_kernel(delta_hbm, q_hbm, side_hbm, kv0_hbm, kv1_hbm, kv2_hbm, gain_ref, out_ref,
+                  delta_ref, q_ref, side_ref, kv_ref, sems):
     half = ROWS // 2
     pairs = [
         (side_hbm.at[:, pl.ds(AUX, HEAD)], side_ref.at[:, pl.ds(AUX, HEAD)]),
         (delta_hbm, delta_ref),
+        (q_hbm, q_ref),
         (side_hbm.at[:, pl.ds(0, AUX)], side_ref.at[:, pl.ds(0, AUX)]),
     ] + [
         (source.at[:, pl.ds(n * HEAD, HEAD)], kv_ref.at[pl.ds(b * ROWS, ROWS), pl.ds(n * HEAD, HEAD)])
@@ -239,14 +301,15 @@
     copies[1].wait()
     delta = dot(chosen, delta_ref[...])
     copies[2].wait()
-    query = side_ref[:, :COS] + delta
+    copies[3].wait()
+    query = q_ref[...] + delta
     gain = gain_ref[...] * (QUERY_SCALE * LOG2E)
     turned = [
         turn(unit(query[:, h * HEAD:(h + 1) * HEAD], gain), side_ref[:, COS:SIN],
              side_ref[:, SIN:AUX]).astype(jnp.bfloat16)
         for h in range(2)
     ]
-    for copy in copies[3:]:
+    for copy in copies[4:]:
         copy.wait()
     for tile in range(2):
         here = slice(tile * half, (tile + 1) * half)
@@ -270,14 +333,15 @@
     near, far = pl.BlockSpec(memory_space=pltpu.VMEM), pl.BlockSpec(memory_space=pl.ANY)
     return pl.pallas_call(
         attend_kernel,
-        in_specs=[far] * 5 + [near],
+        in_specs=[far] * 6 + [near],
         out_specs=near,
         out_shape=jax.ShapeDtypeStruct((ROWS, 2 * HEAD), jnp.bfloat16),
         scratch_shapes=[
             pltpu.VMEM((SLOTS, UP), jnp.bfloat16),
+            pltpu.VMEM((ROWS, 2 * HEAD), jnp.float32),
             pltpu.VMEM((ROWS, SIDE), jnp.float32),
             pltpu.VMEM((3 * ROWS, 3 * HEAD), jnp.bfloat16),
-            pltpu.SemaphoreType.DMA((9,)),
+            pltpu.SemaphoreType.DMA((10,)),
         ],
         compiler_params=pltpu.CompilerParams(vmem_limit_bytes=24 << 20),
         cost_estimate=pl.CostEstimate(
@@ -291,20 +355,14 @@
     tokens, query_weight, key_weight, value_weight, query_norm_gain, key_norm_gain,
     adapter_down_weight, adapter_up_weight, token_adapter_index, packed_prompt_length,
 ):
-    tokens, query_weight, key_weight, value_weight = [
+    down = jnp.swapaxes(adapter_down_weight[0], 0, 1)
+    index = token_adapter_index.reshape(1, ROWS)
+    tokens, query_weight, key_weight, value_weight, down, up, index = [
         pltpu.with_memory_space_constraint(v, pltpu.HBM)
-        for v in (tokens, query_weight, key_weight, value_weight)
-    ]
-    t = lax.axis_index("tp")
-    down = jnp.swapaxes(adapter_down_weight[0], 0, 1)
-    shift = lax.rem(t * SLICE, 128)
-    carried = functools.reduce(
-        lambda other, at: jnp.where(
-            shift == at, jnp.pad(down, ((0, 0), (at, PAD + UP - SLICE - at))), other),
-        (32, 64, 96), jnp.pad(down, ((0, 0), (0, PAD + UP - SLICE))))
-    carried = jnp.where(
-        jnp.arange(PAD + UP)[None, :] < PAD, carried,
-        jnp.pad(adapter_up_weight[0], ((0, 0), (PAD, 0))))
+        for v in (tokens, query_weight, key_weight, value_weight, down, adapter_up_weight[0], index)
+    ]
+    *rows, target, carried = pack(
+        index, down, up, tokens)
     single, other = [
         lax.ppermute(
             carried, ("z", "tp"),
@@ -317,15 +375,15 @@
             double if d in (1, Z - 1) else single, "z", [((i + d) % Z, i) for i in range(Z)])
         for d in NEAR[1:]
     ]
-    *rows, target = pack(token_adapter_index.reshape(1, ROWS), tokens)
     rows = [rows[0]] + [
         lax.ppermute(
             rows[d], "x", [(i, (i + d) % X) for i in range(X)])
         for d in range(1, X)
     ]
-    side, kv = project(
-        packed_prompt_length, tokens, query_weight, key_weight, value_weight,
+    side, kv = project_keys(
+        packed_prompt_length, tokens, key_weight, value_weight,
         key_norm_gain.reshape(1, HEAD), target)
+    query = project_queries(tokens, query_weight)
     kv1, kv0 = [
         lax.ppermute(
             kv, ("x", "z"), [(i, i + d) for i in range(X * Z - d)])
@@ -335,7 +393,7 @@
     delta = lax.all_to_all(
         delta.reshape(X * T, CAP, UP), ("x", "tp"), 0, 0)
     return attend(
-        delta.reshape(SLOTS, UP), side, kv0, kv1, kv, query_norm_gain.reshape(1, HEAD))
+        delta.reshape(SLOTS, UP), query, side, kv0, kv1, kv, query_norm_gain.reshape(1, HEAD))
 
 
 def solution(mesh):

time: 87.3 us -> 87.5 us (level)
  the two profiles are of different devices: /device:TPU:6 before, /device:TPU:34 now
where the time goes in v3:
time: 87.5 us; the launch traced here: 87.2 us
  starting transfers between devices  36.6 us (42%)
  waiting for transfers between devices  26.4 us (30%)
  Pallas kernels  23.9 us (27%)
    ppermute x2, starting transfers between devices, layer(): lax.ppermute(carried, ('z', 'tp'), [(a * T + w, (a + w + d) % Z * T + a)...  12.9 us
    ppermute x2, waiting for transfers between devices, layer(): lax.ppermute(kv, ('x', 'z'), [(i, i + d) for i in range(X * Z - d)])  10.7 us
    ppermute x4, waiting for transfers between devices, layer(): lax.ppermute(double if d in (1, Z - 1) else single, 'z', [((i + d) % Z, i...  10.3 us
    ppermute x2, starting transfers between devices, layer(): lax.ppermute(kv, ('x', 'z'), [(i, i + d) for i in range(X * Z - d)])  9.77 us
    all_to_all x1, starting transfers between devices, layer(): delta = lax.all_to_all(delta.reshape(X * T, CAP, UP), ('x', 'tp'), 0, 0)  6.71 us
    pallas_call x1, Pallas kernels, project_keys(): pl.pallas_call(keys_kernel, in_specs=[pl.BlockSpec(memory_space=pltpu.SME...  5.72 us
    pallas_call x1, Pallas kernels, attend(): pl.pallas_call(attend_kernel, in_specs=[far] * 6 + [near], out_specs=near...  5.19 us
    pallas_call x1, Pallas kernels, pack(): pl.pallas_call(pack_kernel, in_specs=[pl.BlockSpec(memory_space=pltpu.HBM...  4.52 us
  transfers between devices with their start and end apart: 12, of which 7 were waited for; matrix products, arithmetic and copies ran while one was open for 0% of the time, Pallas kernels for 12%

profile of v3, /device:TPU:34, one launch (start us, length us, event | category | flops | bytes accessed | tf_op | source)
XLA Modules:
  0.0 87.2 jit_solution(7985174869779725718)
XLA Ops:
  0.0 4.5 %pack.1 = (bf16[32,5376]{1,0:T(8,128)(2,1)S(1)}, bf16[32,5376]{1,0:T(8,128)(2,1)S(1)}, bf16[32,5376]{1,0:T(8,128)(2,1)S(1)}, bf16[32,5376]{1,0:T(8,128)(2,1)S(1)...) custom-call(s32[1,512]{1,0:T(1,128)} %bitcast.14, bf16[64,672]{1,0:T(8,128)(2,1)} %bitcast.12, ...), custom_call_target="tpu_custom_call" | custom-call | flops 704643072 | bytes 7000000 | tf_op jit(solution)/shard_map/pack/pallas_call | solution.py:77
  4.5 0.0 copy-start
  4.5 0.0 copy-start.1
  4.6 1.9 %collective-permute-start.3 = (bf16[64,1024]{1,0:T(8,128)(2,1)S(1)}, bf16[64,1024]{1,0:T(8,128)(2,1)S(1)}, u32[]{:S(2)}, u32[]{:S(2)}) collective-permute-start(bf16[64,1024]{1,0:T(8,128)(2,1)S(1)} %get-tuple-element.17), channel_id=1, source_target_pairs={{0,0},{1,8},{2,16},{3,24},{4,32},{5,40},{6,48},{7,56},{8,9},{9,17}... | collective-permute-start | bytes 393224 | tf_op jit(solution)/shard_map/ppermute | solution.py:367
  6.5 11.0 %collective-permute-start.4 = (bf16[64,1024]{1,0:T(8,128)(2,1)S(1)}, bf16[64,1024]{1,0:T(8,128)(2,1)S(1)}, u32[]{:S(2)}, u32[]{:S(2)}) collective-permute-start(bf16[64,1024]{1,0:T(8,128)(2,1)S(1)} %get-tuple-element.17), channel_id=1, source_target_pairs={{0,32},{1,40},{2,48},{3,56},{4,0},{5,8},{6,16},{7,24},{8,41},{9,49... | collective-permute-start | bytes 393224 | tf_op jit(solution)/shard_map/ppermute | solution.py:367
  17.5 1.6 %collective-permute-start = (bf16[32,5376]{1,0:T(8,128)(2,1)S(1)}, bf16[32,5376]{1,0:T(8,128)(2,1)S(1)}, u32[]{:S(2)}, u32[]{:S(2)}) collective-permute-start(bf16[32,5376]{1,0:T(8,128)(2,1)S(1)} %get-tuple-element.14), channel_id=1, source_target_pairs={{0,64},{64,128},{128,192},{192,0},{1,65},{65,129},{129,193},{193,1... | collective-permute-start | bytes 1032200 | tf_op jit(solution)/shard_map/ppermute | solution.py:379
  19.1 1.1 %collective-permute-start.1 = (bf16[32,5376]{1,0:T(8,128)(2,1)S(1)}, bf16[32,5376]{1,0:T(8,128)(2,1)S(1)}, u32[]{:S(2)}, u32[]{:S(2)}) collective-permute-start(bf16[32,5376]{1,0:T(8,128)(2,1)S(1)} %get-tuple-element.15), channel_id=1, source_target_pairs={{0,128},{64,192},{128,0},{192,64},{1,129},{65,193},{129,1},{193,65... | collective-permute-start | bytes 1032200 | tf_op jit(solution)/shard_map/ppermute | solution.py:379
  20.2 0.0 collective-permute-done.3
  20.2 1.2 %collective-permute-start.7 = (bf16[64,1024]{1,0:T(8,128)(2,1)S(1)}, bf16[64,1024]{1,0:T(8,128)(2,1)S(1)}, u32[]{:S(2)}, u32[]{:S(2)}) collective-permute-start(bf16[64,1024]{1,0:T(8,128)(2,1)S(1)} %collective-permute-done.3), channel_id=1, source_target_pairs={{16,0},{24,8},{32,16},{40,24},{48,32},{56,40},{0,48},{8,56},{17,1}... | collective-permute-start | bytes 393224 | tf_op jit(solution)/shard_map/ppermute | solution.py:374
  21.4 1.7 %collective-permute-start.8 = (bf16[64,1024]{1,0:T(8,128)(2,1)S(1)}, bf16[64,1024]{1,0:T(8,128)(2,1)S(1)}, u32[]{:S(2)}, u32[]{:S(2)}) collective-permute-start(bf16[64,1024]{1,0:T(8,128)(2,1)S(1)} %collective-permute-done.3), channel_id=1, source_target_pairs={{48,0},{56,8},{0,16},{8,24},{16,32},{24,40},{32,48},{40,56},{49,1}... | collective-permute-start | bytes 393224 | tf_op jit(solution)/shard_map/ppermute | solution.py:374
  23.1 1.6 %collective-permute-done.4 = bf16[64,1024]{1,0:T(8,128)(2,1)S(1)} collective-permute-done((bf16[64,1024]{1,0:T(8,128)(2,1)S(1)}, bf16[64,1024]{1,0:T(8,128)(2,1)S(1)}, u32[]{:S(2)}, u32[]{:S(2)}) %collective-permute-start.4) | collective-permute-done | bytes 131104 | tf_op jit(solution)/shard_map/ppermute | solution.py:367
  24.7 0.7 collective-permute-start.2
  25.4 6.4 %collective-permute-done.7.refs_7_ = bf16[64,1024]{1,0:T(8,128)(2,1)S(1)} collective-permute-done((bf16[64,1024]{1,0:T(8,128)(2,1)S(1)}, bf16[64,1024]{1,0:T(8,128)(2,1)S(1)}, u32[]{:S(2)}, u32[]{:S(2)}) %collective-permute-start.7) | collective-permute-done | bytes 131104 | tf_op jit(solution)/shard_map/ppermute | solution.py:374
  31.8 0.0 collective-permute-start.5
  31.8 1.1 %collective-permute-done.8.refs_8_ = bf16[64,1024]{1,0:T(8,128)(2,1)S(1)} collective-permute-done((bf16[64,1024]{1,0:T(8,128)(2,1)S(1)}, bf16[64,1024]{1,0:T(8,128)(2,1)S(1)}, u32[]{:S(2)}, u32[]{:S(2)}) %collective-permute-start.8) | collective-permute-done | bytes 131104 | tf_op jit(solution)/shard_map/ppermute | solution.py:374
  32.9 0.9 %collective-permute-start.6 = (bf16[128,1024]{1,0:T(8,128)(2,1)S(1)}, bf16[128,1024]{1,0:T(8,128)(2,1)S(1)}, u32[]{:S(2)}, u32[]{:S(2)}) collective-permute-start(bf16[128,1024]{1,0:T(8,128)(2,1)S(1)} %constant_dynamic-update-slice_fusion.refs_4_), channel_id=1, source_target_pairs={{56,0},{0,8},{8,16},{16,24},{24,32},{32,40},{40,48},{48,56},{57,1}... | collective-permute-start | bytes 786440 | tf_op jit(solution)/shard_map/ppermute | solution.py:374
  33.8 0.0 collective-permute-done.refs_1_
  33.8 0.0 collective-permute-done.1.refs_2_
  33.8 3.9 %collective-permute-done.2.refs_3_ = bf16[32,5376]{1,0:T(8,128)(2,1)S(1)} collective-permute-done((bf16[32,5376]{1,0:T(8,128)(2,1)S(1)}, bf16[32,5376]{1,0:T(8,128)(2,1)S(1)}, u32[]{:S(2)}, u32[]{:S(2)}) %collective-permute-start.2) | collective-permute-done | bytes 344096 | tf_op jit(solution)/shard_map/ppermute | solution.py:379
  37.7 2.2 %collective-permute-done.5.refs_5_ = bf16[128,1024]{1,0:T(8,128)(2,1)S(1)} collective-permute-done((bf16[128,1024]{1,0:T(8,128)(2,1)S(1)}, bf16[128,1024]{1,0:T(8,128)(2,1)S(1)}, u32[]{:S(2)}, u32[]{:S(2)}) %collective-permute-start.5) | collective-permute-done | bytes 262176 | tf_op jit(solution)/shard_map/ppermute | solution.py:374
  39.9 0.6 collective-permute-done.6.refs_6_
  40.4 3.9 %adapt.1 = bf16[4,8,32,256]{3,2,1,0:T(8,128)(2,1)} custom-call(bf16[32,5376]{1,0:T(8,128)(2,1)S(1)} %get-tuple-element.13.refs_0_, bf16[32,5376]{1,0:T(8,128)(2,1)S(1)} %collective-permute-done.refs_1_, bf16[32,5376]{1,0:T(8,128)(2,1)S(1)} %collective-permute-done.1.refs_2_, bf16[32,5376]{1,0:T(8,128)(2,1)S(1)} %collective-permute-done.2.refs_3_, ...), custom_call_target="tpu_custom_call" | custom-call | flops 121634816 | bytes 3000000 | tf_op jit(solution)/shard_map/adapt/pallas_call | solution.py:258
  44.4 6.7 %all-to-all-start = ((bf16[32,32,256]{2,1,0:T(8,128)(2,1)}), bf16[32,32,256]{2,1,0:T(8,128)(2,1)S(1)}, u32[]{:S(2)}, u32[]{:S(2)}) async-start(bf16[32,32,256]{2,1,0:T(8,128)(2,1)} %bitcast.4), calls=%async_computation | async-start | bytes 1048576 | tf_op jit(solution)/shard_map/all_to_all | solution.py:393
  51.1 5.7 %project_keys.1 = (f32[512,384]{1,0:T(8,128)S(1)}, bf16[512,256]{1,0:T(8,128)(2,1)S(1)}) custom-call(s32[16]{0:T(128)S(1)} %copy-done, bf16[512,5376]{1,0:T(8,128)(2,1)} %x_ref.5, bf16[5376,128]{1,0:T(8,128)(2,1)} %wk_ref.1, bf16[5376,128]{1,0:T(8,128)(2,1)} %wv_ref.1, f32[1,128]{1,0:T(1,128)S(1)} %bitcast.10, s32[1,512]{1,0:T(1,128)S(1)} %get-tuple-element.18.target_ref), custom_call_target="tpu_custom_call" | custom-call | flops 1409286144 | bytes 9500000 | tf_op jit(solution)/shard_map/project_keys/pallas_call | solution.py:164
  56.9 0.0 copy-start.2
  56.9 2.2 %collective-permute-start.10 = (bf16[512,256]{1,0:T(8,128)(2,1)S(1)}, bf16[512,256]{1,0:T(8,128)(2,1)S(1)}, u32[]{:S(2)}, u32[]{:S(2)}) collective-permute-start(bf16[512,256]{1,0:T(8,128)(2,1)S(1)} %get-tuple-element.20.kv2_hbm), channel_id=1, source_target_pairs={{0,8},{8,16},{16,24},{24,32},{32,40},{40,48},{48,56},{56,64},{64,7... | collective-permute-start | bytes 786440 | tf_op jit(solution)/shard_map/ppermute | solution.py:388
  59.1 7.6 %collective-permute-start.9 = (bf16[512,256]{1,0:T(8,128)(2,1)S(1)}, bf16[512,256]{1,0:T(8,128)(2,1)S(1)}, u32[]{:S(2)}, u32[]{:S(2)}) collective-permute-start(bf16[512,256]{1,0:T(8,128)(2,1)S(1)} %get-tuple-element.20.kv2_hbm), channel_id=1, source_target_pairs={{0,16},{8,24},{16,32},{24,40},{32,48},{40,56},{48,64},{56,72},{64,... | collective-permute-start | bytes 786440 | tf_op jit(solution)/shard_map/ppermute | solution.py:388
  66.7 4.5 %project_queries.1.q_hbm = f32[512,256]{1,0:T(8,128)S(1)} custom-call(bf16[512,5376]{1,0:T(8,128)(2,1)} %x_ref.5, bf16[5376,256]{1,0:T(8,128)(2,1)} %wq_ref.1), custom_call_target="tpu_custom_call" | custom-call | flops 1409286144 | bytes 8800000 | tf_op jit(solution)/shard_map/project_queries/pallas_call | solution.py:204
  71.2 0.0 collective-permute-done.10.kv1_hbm
  71.2 10.7 %collective-permute-done.9.kv0_hbm = bf16[512,256]{1,0:T(8,128)(2,1)S(1)} collective-permute-done((bf16[512,256]{1,0:T(8,128)(2,1)S(1)}, bf16[512,256]{1,0:T(8,128)(2,1)S(1)}, u32[]{:S(2)}, u32[]{:S(2)}) %collective-permute-start.9) | collective-permute-done | bytes 262176 | tf_op jit(solution)/shard_map/ppermute | solution.py:388
  81.8 0.0 all-to-all-done
  81.8 5.2 %attend.1 = bf16[512,256]{1,0:T(8,128)(2,1)} custom-call(bf16[1024,256]{1,0:T(8,128)(2,1)S(1)} %bitcast.9, f32[512,256]{1,0:T(8,128)S(1)} %project_queries.1.q_hbm, f32[512,384]{1,0:T(8,128)S(1)} %get-tuple-element.19.side_hbm, bf16[512,256]{1,0:T(8,128)(2,1)S(1)} %collective-permute-done.9.kv0_hbm, bf16[512,256]{1,0:T(8,128)(2,1)S(1)} %collective-permute-done.10.kv1_hbm, ...), custom_call_target="tpu_custom_call" | custom-call | flops 671088640 | bytes 4000000 | tf_op jit(solution)/shard_map/attend/pallas_call | solution.py:334
  (5 shorter events, 0.0 us)
Async XLA Ops:
  4.5 46.6 %copy-start = (s32[16]{0:T(128)S(1)}, s32[16]{0:T(128)}, u32[]{:S(2)}) copy-start(s32[16]{0:T(128)} %lens_ref.1) | copy-start | bytes 196
  4.5 46.6 %copy-start.1 = (f32[128]{0:T(128)S(1)}, f32[128]{0:T(128)}, u32[]{:S(2)}) copy-start(f32[128]{0:T(128)} %param.15) | copy-start | bytes 1540
  4.6 15.6 %collective-permute-start.3 = (bf16[64,1024]{1,0:T(8,128)(2,1)S(1)}, bf16[64,1024]{1,0:T(8,128)(2,1)S(1)}, u32[]{:S(2)}, u32[]{:S(2)}) collective-permute-start(bf16[64,1024]{1,0:T(8,128)(2,1)S(1)} %get-tuple-element.17), channel_id=1, source_target_pairs={{0,0},{1,8},{2,16},{3,24},{4,32},{5,40},{6,48},{7,56},{8,9},{9,17}... | collective-permute-start | bytes 393224 | tf_op jit(solution)/shard_map/ppermute | solution.py:367
  6.5 18.2 %collective-permute-start.4 = (bf16[64,1024]{1,0:T(8,128)(2,1)S(1)}, bf16[64,1024]{1,0:T(8,128)(2,1)S(1)}, u32[]{:S(2)}, u32[]{:S(2)}) collective-permute-start(bf16[64,1024]{1,0:T(8,128)(2,1)S(1)} %get-tuple-element.17), channel_id=1, source_target_pairs={{0,32},{1,40},{2,48},{3,56},{4,0},{5,8},{6,16},{7,24},{8,41},{9,49... | collective-permute-start | bytes 393224 | tf_op jit(solution)/shard_map/ppermute | solution.py:367
  17.5 16.3 %collective-permute-start = (bf16[32,5376]{1,0:T(8,128)(2,1)S(1)}, bf16[32,5376]{1,0:T(8,128)(2,1)S(1)}, u32[]{:S(2)}, u32[]{:S(2)}) collective-permute-start(bf16[32,5376]{1,0:T(8,128)(2,1)S(1)} %get-tuple-element.14), channel_id=1, source_target_pairs={{0,64},{64,128},{128,192},{192,0},{1,65},{65,129},{129,193},{193,1... | collective-permute-start | bytes 1032200 | tf_op jit(solution)/shard_map/ppermute | solution.py:379
  19.1 14.7 %collective-permute-start.1 = (bf16[32,5376]{1,0:T(8,128)(2,1)S(1)}, bf16[32,5376]{1,0:T(8,128)(2,1)S(1)}, u32[]{:S(2)}, u32[]{:S(2)}) collective-permute-start(bf16[32,5376]{1,0:T(8,128)(2,1)S(1)} %get-tuple-element.15), channel_id=1, source_target_pairs={{0,128},{64,192},{128,0},{192,64},{1,129},{65,193},{129,1},{193,65... | collective-permute-start | bytes 1032200 | tf_op jit(solution)/shard_map/ppermute | solution.py:379
  20.2 11.6 %collective-permute-start.7 = (bf16[64,1024]{1,0:T(8,128)(2,1)S(1)}, bf16[64,1024]{1,0:T(8,128)(2,1)S(1)}, u32[]{:S(2)}, u32[]{:S(2)}) collective-permute-start(bf16[64,1024]{1,0:T(8,128)(2,1)S(1)} %collective-permute-done.3), channel_id=1, source_target_pairs={{16,0},{24,8},{32,16},{40,24},{48,32},{56,40},{0,48},{8,56},{17,1}... | collective-permute-start | bytes 393224 | tf_op jit(solution)/shard_map/ppermute | solution.py:374
  21.4 11.5 %collective-permute-start.8 = (bf16[64,1024]{1,0:T(8,128)(2,1)S(1)}, bf16[64,1024]{1,0:T(8,128)(2,1)S(1)}, u32[]{:S(2)}, u32[]{:S(2)}) collective-permute-start(bf16[64,1024]{1,0:T(8,128)(2,1)S(1)} %collective-permute-done.3), channel_id=1, source_target_pairs={{48,0},{56,8},{0,16},{8,24},{16,32},{24,40},{32,48},{40,56},{49,1}... | collective-permute-start | bytes 393224 | tf_op jit(solution)/shard_map/ppermute | solution.py:374
  24.7 13.0 %collective-permute-start.2 = (bf16[32,5376]{1,0:T(8,128)(2,1)S(1)}, bf16[32,5376]{1,0:T(8,128)(2,1)S(1)}, u32[]{:S(2)}, u32[]{:S(2)}) collective-permute-start(bf16[32,5376]{1,0:T(8,128)(2,1)S(1)} %get-tuple-element.16), channel_id=1, source_target_pairs={{0,192},{64,0},{128,64},{192,128},{1,193},{65,1},{129,65},{193,129... | collective-permute-start | bytes 1032200 | tf_op jit(solution)/shard_map/ppermute | solution.py:379
  31.8 8.1 %collective-permute-start.5 = (bf16[128,1024]{1,0:T(8,128)(2,1)S(1)}, bf16[128,1024]{1,0:T(8,128)(2,1)S(1)}, u32[]{:S(2)}, u32[]{:S(2)}) collective-permute-start(bf16[128,1024]{1,0:T(8,128)(2,1)S(1)} %constant_dynamic-update-slice_fusion.refs_4_), channel_id=1, source_target_pairs={{8,0},{16,8},{24,16},{32,24},{40,32},{48,40},{56,48},{0,56},{9,1},... | collective-permute-start | bytes 786440 | tf_op jit(solution)/shard_map/ppermute | solution.py:374
  32.9 7.6 %collective-permute-start.6 = (bf16[128,1024]{1,0:T(8,128)(2,1)S(1)}, bf16[128,1024]{1,0:T(8,128)(2,1)S(1)}, u32[]{:S(2)}, u32[]{:S(2)}) collective-permute-start(bf16[128,1024]{1,0:T(8,128)(2,1)S(1)} %constant_dynamic-update-slice_fusion.refs_4_), channel_id=1, source_target_pairs={{56,0},{0,8},{8,16},{16,24},{24,32},{32,40},{40,48},{48,56},{57,1}... | collective-permute-start | bytes 786440 | tf_op jit(solution)/shard_map/ppermute | solution.py:374
  44.4 37.4 %all-to-all-start = ((bf16[32,32,256]{2,1,0:T(8,128)(2,1)}), bf16[32,32,256]{2,1,0:T(8,128)(2,1)S(1)}, u32[]{:S(2)}, u32[]{:S(2)}) async-start(bf16[32,32,256]{2,1,0:T(8,128)(2,1)} %bitcast.4), calls=%async_computation | async-start | bytes 1048576 | tf_op jit(solution)/shard_map/all_to_all | solution.py:393
  56.9 25.0 %copy-start.2 = (f32[128]{0:T(128)S(1)}, f32[128]{0:T(128)}, u32[]{:S(2)}) copy-start(f32[128]{0:T(128)} %param.14) | copy-start | bytes 1540
  56.9 14.3 %collective-permute-start.10 = (bf16[512,256]{1,0:T(8,128)(2,1)S(1)}, bf16[512,256]{1,0:T(8,128)(2,1)S(1)}, u32[]{:S(2)}, u32[]{:S(2)}) collective-permute-start(bf16[512,256]{1,0:T(8,128)(2,1)S(1)} %get-tuple-element.20.kv2_hbm), channel_id=1, source_target_pairs={{0,8},{8,16},{16,24},{24,32},{32,40},{40,48},{48,56},{56,64},{64,7... | collective-permute-start | bytes 786440 | tf_op jit(solution)/shard_map/ppermute | solution.py:388
  59.1 22.8 %collective-permute-start.9 = (bf16[512,256]{1,0:T(8,128)(2,1)S(1)}, bf16[512,256]{1,0:T(8,128)(2,1)S(1)}, u32[]{:S(2)}, u32[]{:S(2)}) collective-permute-start(bf16[512,256]{1,0:T(8,128)(2,1)S(1)} %get-tuple-element.20.kv2_hbm), channel_id=1, source_target_pairs={{0,16},{8,24},{16,32},{24,40},{32,48},{40,56},{48,64},{56,72},{64,... | collective-permute-start | bytes 786440 | tf_op jit(solution)/shard_map/ppermute | solution.py:388

commit v4 on v3

v4 whole, which is shorter than its diff:
```python
import jax
import jax.numpy as jnp
from jax import lax
from jax.experimental import pallas as pl
from jax.experimental.pallas import tpu as pltpu
from jax.sharding import Mesh, PartitionSpec as P

WINDOW = 1024
QUERY_SCALE = 0.07715167498104596
LOG2E = 1.4426950408889634
X, Z, T = 4, 8, 8
ROWS, WIDTH, HEAD, RANK, CAP = 512, 5376, 128, 64, 32
SLICE = WIDTH // T
PAD = 768
STEP = 768
STEPS = WIDTH // STEP
UP = 256
SLOTS = X * T * CAP
COS, SIN, AUX, SIDE = 0, HEAD, 2 * HEAD, 3 * HEAD
NEAR = (0, 1, Z - 1, 2, Z - 2)
SPLIT = (2, 2, 2, 1, 1)
PARTS = len(NEAR)


def dot(a, b, ca=1, cb=0):
    return lax.dot_general(a, b, (((ca,), (cb,)), ((), ())), preferred_element_type=jnp.float32)


def unit(field, gain):
    return field / jnp.sqrt(jnp.mean(field * field, axis=-1, keepdims=True) + 1e-06) * gain


def turn(field, cosine, sine):
    return field * cosine + pltpu.roll(field, HEAD // 2, 1) * sine


def fetch(pairs, sems):
    copies = [
        [pltpu.make_async_copy(source, target, sems.at[j, n])
         for n, (source, target) in enumerate(group)]
        for j, group in enumerate(pairs)
    ]
    for group in copies:
        for copy in group:
            copy.start()
    return copies


def front_kernel(
    lens_ref, gain_ref, idx_hbm, down_hbm, up_hbm, x_hbm, wk_hbm, wv_hbm,
    out0, out1, out2, out3, carried_ref, side_ref, kv_ref,
    pick, wide, idx_ref, down_ref, x_held, kv_held, acc, small_sems, sems,
):
    part = [pl.ds(j * STEP, STEP) for j in range(STEPS)]
    small = [
        pltpu.make_async_copy(source, target, small_sems.at[n])
        for n, (source, target) in enumerate((
            (idx_hbm, idx_ref), (down_hbm, down_ref),
            (up_hbm, carried_ref.at[:, pl.ds(PAD, UP)])))
    ]
    for copy in small:
        copy.start()
    copies = fetch([
        ((x_hbm.at[:, part[j]], x_held.at[j]),
         (wk_hbm.at[part[j], :], kv_held.at[j, :, pl.ds(0, HEAD)]),
         (wv_hbm.at[part[j], :], kv_held.at[j, :, pl.ds(HEAD, HEAD)]))
        for j in range(STEPS)
    ], sems)
    x, z, t = lax.axis_index("x"), lax.axis_index("z"), lax.axis_index("tp")
    small[0].wait()
    idx = idx_ref[...]
    named = lax.broadcasted_iota(jnp.int32, (X * T, ROWS), 0) == idx
    earlier = lax.broadcasted_iota(jnp.int32, (ROWS, ROWS), 0) < lax.broadcasted_iota(
        jnp.int32, (ROWS, ROWS), 1
    )
    before = dot(named.astype(jnp.float32).astype(jnp.bfloat16),
                 earlier.astype(jnp.float32).astype(jnp.bfloat16))
    rank = jnp.sum(jnp.where(named, before, 0.0), axis=0, keepdims=True).astype(jnp.int32)
    target = idx * CAP + rank
    slot = lax.broadcasted_iota(jnp.int32, (CAP, ROWS), 0)
    for d in range(X):
        adapter = lax.rem(x + d, X) * T + t
        pick[d * CAP:(d + 1) * CAP, :] = (
            (slot + adapter * CAP == target).astype(jnp.float32).astype(jnp.bfloat16)
        )
    small[1].wait()
    wide[:, PAD - 128:] = jnp.zeros((RANK, 128), jnp.float32)
    wide[:, :SLICE] = down_ref[...].astype(jnp.float32)
    carried_ref[:, :PAD] = pltpu.roll(wide[...], lax.rem(t * SLICE, 128), 1).astype(jnp.bfloat16)
    small[2].wait()
    begin = (x * Z + z) * ROWS
    place = begin + lax.broadcasted_iota(jnp.int32, (ROWS, HEAD), 0)
    start = jnp.zeros((ROWS, HEAD), jnp.int32)
    at = jnp.int32(0)
    for i in range(lens_ref.shape[0]):
        start = jnp.where(place >= at, at, start)
        at = at + lens_ref[i]
    lower = jnp.maximum(start, place - (WINDOW - 1)) - (begin - WINDOW)
    column = jnp.broadcast_to(target.astype(jnp.float32), (HEAD, ROWS))
    lane = lax.broadcasted_iota(jnp.int32, (ROWS, HEAD), 1)
    side_ref[:, AUX:] = jnp.where(lane < HEAD // 2, lower.astype(jnp.float32), jnp.transpose(column))
    pair = jnp.bitwise_and(lane, HEAD // 2 - 1).astype(jnp.float32)
    angle = place.astype(jnp.float32) * jnp.exp(-(2.0 * pair / HEAD) * jnp.log(jnp.float32(10000.0)))
    sine = jnp.sin(angle)
    side_ref[:, COS:SIN] = jnp.cos(angle)
    side_ref[:, SIN:AUX] = jnp.where(lane < HEAD // 2, -sine, sine)
    for j in range(STEPS):
        for copy in copies[j]:
            copy.wait()
        packed = dot(pick[...], x_held[j]).astype(jnp.bfloat16)
        for d, out in enumerate((out0, out1, out2, out3)):
            out[:, j * STEP:(j + 1) * STEP] = packed[d * CAP:(d + 1) * CAP, :]
        kv = dot(x_held[j], kv_held[j])
        if j == 0:
            acc[...] = kv
        else:
            acc[...] += kv
    key = turn(unit(acc[:, :HEAD], gain_ref[...]), side_ref[:, COS:SIN], side_ref[:, SIN:AUX])
    kv_ref[:, :HEAD] = key.astype(jnp.bfloat16)
    kv_ref[:, HEAD:] = acc[:, HEAD:].astype(jnp.bfloat16)


def front(lens, gain, idx, down, up, tokens, wk, wv):
    near, far = pl.BlockSpec(memory_space=pltpu.VMEM), pl.BlockSpec(memory_space=pltpu.HBM)
    return pl.pallas_call(
        front_kernel,
        in_specs=[pl.BlockSpec(memory_space=pltpu.SMEM), near] + [far] * 6,
        out_specs=[near] * (X + 3),
        out_shape=[jax.ShapeDtypeStruct((CAP, WIDTH), jnp.bfloat16)] * X + [
            jax.ShapeDtypeStruct((RANK, PAD + UP), jnp.bfloat16),
            jax.ShapeDtypeStruct((ROWS, SIDE), jnp.float32),
            jax.ShapeDtypeStruct((ROWS, 2 * HEAD), jnp.bfloat16),
        ],
        scratch_shapes=[
            pltpu.VMEM((X * CAP, ROWS), jnp.bfloat16),
            pltpu.VMEM((RANK, PAD), jnp.float32),
            pltpu.VMEM((1, ROWS), jnp.int32),
            pltpu.VMEM((RANK, SLICE), jnp.bfloat16),
            pltpu.VMEM((STEPS, ROWS, STEP), jnp.bfloat16),
            pltpu.VMEM((STEPS, STEP, 2 * HEAD), jnp.bfloat16),
            pltpu.VMEM((ROWS, 2 * HEAD), jnp.float32),
            pltpu.SemaphoreType.DMA((3,)),
            pltpu.SemaphoreType.DMA((STEPS, 3)),
        ],
        compiler_params=pltpu.CompilerParams(vmem_limit_bytes=18 << 20),
        cost_estimate=pl.CostEstimate(
            flops=2 * ROWS * WIDTH * 384, bytes_accessed=10_000_000, transcendentals=0
        ),
        name="front",
    )(lens, gain, idx, down, up, tokens, wk, wv)


def queries_kernel(x_ref, wq_ref, q_ref, x_held, q_held, sems):
    part = [pl.ds(j * STEP, STEP) for j in range(STEPS)]
    copies = fetch([
        ((x_ref.at[:, part[j]], x_held.at[j]), (wq_ref.at[part[j], :], q_held.at[j]))
        for j in range(STEPS)
    ], sems)
    for j in range(STEPS):
        for copy in copies[j]:
            copy.wait()
        q = dot(x_held[j], q_held[j])
        if j == 0:
            q_ref[...] = q
        else:
            q_ref[...] += q


def project_queries(tokens, wq):
    near, far = pl.BlockSpec(memory_space=pltpu.VMEM), pl.BlockSpec(memory_space=pltpu.HBM)
    return pl.pallas_call(
        queries_kernel,
        in_specs=[far] * 2,
        out_specs=near,
        out_shape=jax.ShapeDtypeStruct((ROWS, 2 * HEAD), jnp.float32),
        scratch_shapes=[
            pltpu.VMEM((STEPS, ROWS, STEP), jnp.bfloat16),
            pltpu.VMEM((STEPS, STEP, 2 * HEAD), jnp.bfloat16),
            pltpu.SemaphoreType.DMA((STEPS, 2)),
        ],
        compiler_params=pltpu.CompilerParams(vmem_limit_bytes=16 << 20),
        cost_estimate=pl.CostEstimate(
            flops=2 * ROWS * WIDTH * 256, bytes_accessed=8_800_000, transcendentals=0
        ),
        name="project_queries",
    )(tokens, wq)


def adapt_kernel(*refs):
    rows, weights, out = refs[:X], refs[X:X + PARTS], refs[X + PARTS]
    held = refs[X + PARTS + 1]
    x, z, t = lax.axis_index("x"), lax.axis_index("z"), lax.axis_index("tp")
    for d in range(PARTS):
        for n in range(SPLIT[d]):
            held[lax.rem(z - t + T + NEAR[d] + 4 * n, T)] = weights[d][n * RANK:(n + 1) * RANK, :]
    packed = jnp.concatenate([r[...] for r in rows], axis=0)
    chunks = [(w, n * 256) for w in range(T) for n in range(PAD // 256)]
    groups = len(chunks) // 4
    left, right = [], []
    for j in range(4):
        mine = chunks[j * groups:(j + 1) * groups]
        firsts = [w * SLICE // 128 * 128 + n for w, n in mine]
        left.append(jnp.concatenate([packed[:, at:at + 256] for at in firsts], axis=1))
        right.append(jnp.concatenate([held[w, :, n:n + 256] for w, n in mine], axis=1))
    low = dot(jnp.concatenate(left, axis=0), jnp.concatenate(right, axis=0), 1, 1)
    low = sum(
        low[j * X * CAP:(j + 1) * X * CAP, j * RANK:(j + 1) * RANK] for j in range(4))
    low = low.astype(jnp.bfloat16)
    for w in range(T):
        delta = dot(low, held[w, :, PAD:]).astype(jnp.bfloat16)
        for d in range(X):
            out[lax.rem(x - d + X, X), w] = delta[d * CAP:(d + 1) * CAP, :]


def adapt(rows, weights):
    return pl.pallas_call(
        adapt_kernel,
        in_specs=[pl.BlockSpec(memory_space=pltpu.VMEM)] * (X + PARTS),
        out_specs=pl.BlockSpec(memory_space=pltpu.VMEM),
        out_shape=jax.ShapeDtypeStruct((X, T, CAP, UP), jnp.bfloat16),
        scratch_shapes=[
            pltpu.VMEM((T, RANK, PAD + UP), jnp.bfloat16),
        ],
        compiler_params=pltpu.CompilerParams(vmem_limit_bytes=12 << 20),
        cost_estimate=pl.CostEstimate(
            flops=2 * 128 * RANK * (WIDTH + 2048), bytes_accessed=3_000_000, transcendentals=0
        ),
        name="adapt",
    )(*rows, *weights)


def attend_kernel(delta_ref, q_ref, side_ref, kv0, kv1, kv2, gain_ref, out_ref, kv_ref):
    half = ROWS // 2
    for b, source in enumerate((kv0, kv1, kv2)):
        kv_ref[b * ROWS:(b + 1) * ROWS, :2 * HEAD] = source[...]
    kv_ref[:, 2 * HEAD:] = jnp.ones((3 * ROWS, HEAD), jnp.bfloat16)
    slot = lax.broadcasted_iota(jnp.int32, (ROWS, HEAD), 1)
    column = jnp.broadcast_to(side_ref[:, SIDE - 1:].astype(jnp.int32), (ROWS, HEAD))
    chosen = jnp.concatenate(
        [(column == slot + c * HEAD).astype(jnp.float32).astype(jnp.bfloat16)
         for c in range(SLOTS // HEAD)], axis=1)
    delta = dot(chosen, delta_ref[...])
    query = q_ref[...] + delta
    gain = gain_ref[...] * (QUERY_SCALE * LOG2E)
    turned = [
        turn(unit(query[:, h * HEAD:(h + 1) * HEAD], gain), side_ref[:, COS:SIN],
             side_ref[:, SIN:AUX]).astype(jnp.bfloat16)
        for h in range(2)
    ]
    for tile in range(2):
        here = slice(tile * half, (tile + 1) * half)
        first, past = tile * half, tile * half + WINDOW + half
        q = jnp.concatenate([turned[0][here], turned[1][here]], axis=0)
        s = dot(q, kv_ref[first:past, :HEAD], 1, 1)
        low = side_ref[here, AUX:AUX + 1].astype(jnp.int32) - first
        at = lax.broadcasted_iota(jnp.int32, (half, WINDOW + half), 1)
        high = WINDOW + lax.broadcasted_iota(jnp.int32, (half, 1), 0)
        allowed = (at >= low) & (at <= high)
        s = jnp.where(jnp.concatenate([allowed, allowed], axis=0), s, -1e30)
        peak = jnp.max(s, axis=-1, keepdims=True)
        weights = jnp.exp2(s - peak).astype(jnp.bfloat16)
        mixed = dot(weights, kv_ref[first:past, HEAD:])
        mixed = (mixed[:, :HEAD] / mixed[:, HEAD:]).astype(jnp.bfloat16)
        out_ref[here, :HEAD] = mixed[:half]
        out_ref[here, HEAD:] = mixed[half:]


def attend(*args):
    near = pl.BlockSpec(memory_space=pltpu.VMEM)
    return pl.pallas_call(
        attend_kernel,
        in_specs=[near] * 7,
        out_specs=near,
        out_shape=jax.ShapeDtypeStruct((ROWS, 2 * HEAD), jnp.bfloat16),
        scratch_shapes=[
            pltpu.VMEM((3 * ROWS, 3 * HEAD), jnp.bfloat16),
        ],
        compiler_params=pltpu.CompilerParams(vmem_limit_bytes=24 << 20),
        cost_estimate=pl.CostEstimate(
            flops=4 * 1024 * 1280 * HEAD, bytes_accessed=4_000_000, transcendentals=1024 * 1280
        ),
        name="attend",
    )(*args)


def layer(
    tokens, query_weight, key_weight, value_weight, query_norm_gain, key_norm_gain,
    adapter_down_weight, adapter_up_weight, token_adapter_index, packed_prompt_length,
):
    down = jnp.swapaxes(adapter_down_weight[0], 0, 1)
    index = token_adapter_index.reshape(1, ROWS)
    key_gain = key_norm_gain.reshape(1, HEAD)
    (tokens, query_weight, key_weight, value_weight, down, up, index, key_gain,
     packed_prompt_length) = [
        pltpu.with_memory_space_constraint(v, pltpu.HBM)
        for v in (tokens, query_weight, key_weight, value_weight, down, adapter_up_weight[0],
                  index, key_gain, packed_prompt_length)
    ]
    *rows, carried, side, kv = front(
        packed_prompt_length, key_gain, index, down, up,
        tokens, key_weight, value_weight)
    single, other = [
        lax.ppermute(
            carried, ("z", "tp"),
            [(a * T + w, (a + w + d) % Z * T + a) for a in range(Z) for w in range(T)])
        for d in (0, 4)
    ]
    double = jnp.concatenate([single, other], axis=0)
    weights = [double] + [
        lax.ppermute(
            double if d in (1, Z - 1) else single, "z", [((i + d) % Z, i) for i in range(Z)])
        for d in NEAR[1:]
    ]
    rows = [rows[0]] + [
        lax.ppermute(
            rows[d], "x", [(i, (i + d) % X) for i in range(X)])
        for d in range(1, X)
    ]
    query = project_queries(tokens, query_weight)
    kv1, kv0 = [
        lax.ppermute(
            kv, ("x", "z"), [(i, i + d) for i in range(X * Z - d)])
        for d in (1, 2)
    ]
    delta = adapt(rows, weights)
    delta = lax.all_to_all(
        delta.reshape(X * T, CAP, UP), ("x", "tp"), 0, 0)
    return attend(
        delta.reshape(SLOTS, UP), query, side, kv0, kv1, kv, query_norm_gain.reshape(1, HEAD))


def solution(mesh):
    mesh = Mesh(mesh.devices.reshape(X, Z, T), ("x", "z", "tp"))
    seq = ("x", "z")
    in_specs = (
        P(seq, None), P(None, "tp"), P(None, "tp"), P(None, "tp"), P(), P(),
        P(seq, "tp", None), P(seq, None, "tp"), P(seq, None), P(),
    )
    return jax.shard_map(
        layer, mesh=mesh, in_specs=in_specs, out_specs=P(seq, "tp"), check_vma=False)
```

time: 87.5 us -> 84.8 us (0.969)
  Pallas kernels: 23.9 us -> 21.3 us
    pallas_call x4 -> x3, Pallas kernels: 19.4 us -> 16.8 us  [the longest x1 9.52 us: front(): pl.pallas_call(front_kernel, in_specs=[pl.BlockSpec(memory_space=pltpu.SM...]
  transfers between devices with their start and end apart: 12 -> 12, of which waited for: 7 -> 7; matrix products, arithmetic and copies ran while one was open for 0% -> 0% of each run, Pallas kernels for 12% -> 5%
where the time goes in v4:
time: 84.8 us; the launch traced here: 84.5 us
  starting transfers between devices  36.6 us (43%)
  waiting for transfers between devices  26.4 us (31%)
  Pallas kernels  21.3 us (25%)
    ppermute x2, starting transfers between devices, layer(): lax.ppermute(carried, ('z', 'tp'), [(a * T + w, (a + w + d) % Z * T + a)...  12.9 us
    ppermute x2, waiting for transfers between devices, layer(): lax.ppermute(kv, ('x', 'z'), [(i, i + d) for i in range(X * Z - d)])  10.7 us
    ppermute x4, waiting for transfers between devices, layer(): lax.ppermute(double if d in (1, Z - 1) else single, 'z', [((i + d) % Z, i...  10.2 us
    ppermute x2, starting transfers between devices, layer(): lax.ppermute(kv, ('x', 'z'), [(i, i + d) for i in range(X * Z - d)])  9.77 us
    pallas_call x1, Pallas kernels, front(): pl.pallas_call(front_kernel, in_specs=[pl.BlockSpec(memory_space=pltpu.SM...  9.52 us
    all_to_all x1, starting transfers between devices, layer(): delta = lax.all_to_all(delta.reshape(X * T, CAP, UP), ('x', 'tp'), 0, 0)  6.71 us
    pallas_call x1, Pallas kernels, attend(): pl.pallas_call(attend_kernel, in_specs=[near] * 7, out_specs=near, out_sh...  5.26 us
    pallas_call x1, Pallas kernels, project_queries(): pl.pallas_call(queries_kernel, in_specs=[far] * 2, out_specs=near, out_sh...  4.49 us
  transfers between devices with their start and end apart: 12, of which 7 were waited for; matrix products, arithmetic and copies ran while one was open for 0% of the time, Pallas kernels for 5%

profile of v4, /device:TPU:34, one launch (start us, length us, event | category | flops | bytes accessed | tf_op | source)
XLA Modules:
  0.0 84.5 jit_solution(9826271190018219023)
XLA Ops:
  0.0 9.5 %front.1 = (bf16[32,5376]{1,0:T(8,128)(2,1)S(1)}, bf16[32,5376]{1,0:T(8,128)(2,1)S(1)}, bf16[32,5376]{1,0:T(8,128)(2,1)S(1)}, bf16[32,5376]{1,0:T(8,128)(2,1)S(1...) custom-call(s32[16]{0:T(128)} %lens_ref.1, f32[1,128]{1,0:T(1,128)} %bitcast.14, ...), custom_call_target="tpu_custom_call" | custom-call | flops 2113929216 | bytes 10000000 | tf_op jit(solution)/shard_map/front/pallas_call | solution.py:125
  9.5 1.9 %collective-permute-start.3 = (bf16[64,1024]{1,0:T(8,128)(2,1)S(1)}, bf16[64,1024]{1,0:T(8,128)(2,1)S(1)}, u32[]{:S(2)}, u32[]{:S(2)}) collective-permute-start(bf16[64,1024]{1,0:T(8,128)(2,1)S(1)} %get-tuple-element.16), channel_id=1, source_target_pairs={{0,0},{1,8},{2,16},{3,24},{4,32},{5,40},{6,48},{7,56},{8,9},{9,17}... | collective-permute-start | bytes 393224 | tf_op jit(solution)/shard_map/ppermute | solution.py:303
  11.5 11.0 %collective-permute-start.4 = (bf16[64,1024]{1,0:T(8,128)(2,1)S(1)}, bf16[64,1024]{1,0:T(8,128)(2,1)S(1)}, u32[]{:S(2)}, u32[]{:S(2)}) collective-permute-start(bf16[64,1024]{1,0:T(8,128)(2,1)S(1)} %get-tuple-element.16), channel_id=1, source_target_pairs={{0,32},{1,40},{2,48},{3,56},{4,0},{5,8},{6,16},{7,24},{8,41},{9,49... | collective-permute-start | bytes 393224 | tf_op jit(solution)/shard_map/ppermute | solution.py:303
  22.5 1.6 %collective-permute-start = (bf16[32,5376]{1,0:T(8,128)(2,1)S(1)}, bf16[32,5376]{1,0:T(8,128)(2,1)S(1)}, u32[]{:S(2)}, u32[]{:S(2)}) collective-permute-start(bf16[32,5376]{1,0:T(8,128)(2,1)S(1)} %get-tuple-element.13), channel_id=1, source_target_pairs={{0,64},{64,128},{128,192},{192,0},{1,65},{65,129},{129,193},{193,1... | collective-permute-start | bytes 1032200 | tf_op jit(solution)/shard_map/ppermute | solution.py:315
  24.0 1.1 %collective-permute-start.1 = (bf16[32,5376]{1,0:T(8,128)(2,1)S(1)}, bf16[32,5376]{1,0:T(8,128)(2,1)S(1)}, u32[]{:S(2)}, u32[]{:S(2)}) collective-permute-start(bf16[32,5376]{1,0:T(8,128)(2,1)S(1)} %get-tuple-element.14), channel_id=1, source_target_pairs={{0,128},{64,192},{128,0},{192,64},{1,129},{65,193},{129,1},{193,65... | collective-permute-start | bytes 1032200 | tf_op jit(solution)/shard_map/ppermute | solution.py:315
  25.1 0.0 collective-permute-done.3
  25.1 1.2 %collective-permute-start.7 = (bf16[64,1024]{1,0:T(8,128)(2,1)S(1)}, bf16[64,1024]{1,0:T(8,128)(2,1)S(1)}, u32[]{:S(2)}, u32[]{:S(2)}) collective-permute-start(bf16[64,1024]{1,0:T(8,128)(2,1)S(1)} %collective-permute-done.3), channel_id=1, source_target_pairs={{16,0},{24,8},{32,16},{40,24},{48,32},{56,40},{0,48},{8,56},{17,1}... | collective-permute-start | bytes 393224 | tf_op jit(solution)/shard_map/ppermute | solution.py:310
  26.3 1.7 %collective-permute-start.8 = (bf16[64,1024]{1,0:T(8,128)(2,1)S(1)}, bf16[64,1024]{1,0:T(8,128)(2,1)S(1)}, u32[]{:S(2)}, u32[]{:S(2)}) collective-permute-start(bf16[64,1024]{1,0:T(8,128)(2,1)S(1)} %collective-permute-done.3), channel_id=1, source_target_pairs={{48,0},{56,8},{0,16},{8,24},{16,32},{24,40},{32,48},{40,56},{49,1}... | collective-permute-start | bytes 393224 | tf_op jit(solution)/shard_map/ppermute | solution.py:310
  28.1 1.6 %collective-permute-done.4 = bf16[64,1024]{1,0:T(8,128)(2,1)S(1)} collective-permute-done((bf16[64,1024]{1,0:T(8,128)(2,1)S(1)}, bf16[64,1024]{1,0:T(8,128)(2,1)S(1)}, u32[]{:S(2)}, u32[]{:S(2)}) %collective-permute-start.4) | collective-permute-done | bytes 131104 | tf_op jit(solution)/shard_map/ppermute | solution.py:303
  29.7 0.7 collective-permute-start.2
  30.3 6.4 %collective-permute-done.7.refs_7_ = bf16[64,1024]{1,0:T(8,128)(2,1)S(1)} collective-permute-done((bf16[64,1024]{1,0:T(8,128)(2,1)S(1)}, bf16[64,1024]{1,0:T(8,128)(2,1)S(1)}, u32[]{:S(2)}, u32[]{:S(2)}) %collective-permute-start.7) | collective-permute-done | bytes 131104 | tf_op jit(solution)/shard_map/ppermute | solution.py:310
  36.7 0.0 collective-permute-start.5
  36.7 1.1 %collective-permute-done.8.refs_8_ = bf16[64,1024]{1,0:T(8,128)(2,1)S(1)} collective-permute-done((bf16[64,1024]{1,0:T(8,128)(2,1)S(1)}, bf16[64,1024]{1,0:T(8,128)(2,1)S(1)}, u32[]{:S(2)}, u32[]{:S(2)}) %collective-permute-start.8) | collective-permute-done | bytes 131104 | tf_op jit(solution)/shard_map/ppermute | solution.py:310
  37.8 0.9 %collective-permute-start.6 = (bf16[128,1024]{1,0:T(8,128)(2,1)S(1)}, bf16[128,1024]{1,0:T(8,128)(2,1)S(1)}, u32[]{:S(2)}, u32[]{:S(2)}) collective-permute-start(bf16[128,1024]{1,0:T(8,128)(2,1)S(1)} %constant_dynamic-update-slice_fusion.refs_4_), channel_id=1, source_target_pairs={{56,0},{0,8},{8,16},{16,24},{24,32},{32,40},{40,48},{48,56},{57,1}... | collective-permute-start | bytes 786440 | tf_op jit(solution)/shard_map/ppermute | solution.py:310
  38.8 0.0 collective-permute-done.refs_1_
  38.8 0.0 collective-permute-done.1.refs_2_
  38.8 3.9 %collective-permute-done.2.refs_3_ = bf16[32,5376]{1,0:T(8,128)(2,1)S(1)} collective-permute-done((bf16[32,5376]{1,0:T(8,128)(2,1)S(1)}, bf16[32,5376]{1,0:T(8,128)(2,1)S(1)}, u32[]{:S(2)}, u32[]{:S(2)}) %collective-permute-start.2) | collective-permute-done | bytes 344096 | tf_op jit(solution)/shard_map/ppermute | solution.py:315
  42.6 2.2 %collective-permute-done.5.refs_5_ = bf16[128,1024]{1,0:T(8,128)(2,1)S(1)} collective-permute-done((bf16[128,1024]{1,0:T(8,128)(2,1)S(1)}, bf16[128,1024]{1,0:T(8,128)(2,1)S(1)}, u32[]{:S(2)}, u32[]{:S(2)}) %collective-permute-start.5) | collective-permute-done | bytes 262176 | tf_op jit(solution)/shard_map/ppermute | solution.py:310
  44.8 0.6 collective-permute-done.6.refs_6_
  45.4 2.0 %adapt.1 = bf16[4,8,32,256]{3,2,1,0:T(8,128)(2,1)} custom-call(bf16[32,5376]{1,0:T(8,128)(2,1)S(1)} %get-tuple-element.12.refs_0_, bf16[32,5376]{1,0:T(8,128)(2,1)S(1)} %collective-permute-done.refs_1_, bf16[32,5376]{1,0:T(8,128)(2,1)S(1)} %collective-permute-done.1.refs_2_, bf16[32,5376]{1,0:T(8,128)(2,1)S(1)} %collective-permute-done.2.refs_3_, ...), custom_call_target="tpu_custom_call" | custom-call | flops 121634816 | bytes 3000000 | tf_op jit(solution)/shard_map/adapt/pallas_call | solution.py:216
  47.4 6.7 %all-to-all-start = ((bf16[32,32,256]{2,1,0:T(8,128)(2,1)}), bf16[32,32,256]{2,1,0:T(8,128)(2,1)S(1)}, u32[]{:S(2)}, u32[]{:S(2)}) async-start(bf16[32,32,256]{2,1,0:T(8,128)(2,1)} %bitcast.5), calls=%async_computation | async-start | bytes 1048576 | tf_op jit(solution)/shard_map/all_to_all | solution.py:326
  54.2 0.0 copy-start
  54.2 2.2 %collective-permute-start.10 = (bf16[512,256]{1,0:T(8,128)(2,1)S(1)}, bf16[512,256]{1,0:T(8,128)(2,1)S(1)}, u32[]{:S(2)}, u32[]{:S(2)}) collective-permute-start(bf16[512,256]{1,0:T(8,128)(2,1)S(1)} %get-tuple-element.18.kv2), channel_id=1, source_target_pairs={{0,8},{8,16},{16,24},{24,32},{32,40},{40,48},{48,56},{56,64},{64,7... | collective-permute-start | bytes 786440 | tf_op jit(solution)/shard_map/ppermute | solution.py:321
  56.4 7.6 %collective-permute-start.9 = (bf16[512,256]{1,0:T(8,128)(2,1)S(1)}, bf16[512,256]{1,0:T(8,128)(2,1)S(1)}, u32[]{:S(2)}, u32[]{:S(2)}) collective-permute-start(bf16[512,256]{1,0:T(8,128)(2,1)S(1)} %get-tuple-element.18.kv2), channel_id=1, source_target_pairs={{0,16},{8,24},{16,32},{24,40},{32,48},{40,56},{48,64},{56,72},{64,... | collective-permute-start | bytes 786440 | tf_op jit(solution)/shard_map/ppermute | solution.py:321
  64.0 4.5 %project_queries.1.q_ref = f32[512,256]{1,0:T(8,128)S(1)} custom-call(bf16[512,5376]{1,0:T(8,128)(2,1)} %x_ref.1, bf16[5376,256]{1,0:T(8,128)(2,1)} %wq_ref.1), custom_call_target="tpu_custom_call" | custom-call | flops 1409286144 | bytes 8800000 | tf_op jit(solution)/shard_map/project_queries/pallas_call | solution.py:171
  68.5 0.0 collective-permute-done.10.kv1
  68.5 10.7 %collective-permute-done.9.kv0 = bf16[512,256]{1,0:T(8,128)(2,1)S(1)} collective-permute-done((bf16[512,256]{1,0:T(8,128)(2,1)S(1)}, bf16[512,256]{1,0:T(8,128)(2,1)S(1)}, u32[]{:S(2)}, u32[]{:S(2)}) %collective-permute-start.9) | collective-permute-done | bytes 262176 | tf_op jit(solution)/shard_map/ppermute | solution.py:321
  79.2 0.0 all-to-all-done
  79.2 0.0 copy-done
  79.2 5.3 %attend.1 = bf16[512,256]{1,0:T(8,128)(2,1)} custom-call(bf16[1024,256]{1,0:T(8,128)(2,1)S(1)} %bitcast.9, f32[512,256]{1,0:T(8,128)S(1)} %project_queries.1.q_ref, f32[512,384]{1,0:T(8,128)S(1)} %get-tuple-element.17.side_ref, bf16[512,256]{1,0:T(8,128)(2,1)S(1)} %collective-permute-done.9.kv0, bf16[512,256]{1,0:T(8,128)(2,1)S(1)} %collective-permute-done.10.kv1, ...), custom_call_target="tpu_custom_call" | custom-call | flops 671088640 | bytes 4000000 | tf_op jit(solution)/shard_map/attend/pallas_call | solution.py:270
  (2 shorter events, 0.0 us)
Async XLA Ops:
  9.5 15.6 %collective-permute-start.3 = (bf16[64,1024]{1,0:T(8,128)(2,1)S(1)}, bf16[64,1024]{1,0:T(8,128)(2,1)S(1)}, u32[]{:S(2)}, u32[]{:S(2)}) collective-permute-start(bf16[64,1024]{1,0:T(8,128)(2,1)S(1)} %get-tuple-element.16), channel_id=1, source_target_pairs={{0,0},{1,8},{2,16},{3,24},{4,32},{5,40},{6,48},{7,56},{8,9},{9,17}... | collective-permute-start | bytes 393224 | tf_op jit(solution)/shard_map/ppermute | solution.py:303
  11.5 18.2 %collective-permute-start.4 = (bf16[64,1024]{1,0:T(8,128)(2,1)S(1)}, bf16[64,1024]{1,0:T(8,128)(2,1)S(1)}, u32[]{:S(2)}, u32[]{:S(2)}) collective-permute-start(bf16[64,1024]{1,0:T(8,128)(2,1)S(1)} %get-tuple-element.16), channel_id=1, source_target_pairs={{0,32},{1,40},{2,48},{3,56},{4,0},{5,8},{6,16},{7,24},{8,41},{9,49... | collective-permute-start | bytes 393224 | tf_op jit(solution)/shard_map/ppermute | solution.py:303
  22.5 16.3 %collective-permute-start = (bf16[32,5376]{1,0:T(8,128)(2,1)S(1)}, bf16[32,5376]{1,0:T(8,128)(2,1)S(1)}, u32[]{:S(2)}, u32[]{:S(2)}) collective-permute-start(bf16[32,5376]{1,0:T(8,128)(2,1)S(1)} %get-tuple-element.13), channel_id=1, source_target_pairs={{0,64},{64,128},{128,192},{192,0},{1,65},{65,129},{129,193},{193,1... | collective-permute-start | bytes 1032200 | tf_op jit(solution)/shard_map/ppermute | solution.py:315
  24.0 14.7 %collective-permute-start.1 = (bf16[32,5376]{1,0:T(8,128)(2,1)S(1)}, bf16[32,5376]{1,0:T(8,128)(2,1)S(1)}, u32[]{:S(2)}, u32[]{:S(2)}) collective-permute-start(bf16[32,5376]{1,0:T(8,128)(2,1)S(1)} %get-tuple-element.14), channel_id=1, source_target_pairs={{0,128},{64,192},{128,0},{192,64},{1,129},{65,193},{129,1},{193,65... | collective-permute-start | bytes 1032200 | tf_op jit(solution)/shard_map/ppermute | solution.py:315
  25.1 11.6 %collective-permute-start.7 = (bf16[64,1024]{1,0:T(8,128)(2,1)S(1)}, bf16[64,1024]{1,0:T(8,128)(2,1)S(1)}, u32[]{:S(2)}, u32[]{:S(2)}) collective-permute-start(bf16[64,1024]{1,0:T(8,128)(2,1)S(1)} %collective-permute-done.3), channel_id=1, source_target_pairs={{16,0},{24,8},{32,16},{40,24},{48,32},{56,40},{0,48},{8,56},{17,1}... | collective-permute-start | bytes 393224 | tf_op jit(solution)/shard_map/ppermute | solution.py:310
  26.3 11.5 %collective-permute-start.8 = (bf16[64,1024]{1,0:T(8,128)(2,1)S(1)}, bf16[64,1024]{1,0:T(8,128)(2,1)S(1)}, u32[]{:S(2)}, u32[]{:S(2)}) collective-permute-start(bf16[64,1024]{1,0:T(8,128)(2,1)S(1)} %collective-permute-done.3), channel_id=1, source_target_pairs={{48,0},{56,8},{0,16},{8,24},{16,32},{24,40},{32,48},{40,56},{49,1}... | collective-permute-start | bytes 393224 | tf_op jit(solution)/shard_map/ppermute | solution.py:310
  29.7 13.0 %collective-permute-start.2 = (bf16[32,5376]{1,0:T(8,128)(2,1)S(1)}, bf16[32,5376]{1,0:T(8,128)(2,1)S(1)}, u32[]{:S(2)}, u32[]{:S(2)}) collective-permute-start(bf16[32,5376]{1,0:T(8,128)(2,1)S(1)} %get-tuple-element.15), channel_id=1, source_target_pairs={{0,192},{64,0},{128,64},{192,128},{1,193},{65,1},{129,65},{193,129... | collective-permute-start | bytes 1032200 | tf_op jit(solution)/shard_map/ppermute | solution.py:315
  36.7 8.1 %collective-permute-start.5 = (bf16[128,1024]{1,0:T(8,128)(2,1)S(1)}, bf16[128,1024]{1,0:T(8,128)(2,1)S(1)}, u32[]{:S(2)}, u32[]{:S(2)}) collective-permute-start(bf16[128,1024]{1,0:T(8,128)(2,1)S(1)} %constant_dynamic-update-slice_fusion.refs_4_), channel_id=1, source_target_pairs={{8,0},{16,8},{24,16},{32,24},{40,32},{48,40},{56,48},{0,56},{9,1},... | collective-permute-start | bytes 786440 | tf_op jit(solution)/shard_map/ppermute | solution.py:310
  37.8 7.6 %collective-permute-start.6 = (bf16[128,1024]{1,0:T(8,128)(2,1)S(1)}, bf16[128,1024]{1,0:T(8,128)(2,1)S(1)}, u32[]{:S(2)}, u32[]{:S(2)}) collective-permute-start(bf16[128,1024]{1,0:T(8,128)(2,1)S(1)} %constant_dynamic-update-slice_fusion.refs_4_), channel_id=1, source_target_pairs={{56,0},{0,8},{8,16},{16,24},{24,32},{32,40},{40,48},{48,56},{57,1}... | collective-permute-start | bytes 786440 | tf_op jit(solution)/shard_map/ppermute | solution.py:310
  47.4 31.7 %all-to-all-start = ((bf16[32,32,256]{2,1,0:T(8,128)(2,1)}), bf16[32,32,256]{2,1,0:T(8,128)(2,1)S(1)}, u32[]{:S(2)}, u32[]{:S(2)}) async-start(bf16[32,32,256]{2,1,0:T(8,128)(2,1)} %bitcast.5), calls=%async_computation | async-start | bytes 1048576 | tf_op jit(solution)/shard_map/all_to_all | solution.py:326
  54.2 25.0 %copy-start = (f32[128]{0:T(128)S(1)}, f32[128]{0:T(128)}, u32[]{:S(2)}) copy-start(f32[128]{0:T(128)} %param.14) | copy-start | bytes 1540
  54.2 14.3 %collective-permute-start.10 = (bf16[512,256]{1,0:T(8,128)(2,1)S(1)}, bf16[512,256]{1,0:T(8,128)(2,1)S(1)}, u32[]{:S(2)}, u32[]{:S(2)}) collective-permute-start(bf16[512,256]{1,0:T(8,128)(2,1)S(1)} %get-tuple-element.18.kv2), channel_id=1, source_target_pairs={{0,8},{8,16},{16,24},{24,32},{32,40},{40,48},{48,56},{56,64},{64,7... | collective-permute-start | bytes 786440 | tf_op jit(solution)/shard_map/ppermute | solution.py:321
  56.4 22.8 %collective-permute-start.9 = (bf16[512,256]{1,0:T(8,128)(2,1)S(1)}, bf16[512,256]{1,0:T(8,128)(2,1)S(1)}, u32[]{:S(2)}, u32[]{:S(2)}) collective-permute-start(bf16[512,256]{1,0:T(8,128)(2,1)S(1)} %get-tuple-element.18.kv2), channel_id=1, source_target_pairs={{0,16},{8,24},{16,32},{24,40},{32,48},{40,56},{48,64},{56,72},{64,... | collective-permute-start | bytes 786440 | tf_op jit(solution)/shard_map/ppermute | solution.py:321

commit v5 on v3

--- a/solution.py
+++ b/solution.py
@@ -1,3 +1,4 @@
+import functools
 import jax
 import jax.numpy as jnp
 from jax import lax
@@ -8,6 +9,7 @@
 WINDOW = 1024
 QUERY_SCALE = 0.07715167498104596
 LOG2E = 1.4426950408889634
+TILES = 4
 X, Z, T = 4, 8, 8
 ROWS, WIDTH, HEAD, RANK, CAP = 512, 5376, 128, 64, 32
 SLICE = WIDTH // T
@@ -26,16 +28,10 @@
     return lax.dot_general(a, b, (((ca,), (cb,)), ((), ())), preferred_element_type=jnp.float32)
 
 
-def pack_kernel(idx_hbm, down_hbm, up_hbm, x_ref, out0, out1, out2, out3, target_ref, carried_ref,
-                pick, wide, idx_ref, down_ref, held, sems, small_sems):
-    small = [
-        pltpu.make_async_copy(source, target, small_sems.at[n])
-        for n, (source, target) in enumerate((
-            (idx_hbm, idx_ref), (down_hbm, down_ref),
-            (up_hbm, carried_ref.at[:, pl.ds(PAD, UP)])))
-    ]
-    for copy in small:
-        copy.start()
+def pack_kernel(idx_hbm, x_ref, out0, out1, out2, out3, target_ref, pick, idx_ref, held, sems,
+                idx_sem):
+    small = pltpu.make_async_copy(idx_hbm, idx_ref, idx_sem.at[0])
+    small.start()
     copies = [
         pltpu.make_async_copy(x_ref.at[:, pl.ds(j * STEP, STEP)], held.at[j], sems.at[j])
         for j in range(STEPS)
@@ -43,7 +39,7 @@
     for copy in copies:
         copy.start()
     x, t = lax.axis_index("x"), lax.axis_index("tp")
-    small[0].wait()
+    small.wait()
     idx = idx_ref[...]
     named = lax.broadcasted_iota(jnp.int32, (X * T, ROWS), 0) == idx
     earlier = lax.broadcasted_iota(jnp.int32, (ROWS, ROWS), 0) < lax.broadcasted_iota(
@@ -60,11 +56,6 @@
         pick[d * CAP:(d + 1) * CAP, :] = (
             (slot + adapter * CAP == target).astype(jnp.float32).astype(jnp.bfloat16)
         )
-    small[1].wait()
-    wide[:, PAD - 128:] = jnp.zeros((RANK, 128), jnp.float32)
-    wide[:, :SLICE] = down_ref[...].astype(jnp.float32)
-    carried_ref[:, :PAD] = pltpu.roll(wide[...], lax.rem(t * SLICE, 128), 1).astype(jnp.bfloat16)
-    small[2].wait()
     for j in range(STEPS):
         copies[j].wait()
         packed = dot(pick[...], held[j]).astype(jnp.bfloat16)
@@ -72,31 +63,28 @@
             out[:, j * STEP:(j + 1) * STEP] = packed[d * CAP:(d + 1) * CAP, :]
 
 
-def pack(idx, down, up, tokens):
+def pack(idx, tokens):
     row = jax.ShapeDtypeStruct((CAP, WIDTH), jnp.bfloat16)
     return pl.pallas_call(
         pack_kernel,
-        in_specs=[pl.BlockSpec(memory_space=pltpu.HBM)] * 4,
-        out_specs=[pl.BlockSpec(memory_space=pltpu.VMEM)] * (X + 2),
+        in_specs=[pl.BlockSpec(memory_space=pltpu.HBM)] * 2,
+        out_specs=[pl.BlockSpec(memory_space=pltpu.VMEM)] * (X + 1),
         out_shape=[row] * X + [
             jax.ShapeDtypeStruct((1, ROWS), jnp.int32),
-            jax.ShapeDtypeStruct((RANK, PAD + UP), jnp.bfloat16),
         ],
         scratch_shapes=[
             pltpu.VMEM((X * CAP, ROWS), jnp.bfloat16),
-            pltpu.VMEM((RANK, PAD), jnp.float32),
             pltpu.VMEM((1, ROWS), jnp.int32),
-            pltpu.VMEM((RANK, SLICE), jnp.bfloat16),
             pltpu.VMEM((STEPS, ROWS, STEP), jnp.bfloat16),
             pltpu.SemaphoreType.DMA((STEPS,)),
-            pltpu.SemaphoreType.DMA((3,)),
+            pltpu.SemaphoreType.DMA((1,)),
         ],
         cost_estimate=pl.CostEstimate(
             flops=2 * X * CAP * ROWS * WIDTH, bytes_accessed=7_000_000, transcendentals=0
         ),
         compiler_params=pltpu.CompilerParams(vmem_limit_bytes=12 << 20),
         name="pack",
-    )(idx, down, up, tokens)
+    )(idx, tokens)
 
 
 def unit(field, gain):
@@ -131,21 +119,8 @@
         for j in range(STEPS)
     ], sems)
     begin = (lax.axis_index("x") * Z + lax.axis_index("z")) * ROWS
-    place = begin + lax.broadcasted_iota(jnp.int32, (ROWS, HEAD), 0)
-    start = jnp.zeros((ROWS, HEAD), jnp.int32)
-    at = jnp.int32(0)
-    for i in range(lens_ref.shape[0]):
-        start = jnp.where(place >= at, at, start)
-        at = at + lens_ref[i]
-    lower = jnp.maximum(start, place - (WINDOW - 1)) - (begin - WINDOW)
     wide = jnp.broadcast_to(target_ref[...].astype(jnp.float32), (HEAD, ROWS))
-    lane = lax.broadcasted_iota(jnp.int32, (ROWS, HEAD), 1)
-    side_ref[:, AUX:] = jnp.where(lane < HEAD // 2, lower.astype(jnp.float32), jnp.transpose(wide))
-    pair = jnp.bitwise_and(lane, HEAD // 2 - 1).astype(jnp.float32)
-    angle = place.astype(jnp.float32) * jnp.exp(-(2.0 * pair / HEAD) * jnp.log(jnp.float32(10000.0)))
-    sine = jnp.sin(angle)
-    side_ref[:, COS:SIN] = jnp.cos(angle)
-    side_ref[:, SIN:AUX] = jnp.where(lane < HEAD // 2, -sine, sine)
+    side_ref[:, AUX:] = jnp.transpose(wide)
     for j in range(STEPS):
         for copy in copies[j]:
             copy.wait()
@@ -154,6 +129,24 @@
             acc[...] = kv
         else:
             acc[...] += kv
+        first, past = ROWS // 8 * j // STEPS * 8, ROWS // 8 * (j + 1) // STEPS * 8
+        shape = (past - first, HEAD)
+        place = begin + first + lax.broadcasted_iota(jnp.int32, shape, 0)
+        start = jnp.zeros(shape, jnp.int32)
+        at = jnp.int32(0)
+        for i in range(lens_ref.shape[0]):
+            start = jnp.where(place >= at, at, start)
+            at = at + lens_ref[i]
+        lower = jnp.maximum(start, place - (WINDOW - 1)) - (begin - WINDOW)
+        lane = lax.broadcasted_iota(jnp.int32, shape, 1)
+        side_ref[first:past, AUX:] = jnp.where(
+            lane < HEAD // 2, lower.astype(jnp.float32), side_ref[first:past, AUX:])
+        pair = jnp.bitwise_and(lane, HEAD // 2 - 1).astype(jnp.float32)
+        angle = place.astype(jnp.float32) * jnp.exp(
+            -(2.0 * pair / HEAD) * jnp.log(jnp.float32(10000.0)))
+        sine = jnp.sin(angle)
+        side_ref[first:past, COS:SIN] = jnp.cos(angle)
+        side_ref[first:past, SIN:AUX] = jnp.where(lane < HEAD // 2, -sine, sine)
     key = turn(unit(acc[:, :HEAD], gain_ref[...]), side_ref[:, COS:SIN], side_ref[:, SIN:AUX])
     kv_ref[:, :HEAD] = key.astype(jnp.bfloat16)
     kv_ref[:, HEAD:] = acc[:, HEAD:].astype(jnp.bfloat16)
@@ -221,21 +214,12 @@
 
 def adapt_kernel(*refs):
     rows, weights, out = refs[:X], refs[X:X + PARTS], refs[X + PARTS]
-    packed, held, sems = refs[X + PARTS + 1:]
+    held = refs[X + PARTS + 1]
     x, z, t = lax.axis_index("x"), lax.axis_index("z"), lax.axis_index("tp")
-    copies = [
-        pltpu.make_async_copy(
-            weights[d].at[pl.ds(n * RANK, RANK), :],
-            held.at[lax.rem(z - t + T + NEAR[d] + 4 * n, T)], sems.at[X + sum(SPLIT[:d]) + n])
-        for d in range(PARTS) for n in range(SPLIT[d])
-    ] + [
-        pltpu.make_async_copy(rows[d], packed.at[pl.ds(d * CAP, CAP), :], sems.at[d])
-        for d in range(X)
-    ]
-    for copy in copies:
-        copy.start()
-    for copy in copies:
-        copy.wait()
+    for d in range(PARTS):
+        for n in range(SPLIT[d]):
+            held[lax.rem(z - t + T + NEAR[d] + 4 * n, T)] = weights[d][n * RANK:(n + 1) * RANK, :]
+    packed = jnp.concatenate([r[...] for r in rows], axis=0)
     chunks = [(w, n * 256) for w in range(T) for n in range(PAD // 256)]
     groups = len(chunks) // 4
     left, right = [], []
@@ -257,13 +241,11 @@
 def adapt(rows, weights):
     return pl.pallas_call(
         adapt_kernel,
-        in_specs=[pl.BlockSpec(memory_space=pl.ANY)] * (X + PARTS),
+        in_specs=[pl.BlockSpec(memory_space=pltpu.VMEM)] * (X + PARTS),
         out_specs=pl.BlockSpec(memory_space=pltpu.VMEM),
         out_shape=jax.ShapeDtypeStruct((X, T, CAP, UP), jnp.bfloat16),
         scratch_shapes=[
-            pltpu.VMEM((X * CAP, WIDTH), jnp.bfloat16),
             pltpu.VMEM((T, RANK, PAD + UP), jnp.bfloat16),
-            pltpu.SemaphoreType.DMA((X + T,)),
         ],
         compiler_params=pltpu.CompilerParams(vmem_limit_bytes=12 << 20),
         cost_estimate=pl.CostEstimate(
@@ -273,35 +255,17 @@
     )(*rows, *weights)
 
 
-def attend_kernel(delta_hbm, q_hbm, side_hbm, kv0_hbm, kv1_hbm, kv2_hbm, gain_ref, out_ref,
-                  delta_ref, q_ref, side_ref, kv_ref, sems):
-    half = ROWS // 2
-    pairs = [
-        (side_hbm.at[:, pl.ds(AUX, HEAD)], side_ref.at[:, pl.ds(AUX, HEAD)]),
-        (delta_hbm, delta_ref),
-        (q_hbm, q_ref),
-        (side_hbm.at[:, pl.ds(0, AUX)], side_ref.at[:, pl.ds(0, AUX)]),
-    ] + [
-        (source.at[:, pl.ds(n * HEAD, HEAD)], kv_ref.at[pl.ds(b * ROWS, ROWS), pl.ds(n * HEAD, HEAD)])
-        for b, source in enumerate((kv0_hbm, kv1_hbm, kv2_hbm)) for n in range(2)
-    ]
-    copies = [
-        pltpu.make_async_copy(source, target, sems.at[n])
-        for n, (source, target) in enumerate(pairs)
-    ]
-    for copy in copies:
-        copy.start()
+def attend_kernel(delta_ref, q_ref, side_ref, kv0, kv1, kv2, gain_ref, out_ref, kv_ref):
+    half = ROWS // TILES
+    for b, source in enumerate((kv0, kv1, kv2)):
+        kv_ref[b * ROWS:(b + 1) * ROWS, :2 * HEAD] = source[...]
     kv_ref[:, 2 * HEAD:] = jnp.ones((3 * ROWS, HEAD), jnp.bfloat16)
     slot = lax.broadcasted_iota(jnp.int32, (ROWS, HEAD), 1)
-    copies[0].wait()
     column = jnp.broadcast_to(side_ref[:, SIDE - 1:].astype(jnp.int32), (ROWS, HEAD))
     chosen = jnp.concatenate(
         [(column == slot + c * HEAD).astype(jnp.float32).astype(jnp.bfloat16)
          for c in range(SLOTS // HEAD)], axis=1)
-    copies[1].wait()
     delta = dot(chosen, delta_ref[...])
-    copies[2].wait()
-    copies[3].wait()
     query = q_ref[...] + delta
     gain = gain_ref[...] * (QUERY_SCALE * LOG2E)
     turned = [
@@ -309,9 +273,7 @@
              side_ref[:, SIN:AUX]).astype(jnp.bfloat16)
         for h in range(2)
     ]
-    for copy in copies[4:]:
-        copy.wait()
-    for tile in range(2):
+    for tile in range(TILES):
         here = slice(tile * half, (tile + 1) * half)
         first, past = tile * half, tile * half + WINDOW + half
         q = jnp.concatenate([turned[0][here], turned[1][here]], axis=0)
@@ -330,18 +292,14 @@
 
 
 def attend(*args):
-    near, far = pl.BlockSpec(memory_space=pltpu.VMEM), pl.BlockSpec(memory_space=pl.ANY)
+    near = pl.BlockSpec(memory_space=pltpu.VMEM)
     return pl.pallas_call(
         attend_kernel,
-        in_specs=[far] * 6 + [near],
+        in_specs=[near] * 7,
         out_specs=near,
         out_shape=jax.ShapeDtypeStruct((ROWS, 2 * HEAD), jnp.bfloat16),
         scratch_shapes=[
-            pltpu.VMEM((SLOTS, UP), jnp.bfloat16),
-            pltpu.VMEM((ROWS, 2 * HEAD), jnp.float32),
-            pltpu.VMEM((ROWS, SIDE), jnp.float32),
             pltpu.VMEM((3 * ROWS, 3 * HEAD), jnp.bfloat16),
-            pltpu.SemaphoreType.DMA((10,)),
         ],
         compiler_params=pltpu.CompilerParams(vmem_limit_bytes=24 << 20),
         cost_estimate=pl.CostEstimate(
@@ -356,13 +314,20 @@
     adapter_down_weight, adapter_up_weight, token_adapter_index, packed_prompt_length,
 ):
     down = jnp.swapaxes(adapter_down_weight[0], 0, 1)
-    index = token_adapter_index.reshape(1, ROWS)
-    tokens, query_weight, key_weight, value_weight, down, up, index = [
+    index, key_gain = token_adapter_index.reshape(1, ROWS), key_norm_gain.reshape(1, HEAD)
+    (tokens, query_weight, key_weight, value_weight, index, key_gain, packed_prompt_length) = [
         pltpu.with_memory_space_constraint(v, pltpu.HBM)
-        for v in (tokens, query_weight, key_weight, value_weight, down, adapter_up_weight[0], index)
-    ]
-    *rows, target, carried = pack(
-        index, down, up, tokens)
+        for v in (tokens, query_weight, key_weight, value_weight, index, key_gain,
+                  packed_prompt_length)
+    ]
+    shift = lax.rem(lax.axis_index("tp") * SLICE, 128)
+    carried = functools.reduce(
+        lambda other, at: jnp.where(
+            shift == at, jnp.pad(down, ((0, 0), (at, PAD + UP - SLICE - at))), other),
+        (32, 64, 96), jnp.pad(down, ((0, 0), (0, PAD + UP - SLICE))))
+    carried = jnp.where(
+        jnp.arange(PAD + UP)[None, :] < PAD, carried,
+        jnp.pad(adapter_up_weight[0], ((0, 0), (PAD, 0))))
     single, other = [
         lax.ppermute(
             carried, ("z", "tp"),
@@ -375,6 +340,7 @@
             double if d in (1, Z - 1) else single, "z", [((i + d) % Z, i) for i in range(Z)])
         for d in NEAR[1:]
     ]
+    *rows, target = pack(index, tokens)
     rows = [rows[0]] + [
         lax.ppermute(
             rows[d], "x", [(i, (i + d) % X) for i in range(X)])
@@ -382,7 +348,7 @@
     ]
     side, kv = project_keys(
         packed_prompt_length, tokens, key_weight, value_weight,
-        key_norm_gain.reshape(1, HEAD), target)
+        key_gain, target)
     query = project_queries(tokens, query_weight)
     kv1, kv0 = [
         lax.ppermute(

time: 87.5 us -> 82.5 us (0.943)
  waiting for transfers between devices: 26.4 us -> 19.8 us
  starting transfers between devices: 36.6 us -> 39.9 us
  Pallas kernels: 23.9 us -> 21.1 us
  other arithmetic: 0 us -> 1.29 us
    ppermute x4, waiting for transfers between devices: 10.3 us -> 3.08 us  [layer(): lax.ppermute(double if d in (1, Z - 1) else single, 'z', [((i + d) % Z, i...]
    ppermute x3, waiting for transfers between devices: 3.88 us -> 6.83 us  [layer(): lax.ppermute(rows[d], 'x', [(i, (i + d) % X) for i in range(X)])]
    pallas_call x2, Pallas kernels: 9.14 us -> 6.32 us  [the longest x1 4.28 us: attend(): pl.pallas_call(attend_kernel, in_specs=[near] * 7, out_specs=near, out_sh...]
    ppermute x4, starting transfers between devices: 3.86 us -> 6.17 us  [layer(): lax.ppermute(double if d in (1, Z - 1) else single, 'z', [((i + d) % Z, i...]
    ppermute x2, waiting for transfers between devices: 1.58 us -> 0.01 us  [layer(): lax.ppermute(carried, ('z', 'tp'), [(a * T + w, (a + w + d) % Z * T + a)...]
    ppermute x3, starting transfers between devices: 3.34 us -> 4.91 us  [layer(): lax.ppermute(rows[d], 'x', [(i, (i + d) % X) for i in range(X)])]
    select_n x0 -> x1, other arithmetic: none -> 1.28 us  [layer(): jnp.where(jnp.arange(PAD + UP)[None, :] < PAD, carried, jnp.pad(adapter_u...]
    all_to_all x1, starting transfers between devices: 6.71 us -> 5.75 us  [layer(): delta = lax.all_to_all(delta.reshape(X * T, CAP, UP), ('x', 'tp'), 0, 0)]
  transfers between devices with their start and end apart: 12 -> 12, of which waited for: 7 -> 6; matrix products, arithmetic and copies ran while one was open for 0% -> 0% of each run, Pallas kernels for 12% -> 18%
where the time goes in v5:
time: 82.5 us; the launch traced here: 82.2 us
  starting transfers between devices  39.9 us (48%)
  Pallas kernels  21.1 us (26%)
  waiting for transfers between devices  19.8 us (24%)
  other arithmetic  1.29 us (2%)
    ppermute x2, starting transfers between devices, layer(): lax.ppermute(carried, ('z', 'tp'), [(a * T + w, (a + w + d) % Z * T + a)...  12.9 us
    ppermute x2, starting transfers between devices, layer(): lax.ppermute(kv, ('x', 'z'), [(i, i + d) for i in range(X * Z - d)])  10.2 us
    ppermute x2, waiting for transfers between devices, layer(): lax.ppermute(kv, ('x', 'z'), [(i, i + d) for i in range(X * Z - d)])  9.86 us
    ppermute x3, waiting for transfers between devices, layer(): lax.ppermute(rows[d], 'x', [(i, (i + d) % X) for i in range(X)])  6.83 us
    ppermute x4, starting transfers between devices, layer(): lax.ppermute(double if d in (1, Z - 1) else single, 'z', [((i + d) % Z, i...  6.17 us
    all_to_all x1, starting transfers between devices, layer(): delta = lax.all_to_all(delta.reshape(X * T, CAP, UP), ('x', 'tp'), 0, 0)  5.75 us
    pallas_call x1, Pallas kernels, project_keys(): pl.pallas_call(keys_kernel, in_specs=[pl.BlockSpec(memory_space=pltpu.SME...  5.65 us
    ppermute x3, starting transfers between devices, layer(): lax.ppermute(rows[d], 'x', [(i, (i + d) % X) for i in range(X)])  4.91 us
  transfers between devices with their start and end apart: 12, of which 6 were waited for; matrix products, arithmetic and copies ran while one was open for 0% of the time, Pallas kernels for 18%

profile of v5, /device:TPU:34, one launch (start us, length us, event | category | flops | bytes accessed | tf_op | source)
XLA Modules:
  0.0 82.2 jit_solution(11302536880380256534)
XLA Ops:
  0.0 1.3 %pad_select_fusion = bf16[64,1024]{1,0:T(8,128)(2,1)S(1)} fusion(bf16[64,256]{1,0:T(8,128)(2,1)} %bitcast.12, bf16[64,672]{1,0:T(8,128)(2,1)} %bitcast.11, pred[]{:T(512)S(6)} %eq.11, pred[]{:T(512)S(6)} %eq.10, pred[]{:T(512)S(6)} %eq.9, pred[1024]{0:T(1024)(128)(4,1)S(1)} %iota_compare_fusion), kind=kLoop, calls=%fused_computation | loop fusion | flops 262144 | bytes 250883 | tf_op jit(solution)/shard_map/jit(_where)/select_n | solution.py:328
  1.3 1.9 %collective-permute-start.3 = (bf16[64,1024]{1,0:T(8,128)(2,1)S(1)}, bf16[64,1024]{1,0:T(8,128)(2,1)S(1)}, u32[]{:S(2)}, u32[]{:S(2)}) collective-permute-start(bf16[64,1024]{1,0:T(8,128)(2,1)S(1)} %pad_select_fusion), channel_id=1, source_target_pairs={{0,0},{1,8},{2,16},{3,24},{4,32},{5,40},{6,48},{7,56},{8,9},{9,17}... | collective-permute-start | bytes 393224 | tf_op jit(solution)/shard_map/ppermute | solution.py:332
  3.2 11.0 %collective-permute-start.4 = (bf16[64,1024]{1,0:T(8,128)(2,1)S(1)}, bf16[64,1024]{1,0:T(8,128)(2,1)S(1)}, u32[]{:S(2)}, u32[]{:S(2)}) collective-permute-start(bf16[64,1024]{1,0:T(8,128)(2,1)S(1)} %pad_select_fusion), channel_id=1, source_target_pairs={{0,32},{1,40},{2,48},{3,56},{4,0},{5,8},{6,16},{7,24},{8,41},{9,49... | collective-permute-start | bytes 393224 | tf_op jit(solution)/shard_map/ppermute | solution.py:332
  14.2 4.6 %pack.1 = (bf16[32,5376]{1,0:T(8,128)(2,1)S(1)}, bf16[32,5376]{1,0:T(8,128)(2,1)S(1)}, bf16[32,5376]{1,0:T(8,128)(2,1)S(1)}, bf16[32,5376]{1,0:T(8,128)(2,1)S(1)}, s32[1,512]{1,0:T(1,128)S(1)}) custom-call(s32[1,512]{1,0:T(1,128)} %bitcast.13, bf16[512,5376]{1,0:T(8,128)(2,1)} %x_ref.5), custom_call_target="tpu_custom_call" | custom-call | flops 704643072 | bytes 7000000 | tf_op jit(solution)/shard_map/pack/pallas_call | solution.py:68
  18.8 1.6 %collective-permute-start = (bf16[32,5376]{1,0:T(8,128)(2,1)S(1)}, bf16[32,5376]{1,0:T(8,128)(2,1)S(1)}, u32[]{:S(2)}, u32[]{:S(2)}) collective-permute-start(bf16[32,5376]{1,0:T(8,128)(2,1)S(1)} %get-tuple-element.13), channel_id=1, source_target_pairs={{0,64},{64,128},{128,192},{192,0},{1,65},{65,129},{129,193},{193,1... | collective-permute-start | bytes 1032200 | tf_op jit(solution)/shard_map/ppermute | solution.py:345
  20.4 1.1 %collective-permute-start.1 = (bf16[32,5376]{1,0:T(8,128)(2,1)S(1)}, bf16[32,5376]{1,0:T(8,128)(2,1)S(1)}, u32[]{:S(2)}, u32[]{:S(2)}) collective-permute-start(bf16[32,5376]{1,0:T(8,128)(2,1)S(1)} %get-tuple-element.14), channel_id=1, source_target_pairs={{0,128},{64,192},{128,0},{192,64},{1,129},{65,193},{129,1},{193,65... | collective-permute-start | bytes 1032200 | tf_op jit(solution)/shard_map/ppermute | solution.py:345
  21.5 0.0 collective-permute-done.3
  21.5 0.1 collective-permute-start.7
  21.7 2.8 %collective-permute-start.8 = (bf16[64,1024]{1,0:T(8,128)(2,1)S(1)}, bf16[64,1024]{1,0:T(8,128)(2,1)S(1)}, u32[]{:S(2)}, u32[]{:S(2)}) collective-permute-start(bf16[64,1024]{1,0:T(8,128)(2,1)S(1)} %collective-permute-done.3), channel_id=1, source_target_pairs={{48,0},{56,8},{0,16},{8,24},{16,32},{24,40},{32,48},{40,56},{49,1}... | collective-permute-start | bytes 393224 | tf_op jit(solution)/shard_map/ppermute | solution.py:339
  24.5 0.0 collective-permute-done.4
  24.5 2.2 %collective-permute-start.2 = (bf16[32,5376]{1,0:T(8,128)(2,1)S(1)}, bf16[32,5376]{1,0:T(8,128)(2,1)S(1)}, u32[]{:S(2)}, u32[]{:S(2)}) collective-permute-start(bf16[32,5376]{1,0:T(8,128)(2,1)S(1)} %get-tuple-element.15), channel_id=1, source_target_pairs={{0,192},{64,0},{128,64},{192,128},{1,193},{65,1},{129,65},{193,129... | collective-permute-start | bytes 1032200 | tf_op jit(solution)/shard_map/ppermute | solution.py:345
  26.7 1.3 %collective-permute-done.7.refs_7_ = bf16[64,1024]{1,0:T(8,128)(2,1)S(1)} collective-permute-done((bf16[64,1024]{1,0:T(8,128)(2,1)S(1)}, bf16[64,1024]{1,0:T(8,128)(2,1)S(1)}, u32[]{:S(2)}, u32[]{:S(2)}) %collective-permute-start.7) | collective-permute-done | bytes 131104 | tf_op jit(solution)/shard_map/ppermute | solution.py:339
  28.0 3.2 %collective-permute-start.5 = (bf16[128,1024]{1,0:T(8,128)(2,1)S(1)}, bf16[128,1024]{1,0:T(8,128)(2,1)S(1)}, u32[]{:S(2)}, u32[]{:S(2)}) collective-permute-start(bf16[128,1024]{1,0:T(8,128)(2,1)S(1)} %constant_dynamic-update-slice_fusion.refs_4_), channel_id=1, source_target_pairs={{8,0},{16,8},{24,16},{32,24},{40,32},{48,40},{56,48},{0,56},{9,1},... | collective-permute-start | bytes 786440 | tf_op jit(solution)/shard_map/ppermute | solution.py:339
  31.2 1.0 %collective-permute-done.8.refs_8_ = bf16[64,1024]{1,0:T(8,128)(2,1)S(1)} collective-permute-done((bf16[64,1024]{1,0:T(8,128)(2,1)S(1)}, bf16[64,1024]{1,0:T(8,128)(2,1)S(1)}, u32[]{:S(2)}, u32[]{:S(2)}) %collective-permute-start.8) | collective-permute-done | bytes 131104 | tf_op jit(solution)/shard_map/ppermute | solution.py:339
  32.1 0.0 collective-permute-start.6
  32.2 0.0 collective-permute-done.refs_1_
  32.2 0.7 collective-permute-done.1.refs_2_
  32.9 6.1 %collective-permute-done.2.refs_3_ = bf16[32,5376]{1,0:T(8,128)(2,1)S(1)} collective-permute-done((bf16[32,5376]{1,0:T(8,128)(2,1)S(1)}, bf16[32,5376]{1,0:T(8,128)(2,1)S(1)}, u32[]{:S(2)}, u32[]{:S(2)}) %collective-permute-start.2) | collective-permute-done | bytes 344096 | tf_op jit(solution)/shard_map/ppermute | solution.py:345
  39.0 0.0 collective-permute-done.5.refs_5_
  39.0 0.9 %collective-permute-done.6.refs_6_ = bf16[128,1024]{1,0:T(8,128)(2,1)S(1)} collective-permute-done((bf16[128,1024]{1,0:T(8,128)(2,1)S(1)}, bf16[128,1024]{1,0:T(8,128)(2,1)S(1)}, u32[]{:S(2)}, u32[]{:S(2)}) %collective-permute-start.6) | collective-permute-done | bytes 262176 | tf_op jit(solution)/shard_map/ppermute | solution.py:339
  39.9 2.0 %adapt.1 = bf16[4,8,32,256]{3,2,1,0:T(8,128)(2,1)} custom-call(bf16[32,5376]{1,0:T(8,128)(2,1)S(1)} %get-tuple-element.12.refs_0_, bf16[32,5376]{1,0:T(8,128)(2,1)S(1)} %collective-permute-done.refs_1_, bf16[32,5376]{1,0:T(8,128)(2,1)S(1)} %collective-permute-done.1.refs_2_, bf16[32,5376]{1,0:T(8,128)(2,1)S(1)} %collective-permute-done.2.refs_3_, ...), custom_call_target="tpu_custom_call" | custom-call | flops 121634816 | bytes 3000000 | tf_op jit(solution)/shard_map/adapt/pallas_call | solution.py:242
  41.9 5.8 %all-to-all-start = ((bf16[32,32,256]{2,1,0:T(8,128)(2,1)}), bf16[32,32,256]{2,1,0:T(8,128)(2,1)S(1)}, u32[]{:S(2)}, u32[]{:S(2)}) async-start(bf16[32,32,256]{2,1,0:T(8,128)(2,1)} %bitcast.5), calls=%async_computation | async-start | bytes 1048576 | tf_op jit(solution)/shard_map/all_to_all | solution.py:359
  47.7 5.6 %project_keys.1 = (f32[512,384]{1,0:T(8,128)S(1)}, bf16[512,256]{1,0:T(8,128)(2,1)S(1)}) custom-call(s32[16]{0:T(128)} %lens_ref.1, bf16[512,5376]{1,0:T(8,128)(2,1)} %x_ref.5, bf16[5376,128]{1,0:T(8,128)(2,1)} %wk_ref.1, bf16[5376,128]{1,0:T(8,128)(2,1)} %wv_ref.1, f32[1,128]{1,0:T(1,128)} %bitcast.14, s32[1,512]{1,0:T(1,128)S(1)} %get-tuple-element.16.target_ref), custom_call_target="tpu_custom_call" | custom-call | flops 1409286144 | bytes 9500000 | tf_op jit(solution)/shard_map/project_keys/pallas_call | solution.py:157
  53.3 0.0 copy-start
  53.3 3.1 %collective-permute-start.10 = (bf16[512,256]{1,0:T(8,128)(2,1)S(1)}, bf16[512,256]{1,0:T(8,128)(2,1)S(1)}, u32[]{:S(2)}, u32[]{:S(2)}) collective-permute-start(bf16[512,256]{1,0:T(8,128)(2,1)S(1)} %get-tuple-element.18.kv2), channel_id=1, source_target_pairs={{0,8},{8,16},{16,24},{24,32},{32,40},{40,48},{48,56},{56,64},{64,7... | collective-permute-start | bytes 786440 | tf_op jit(solution)/shard_map/ppermute | solution.py:354
  56.4 7.1 %collective-permute-start.9 = (bf16[512,256]{1,0:T(8,128)(2,1)S(1)}, bf16[512,256]{1,0:T(8,128)(2,1)S(1)}, u32[]{:S(2)}, u32[]{:S(2)}) collective-permute-start(bf16[512,256]{1,0:T(8,128)(2,1)S(1)} %get-tuple-element.18.kv2), channel_id=1, source_target_pairs={{0,16},{8,24},{16,32},{24,40},{32,48},{40,56},{48,64},{56,72},{64,... | collective-permute-start | bytes 786440 | tf_op jit(solution)/shard_map/ppermute | solution.py:354
  63.6 4.5 %project_queries.1.q_ref = f32[512,256]{1,0:T(8,128)S(1)} custom-call(bf16[512,5376]{1,0:T(8,128)(2,1)} %x_ref.5, bf16[5376,256]{1,0:T(8,128)(2,1)} %wq_ref.1), custom_call_target="tpu_custom_call" | custom-call | flops 1409286144 | bytes 8800000 | tf_op jit(solution)/shard_map/project_queries/pallas_call | solution.py:197
  68.1 0.0 collective-permute-done.10.kv1
  68.1 9.9 %collective-permute-done.9.kv0 = bf16[512,256]{1,0:T(8,128)(2,1)S(1)} collective-permute-done((bf16[512,256]{1,0:T(8,128)(2,1)S(1)}, bf16[512,256]{1,0:T(8,128)(2,1)S(1)}, u32[]{:S(2)}, u32[]{:S(2)}) %collective-permute-start.9) | collective-permute-done | bytes 262176 | tf_op jit(solution)/shard_map/ppermute | solution.py:354
  77.9 0.0 all-to-all-done
  77.9 0.0 copy-done
  77.9 4.3 %attend.1 = bf16[512,256]{1,0:T(8,128)(2,1)} custom-call(bf16[1024,256]{1,0:T(8,128)(2,1)S(1)} %bitcast.9, f32[512,256]{1,0:T(8,128)S(1)} %project_queries.1.q_ref, f32[512,384]{1,0:T(8,128)S(1)} %get-tuple-element.17.side_ref, bf16[512,256]{1,0:T(8,128)(2,1)S(1)} %collective-permute-done.9.kv0, bf16[512,256]{1,0:T(8,128)(2,1)S(1)} %collective-permute-done.10.kv1, ...), custom_call_target="tpu_custom_call" | custom-call | flops 671088640 | bytes 4000000 | tf_op jit(solution)/shard_map/attend/pallas_call | solution.py:296
  (3 shorter events, 0.0 us)
Async XLA Ops:
  1.3 20.2 %collective-permute-start.3 = (bf16[64,1024]{1,0:T(8,128)(2,1)S(1)}, bf16[64,1024]{1,0:T(8,128)(2,1)S(1)}, u32[]{:S(2)}, u32[]{:S(2)}) collective-permute-start(bf16[64,1024]{1,0:T(8,128)(2,1)S(1)} %pad_select_fusion), channel_id=1, source_target_pairs={{0,0},{1,8},{2,16},{3,24},{4,32},{5,40},{6,48},{7,56},{8,9},{9,17}... | collective-permute-start | bytes 393224 | tf_op jit(solution)/shard_map/ppermute | solution.py:332
  3.2 21.2 %collective-permute-start.4 = (bf16[64,1024]{1,0:T(8,128)(2,1)S(1)}, bf16[64,1024]{1,0:T(8,128)(2,1)S(1)}, u32[]{:S(2)}, u32[]{:S(2)}) collective-permute-start(bf16[64,1024]{1,0:T(8,128)(2,1)S(1)} %pad_select_fusion), channel_id=1, source_target_pairs={{0,32},{1,40},{2,48},{3,56},{4,0},{5,8},{6,16},{7,24},{8,41},{9,49... | collective-permute-start | bytes 393224 | tf_op jit(solution)/shard_map/ppermute | solution.py:332
  18.8 13.4 %collective-permute-start = (bf16[32,5376]{1,0:T(8,128)(2,1)S(1)}, bf16[32,5376]{1,0:T(8,128)(2,1)S(1)}, u32[]{:S(2)}, u32[]{:S(2)}) collective-permute-start(bf16[32,5376]{1,0:T(8,128)(2,1)S(1)} %get-tuple-element.13), channel_id=1, source_target_pairs={{0,64},{64,128},{128,192},{192,0},{1,65},{65,129},{129,193},{193,1... | collective-permute-start | bytes 1032200 | tf_op jit(solution)/shard_map/ppermute | solution.py:345
  20.4 12.5 %collective-permute-start.1 = (bf16[32,5376]{1,0:T(8,128)(2,1)S(1)}, bf16[32,5376]{1,0:T(8,128)(2,1)S(1)}, u32[]{:S(2)}, u32[]{:S(2)}) collective-permute-start(bf16[32,5376]{1,0:T(8,128)(2,1)S(1)} %get-tuple-element.14), channel_id=1, source_target_pairs={{0,128},{64,192},{128,0},{192,64},{1,129},{65,193},{129,1},{193,65... | collective-permute-start | bytes 1032200 | tf_op jit(solution)/shard_map/ppermute | solution.py:345
  21.5 6.5 %collective-permute-start.7 = (bf16[64,1024]{1,0:T(8,128)(2,1)S(1)}, bf16[64,1024]{1,0:T(8,128)(2,1)S(1)}, u32[]{:S(2)}, u32[]{:S(2)}) collective-permute-start(bf16[64,1024]{1,0:T(8,128)(2,1)S(1)} %collective-permute-done.3), channel_id=1, source_target_pairs={{16,0},{24,8},{32,16},{40,24},{48,32},{56,40},{0,48},{8,56},{17,1}... | collective-permute-start | bytes 393224 | tf_op jit(solution)/shard_map/ppermute | solution.py:339
  21.7 10.5 %collective-permute-start.8 = (bf16[64,1024]{1,0:T(8,128)(2,1)S(1)}, bf16[64,1024]{1,0:T(8,128)(2,1)S(1)}, u32[]{:S(2)}, u32[]{:S(2)}) collective-permute-start(bf16[64,1024]{1,0:T(8,128)(2,1)S(1)} %collective-permute-done.3), channel_id=1, source_target_pairs={{48,0},{56,8},{0,16},{8,24},{16,32},{24,40},{32,48},{40,56},{49,1}... | collective-permute-start | bytes 393224 | tf_op jit(solution)/shard_map/ppermute | solution.py:339
  24.5 14.6 %collective-permute-start.2 = (bf16[32,5376]{1,0:T(8,128)(2,1)S(1)}, bf16[32,5376]{1,0:T(8,128)(2,1)S(1)}, u32[]{:S(2)}, u32[]{:S(2)}) collective-permute-start(bf16[32,5376]{1,0:T(8,128)(2,1)S(1)} %get-tuple-element.15), channel_id=1, source_target_pairs={{0,192},{64,0},{128,64},{192,128},{1,193},{65,1},{129,65},{193,129... | collective-permute-start | bytes 1032200 | tf_op jit(solution)/shard_map/ppermute | solution.py:345
  28.0 11.0 %collective-permute-start.5 = (bf16[128,1024]{1,0:T(8,128)(2,1)S(1)}, bf16[128,1024]{1,0:T(8,128)(2,1)S(1)}, u32[]{:S(2)}, u32[]{:S(2)}) collective-permute-start(bf16[128,1024]{1,0:T(8,128)(2,1)S(1)} %constant_dynamic-update-slice_fusion.refs_4_), channel_id=1, source_target_pairs={{8,0},{16,8},{24,16},{32,24},{40,32},{48,40},{56,48},{0,56},{9,1},... | collective-permute-start | bytes 786440 | tf_op jit(solution)/shard_map/ppermute | solution.py:339
  32.1 7.7 %collective-permute-start.6 = (bf16[128,1024]{1,0:T(8,128)(2,1)S(1)}, bf16[128,1024]{1,0:T(8,128)(2,1)S(1)}, u32[]{:S(2)}, u32[]{:S(2)}) collective-permute-start(bf16[128,1024]{1,0:T(8,128)(2,1)S(1)} %constant_dynamic-update-slice_fusion.refs_4_), channel_id=1, source_target_pairs={{56,0},{0,8},{8,16},{16,24},{24,32},{32,40},{40,48},{48,56},{57,1}... | collective-permute-start | bytes 786440 | tf_op jit(solution)/shard_map/ppermute | solution.py:339
  41.9 36.0 %all-to-all-start = ((bf16[32,32,256]{2,1,0:T(8,128)(2,1)}), bf16[32,32,256]{2,1,0:T(8,128)(2,1)S(1)}, u32[]{:S(2)}, u32[]{:S(2)}) async-start(bf16[32,32,256]{2,1,0:T(8,128)(2,1)} %bitcast.5), calls=%async_computation | async-start | bytes 1048576 | tf_op jit(solution)/shard_map/all_to_all | solution.py:359
  53.3 24.6 %copy-start = (f32[128]{0:T(128)S(1)}, f32[128]{0:T(128)}, u32[]{:S(2)}) copy-start(f32[128]{0:T(128)} %param.14) | copy-start | bytes 1540
  53.3 14.7 %collective-permute-start.10 = (bf16[512,256]{1,0:T(8,128)(2,1)S(1)}, bf16[512,256]{1,0:T(8,128)(2,1)S(1)}, u32[]{:S(2)}, u32[]{:S(2)}) collective-permute-start(bf16[512,256]{1,0:T(8,128)(2,1)S(1)} %get-tuple-element.18.kv2), channel_id=1, source_target_pairs={{0,8},{8,16},{16,24},{24,32},{32,40},{40,48},{48,56},{56,64},{64,7... | collective-permute-start | bytes 786440 | tf_op jit(solution)/shard_map/ppermute | solution.py:354
  56.4 21.5 %collective-permute-start.9 = (bf16[512,256]{1,0:T(8,128)(2,1)S(1)}, bf16[512,256]{1,0:T(8,128)(2,1)S(1)}, u32[]{:S(2)}, u32[]{:S(2)}) collective-permute-start(bf16[512,256]{1,0:T(8,128)(2,1)S(1)} %get-tuple-element.18.kv2), channel_id=1, source_target_pairs={{0,16},{8,24},{16,32},{24,40},{32,48},{40,56},{48,64},{56,72},{64,... | collective-permute-start | bytes 786440 | tf_op jit(solution)/shard_map/ppermute | solution.py:354

commit v6 on v5

--- a/solution.py
+++ b/solution.py
@@ -28,10 +28,7 @@
     return lax.dot_general(a, b, (((ca,), (cb,)), ((), ())), preferred_element_type=jnp.float32)
 
 
-def pack_kernel(idx_hbm, x_ref, out0, out1, out2, out3, target_ref, pick, idx_ref, held, sems,
-                idx_sem):
-    small = pltpu.make_async_copy(idx_hbm, idx_ref, idx_sem.at[0])
-    small.start()
+def pack_kernel(idx_ref, x_ref, out0, out1, out2, out3, target_ref, held, pick, sems):
     copies = [
         pltpu.make_async_copy(x_ref.at[:, pl.ds(j * STEP, STEP)], held.at[j], sems.at[j])
         for j in range(STEPS)
@@ -39,7 +36,6 @@
     for copy in copies:
         copy.start()
     x, t = lax.axis_index("x"), lax.axis_index("tp")
-    small.wait()
     idx = idx_ref[...]
     named = lax.broadcasted_iota(jnp.int32, (X * T, ROWS), 0) == idx
     earlier = lax.broadcasted_iota(jnp.int32, (ROWS, ROWS), 0) < lax.broadcasted_iota(
@@ -67,17 +63,15 @@
     row = jax.ShapeDtypeStruct((CAP, WIDTH), jnp.bfloat16)
     return pl.pallas_call(
         pack_kernel,
-        in_specs=[pl.BlockSpec(memory_space=pltpu.HBM)] * 2,
-        out_specs=[pl.BlockSpec(memory_space=pltpu.VMEM)] * (X + 1),
+        in_specs=[pl.BlockSpec(memory_space=pltpu.VMEM), pl.BlockSpec(memory_space=pltpu.HBM)],
+        out_specs=[pl.BlockSpec(memory_space=pltpu.VMEM)] * (X + 2),
         out_shape=[row] * X + [
             jax.ShapeDtypeStruct((1, ROWS), jnp.int32),
+            jax.ShapeDtypeStruct((STEPS, ROWS, STEP), jnp.bfloat16),
         ],
         scratch_shapes=[
             pltpu.VMEM((X * CAP, ROWS), jnp.bfloat16),
-            pltpu.VMEM((1, ROWS), jnp.int32),
-            pltpu.VMEM((STEPS, ROWS, STEP), jnp.bfloat16),
             pltpu.SemaphoreType.DMA((STEPS,)),
-            pltpu.SemaphoreType.DMA((1,)),
         ],
         cost_estimate=pl.CostEstimate(
             flops=2 * X * CAP * ROWS * WIDTH, bytes_accessed=7_000_000, transcendentals=0
@@ -108,23 +102,30 @@
 
 
 def keys_kernel(
-    lens_ref, x_ref, wk_ref, wv_ref, gain_ref, target_ref, side_ref, kv_ref, x_held, kv_held, acc,
-    sems,
+    lens_ref, x_held, wk_ref, wv_ref, gain_ref, target_ref, side_ref, kv_ref, kv_held, acc, sems,
 ):
     part = [pl.ds(j * STEP, STEP) for j in range(STEPS)]
     copies = fetch([
-        ((x_ref.at[:, part[j]], x_held.at[j]),
-         (wk_ref.at[part[j], :], kv_held.at[j, :, pl.ds(0, HEAD)]),
-         (wv_ref.at[part[j], :], kv_held.at[j, :, pl.ds(HEAD, HEAD)]))
+        ((wk_ref.at[part[j], :], kv_held.at[0, j]),
+         (wv_ref.at[part[j], :], kv_held.at[1, j]))
         for j in range(STEPS)
     ], sems)
     begin = (lax.axis_index("x") * Z + lax.axis_index("z")) * ROWS
     wide = jnp.broadcast_to(target_ref[...].astype(jnp.float32), (HEAD, ROWS))
     side_ref[:, AUX:] = jnp.transpose(wide)
+    lane = lax.broadcasted_iota(jnp.int32, (8, HEAD), 1)
+    sign = jnp.where(lane[:1] < HEAD // 2, -1.0, 1.0)
+    pair = jnp.bitwise_and(lane, HEAD // 2 - 1).astype(jnp.float32)
+    freq = jnp.exp(-(2.0 * pair / HEAD) * jnp.log(jnp.float32(10000.0)))
+    row = lax.broadcasted_iota(jnp.int32, (8, HEAD), 0)
+    base = (begin + 64 * row).astype(jnp.float32) * freq
+    base_cos, base_sin = jnp.cos(base), jnp.sin(base)
+    step = lax.broadcasted_iota(jnp.int32, (64, HEAD), 0).astype(jnp.float32) * freq[:1]
+    step_cos, step_sin = jnp.cos(step), jnp.sin(step)
     for j in range(STEPS):
         for copy in copies[j]:
             copy.wait()
-        kv = dot(x_held[j], kv_held[j])
+        kv = dot(x_held[j], jnp.concatenate([kv_held[0, j], kv_held[1, j]], axis=1))
         if j == 0:
             acc[...] = kv
         else:
@@ -141,12 +142,11 @@
         lane = lax.broadcasted_iota(jnp.int32, shape, 1)
         side_ref[first:past, AUX:] = jnp.where(
             lane < HEAD // 2, lower.astype(jnp.float32), side_ref[first:past, AUX:])
-        pair = jnp.bitwise_and(lane, HEAD // 2 - 1).astype(jnp.float32)
-        angle = place.astype(jnp.float32) * jnp.exp(
-            -(2.0 * pair / HEAD) * jnp.log(jnp.float32(10000.0)))
-        sine = jnp.sin(angle)
-        side_ref[first:past, COS:SIN] = jnp.cos(angle)
-        side_ref[first:past, SIN:AUX] = jnp.where(lane < HEAD // 2, -sine, sine)
+        for block in (range(8) if j == STEPS - 1 else ()):
+            there = slice(block * 64, block * 64 + 64)
+            c, d = base_cos[block:block + 1, :], base_sin[block:block + 1, :]
+            side_ref[there, COS:SIN] = c * step_cos - d * step_sin
+            side_ref[there, SIN:AUX] = sign * (d * step_cos + c * step_sin)
     key = turn(unit(acc[:, :HEAD], gain_ref[...]), side_ref[:, COS:SIN], side_ref[:, SIN:AUX])
     kv_ref[:, :HEAD] = key.astype(jnp.bfloat16)
     kv_ref[:, HEAD:] = acc[:, HEAD:].astype(jnp.bfloat16)
@@ -156,17 +156,16 @@
     near, far = pl.BlockSpec(memory_space=pltpu.VMEM), pl.BlockSpec(memory_space=pltpu.HBM)
     return pl.pallas_call(
         keys_kernel,
-        in_specs=[pl.BlockSpec(memory_space=pltpu.SMEM)] + [far] * 3 + [near] * 2,
+        in_specs=[pl.BlockSpec(memory_space=pltpu.SMEM), near] + [far] * 2 + [near] * 2,
         out_specs=[near] * 2,
         out_shape=[
             jax.ShapeDtypeStruct((ROWS, SIDE), jnp.float32),
             jax.ShapeDtypeStruct((ROWS, 2 * HEAD), jnp.bfloat16),
         ],
         scratch_shapes=[
-            pltpu.VMEM((STEPS, ROWS, STEP), jnp.bfloat16),
-            pltpu.VMEM((STEPS, STEP, 2 * HEAD), jnp.bfloat16),
+            pltpu.VMEM((2, STEPS, STEP, HEAD), jnp.bfloat16),
             pltpu.VMEM((ROWS, 2 * HEAD), jnp.float32),
-            pltpu.SemaphoreType.DMA((STEPS, 3)),
+            pltpu.SemaphoreType.DMA((STEPS, 2)),
         ],
         compiler_params=pltpu.CompilerParams(vmem_limit_bytes=16 << 20),
         cost_estimate=pl.CostEstimate(
@@ -315,10 +314,9 @@
 ):
     down = jnp.swapaxes(adapter_down_weight[0], 0, 1)
     index, key_gain = token_adapter_index.reshape(1, ROWS), key_norm_gain.reshape(1, HEAD)
-    (tokens, query_weight, key_weight, value_weight, index, key_gain, packed_prompt_length) = [
+    tokens, query_weight, key_weight, value_weight, key_gain, packed_prompt_length = [
         pltpu.with_memory_space_constraint(v, pltpu.HBM)
-        for v in (tokens, query_weight, key_weight, value_weight, index, key_gain,
-                  packed_prompt_length)
+        for v in (tokens, query_weight, key_weight, value_weight, key_gain, packed_prompt_length)
     ]
     shift = lax.rem(lax.axis_index("tp") * SLICE, 128)
     carried = functools.reduce(
@@ -340,14 +338,14 @@
             double if d in (1, Z - 1) else single, "z", [((i + d) % Z, i) for i in range(Z)])
         for d in NEAR[1:]
     ]
-    *rows, target = pack(index, tokens)
+    *rows, target, held = pack(index, tokens)
     rows = [rows[0]] + [
         lax.ppermute(
             rows[d], "x", [(i, (i + d) % X) for i in range(X)])
         for d in range(1, X)
     ]
     side, kv = project_keys(
-        packed_prompt_length, tokens, key_weight, value_weight,
+        packed_prompt_length, held, key_weight, value_weight,
         key_gain, target)
     query = project_queries(tokens, query_weight)
     kv1, kv0 = [

time: 82.5 us -> 86.7 us (1.051)
  local copies, waits for them, and re-layouts: 0.03 us -> 5.67 us
  Pallas kernels: 21.1 us -> 19.5 us
    unnamed x3 -> x9, local copies, waits for them, and re-layouts: 0.02 us -> 5.66 us
    pallas_call x1, Pallas kernels: 4.6 us -> 3.31 us  [pack(): pl.pallas_call(pack_kernel, in_specs=[pl.BlockSpec(memory_space=pltpu.VME...]
  transfers between devices with their start and end apart: 12 -> 12, of which waited for: 6 -> 6; matrix products, arithmetic and copies ran while one was open for 0% -> 0% of each run, Pallas kernels for 18% -> 15%
where the time goes in v6:
time: 86.7 us; the launch traced here: 86.4 us
  starting transfers between devices  39.3 us (45%)
  waiting for transfers between devices  20.5 us (24%)
  Pallas kernels  19.5 us (22%)
  local copies, waits for them, and re-layouts  5.67 us (7%)
  other arithmetic  1.27 us (1%)
    ppermute x2, starting transfers between devices, layer(): lax.ppermute(carried, ('z', 'tp'), [(a * T + w, (a + w + d) % Z * T + a)...  12.9 us
    ppermute x2, starting transfers between devices, layer(): lax.ppermute(kv, ('x', 'z'), [(i, i + d) for i in range(X * Z - d)])  10.2 us
    ppermute x2, waiting for transfers between devices, layer(): lax.ppermute(kv, ('x', 'z'), [(i, i + d) for i in range(X * Z - d)])  10 us
    ppermute x3, waiting for transfers between devices, layer(): lax.ppermute(rows[d], 'x', [(i, (i + d) % X) for i in range(X)])  6.83 us
    all_to_all x1, starting transfers between devices, layer(): delta = lax.all_to_all(delta.reshape(X * T, CAP, UP), ('x', 'tp'), 0, 0)  5.76 us
    unnamed x9, local copies, waits for them, and re-layouts  5.66 us
    ppermute x4, starting transfers between devices, layer(): lax.ppermute(double if d in (1, Z - 1) else single, 'z', [((i + d) % Z, i...  5.58 us
    pallas_call x1, Pallas kernels, project_keys(): pl.pallas_call(keys_kernel, in_specs=[pl.BlockSpec(memory_space=pltpu.SME...  5.35 us
  transfers between devices with their start and end apart: 12, of which 6 were waited for; matrix products, arithmetic and copies ran while one was open for 0% of the time, Pallas kernels for 15%

profile of v6, /device:TPU:34, one launch (start us, length us, event | category | flops | bytes accessed | tf_op | source)
XLA Modules:
  0.0 86.4 jit_solution(9291310974870971697)
XLA Ops:
  0.0 1.3 %pad_select_fusion = bf16[64,1024]{1,0:T(8,128)(2,1)S(1)} fusion(bf16[64,256]{1,0:T(8,128)(2,1)} %bitcast.13, bf16[64,672]{1,0:T(8,128)(2,1)} %bitcast.12, pred[]{:T(512)S(6)} %eq.11, pred[]{:T(512)S(6)} %eq.10, pred[]{:T(512)S(6)} %eq.9, pred[1024]{0:T(1024)(128)(4,1)S(1)} %iota_compare_fusion), kind=kLoop, calls=%fused_computation | loop fusion | flops 262144 | bytes 250883 | tf_op jit(solution)/shard_map/jit(_where)/select_n | solution.py:326
  1.3 1.9 %collective-permute-start.3 = (bf16[64,1024]{1,0:T(8,128)(2,1)S(1)}, bf16[64,1024]{1,0:T(8,128)(2,1)S(1)}, u32[]{:S(2)}, u32[]{:S(2)}) collective-permute-start(bf16[64,1024]{1,0:T(8,128)(2,1)S(1)} %pad_select_fusion), channel_id=1, source_target_pairs={{0,0},{1,8},{2,16},{3,24},{4,32},{5,40},{6,48},{7,56},{8,9},{9,17}... | collective-permute-start | bytes 393224 | tf_op jit(solution)/shard_map/ppermute | solution.py:330
  3.2 11.0 %collective-permute-start.4 = (bf16[64,1024]{1,0:T(8,128)(2,1)S(1)}, bf16[64,1024]{1,0:T(8,128)(2,1)S(1)}, u32[]{:S(2)}, u32[]{:S(2)}) collective-permute-start(bf16[64,1024]{1,0:T(8,128)(2,1)S(1)} %pad_select_fusion), channel_id=1, source_target_pairs={{0,32},{1,40},{2,48},{3,56},{4,0},{5,8},{6,16},{7,24},{8,41},{9,49... | collective-permute-start | bytes 393224 | tf_op jit(solution)/shard_map/ppermute | solution.py:330
  14.2 0.0 copy-start.2
  14.2 0.7 copy-done.2
  14.9 3.3 %pack.1 = (bf16[32,5376]{1,0:T(8,128)(2,1)S(1)}, bf16[32,5376]{1,0:T(8,128)(2,1)S(1)}, bf16[32,5376]{1,0:T(8,128)(2,1)S(1)}, bf16[32,5376]{1,0:T(8,128)(2,1)S(1)...) custom-call(s32[1,512]{1,0:T(1,128)S(1)} %bitcast.10, bf16[512,5376]{1,0:T(8,128)(2,1)} %x_ref.3), custom_call_target="tpu_custom_call" | custom-call | flops 704643072 | bytes 7000000 | tf_op jit(solution)/shard_map/pack/pallas_call | solution.py:64
  18.2 2.4 %copy-done = bf16[7,512,768]{2,1,0:T(8,128)(2,1)} copy-done((bf16[7,512,768]{2,1,0:T(8,128)(2,1)}, bf16[7,512,768]{2,1,0:T(8,128)(2,1)S(1)}, u32[]{:S(2)}) %copy-start) | copy-done | bytes 5505048
  20.6 1.5 %collective-permute-start = (bf16[32,5376]{1,0:T(8,128)(2,1)S(1)}, bf16[32,5376]{1,0:T(8,128)(2,1)S(1)}, u32[]{:S(2)}, u32[]{:S(2)}) collective-permute-start(bf16[32,5376]{1,0:T(8,128)(2,1)S(1)} %get-tuple-element.14), channel_id=1, source_target_pairs={{0,64},{64,128},{128,192},{192,0},{1,65},{65,129},{129,193},{193,1... | collective-permute-start | bytes 1032200 | tf_op jit(solution)/shard_map/ppermute | solution.py:343
  22.1 1.1 %collective-permute-start.1 = (bf16[32,5376]{1,0:T(8,128)(2,1)S(1)}, bf16[32,5376]{1,0:T(8,128)(2,1)S(1)}, u32[]{:S(2)}, u32[]{:S(2)}) collective-permute-start(bf16[32,5376]{1,0:T(8,128)(2,1)S(1)} %get-tuple-element.15), channel_id=1, source_target_pairs={{0,128},{64,192},{128,0},{192,64},{1,129},{65,193},{129,1},{193,65... | collective-permute-start | bytes 1032200 | tf_op jit(solution)/shard_map/ppermute | solution.py:343
  23.2 0.0 collective-permute-done.3
  23.2 0.1 collective-permute-start.7
  23.4 2.8 %collective-permute-start.8 = (bf16[64,1024]{1,0:T(8,128)(2,1)S(1)}, bf16[64,1024]{1,0:T(8,128)(2,1)S(1)}, u32[]{:S(2)}, u32[]{:S(2)}) collective-permute-start(bf16[64,1024]{1,0:T(8,128)(2,1)S(1)} %collective-permute-done.3), channel_id=1, source_target_pairs={{48,0},{56,8},{0,16},{8,24},{16,32},{24,40},{32,48},{40,56},{49,1}... | collective-permute-start | bytes 393224 | tf_op jit(solution)/shard_map/ppermute | solution.py:337
  26.2 0.0 collective-permute-done.4
  26.2 2.2 %collective-permute-start.2 = (bf16[32,5376]{1,0:T(8,128)(2,1)S(1)}, bf16[32,5376]{1,0:T(8,128)(2,1)S(1)}, u32[]{:S(2)}, u32[]{:S(2)}) collective-permute-start(bf16[32,5376]{1,0:T(8,128)(2,1)S(1)} %get-tuple-element.16), channel_id=1, source_target_pairs={{0,192},{64,0},{128,64},{192,128},{1,193},{65,1},{129,65},{193,129... | collective-permute-start | bytes 1032200 | tf_op jit(solution)/shard_map/ppermute | solution.py:343
  28.4 1.3 %collective-permute-done.7.refs_7_ = bf16[64,1024]{1,0:T(8,128)(2,1)S(1)} collective-permute-done((bf16[64,1024]{1,0:T(8,128)(2,1)S(1)}, bf16[64,1024]{1,0:T(8,128)(2,1)S(1)}, u32[]{:S(2)}, u32[]{:S(2)}) %collective-permute-start.7) | collective-permute-done | bytes 131104 | tf_op jit(solution)/shard_map/ppermute | solution.py:337
  29.7 2.6 %collective-permute-start.5 = (bf16[128,1024]{1,0:T(8,128)(2,1)S(1)}, bf16[128,1024]{1,0:T(8,128)(2,1)S(1)}, u32[]{:S(2)}, u32[]{:S(2)}) collective-permute-start(bf16[128,1024]{1,0:T(8,128)(2,1)S(1)} %constant_dynamic-update-slice_fusion.refs_4_), channel_id=1, source_target_pairs={{8,0},{16,8},{24,16},{32,24},{40,32},{48,40},{56,48},{0,56},{9,1},... | collective-permute-start | bytes 786440 | tf_op jit(solution)/shard_map/ppermute | solution.py:337
  32.3 1.5 %collective-permute-done.8.refs_8_ = bf16[64,1024]{1,0:T(8,128)(2,1)S(1)} collective-permute-done((bf16[64,1024]{1,0:T(8,128)(2,1)S(1)}, bf16[64,1024]{1,0:T(8,128)(2,1)S(1)}, u32[]{:S(2)}, u32[]{:S(2)}) %collective-permute-start.8) | collective-permute-done | bytes 131104 | tf_op jit(solution)/shard_map/ppermute | solution.py:337
  33.9 0.0 collective-permute-start.6
  33.9 0.0 collective-permute-done.refs_1_
  33.9 0.7 collective-permute-done.1.refs_2_
  34.6 6.1 %collective-permute-done.2.refs_3_ = bf16[32,5376]{1,0:T(8,128)(2,1)S(1)} collective-permute-done((bf16[32,5376]{1,0:T(8,128)(2,1)S(1)}, bf16[32,5376]{1,0:T(8,128)(2,1)S(1)}, u32[]{:S(2)}, u32[]{:S(2)}) %collective-permute-start.2) | collective-permute-done | bytes 344096 | tf_op jit(solution)/shard_map/ppermute | solution.py:343
  40.7 0.9 collective-permute-done.6.refs_6_
  41.6 2.0 %adapt.1 = bf16[4,8,32,256]{3,2,1,0:T(8,128)(2,1)} custom-call(bf16[32,5376]{1,0:T(8,128)(2,1)S(1)} %get-tuple-element.13.refs_0_, bf16[32,5376]{1,0:T(8,128)(2,1)S(1)} %collective-permute-done.refs_1_, bf16[32,5376]{1,0:T(8,128)(2,1)S(1)} %collective-permute-done.1.refs_2_, bf16[32,5376]{1,0:T(8,128)(2,1)S(1)} %collective-permute-done.2.refs_3_, ...), custom_call_target="tpu_custom_call" | custom-call | flops 121634816 | bytes 3000000 | tf_op jit(solution)/shard_map/adapt/pallas_call | solution.py:241
  43.6 5.8 %all-to-all-start = ((bf16[32,32,256]{2,1,0:T(8,128)(2,1)}), bf16[32,32,256]{2,1,0:T(8,128)(2,1)S(1)}, u32[]{:S(2)}, u32[]{:S(2)}) async-start(bf16[32,32,256]{2,1,0:T(8,128)(2,1)} %bitcast.5), calls=%async_computation | async-start | bytes 1048576 | tf_op jit(solution)/shard_map/all_to_all | solution.py:357
  49.4 2.6 %copy-done.1 = bf16[7,512,768]{2,1,0:T(8,128)(2,1)S(1)} copy-done((bf16[7,512,768]{2,1,0:T(8,128)(2,1)S(1)}, bf16[7,512,768]{2,1,0:T(8,128)(2,1)}, u32[]{:S(2)}) %copy-start.1) | copy-done | bytes 5505048
  52.0 5.3 %project_keys.1 = (f32[512,384]{1,0:T(8,128)S(1)}, bf16[512,256]{1,0:T(8,128)(2,1)S(1)}) custom-call(s32[16]{0:T(128)} %lens_ref.1, bf16[7,512,768]{2,1,0:T(8,128)(2,1)S(1)} %copy-done.1, bf16[5376,128]{1,0:T(8,128)(2,1)} %wk_ref.1, bf16[5376,128]{1,0:T(8,128)(2,1)} %wv_ref.1, f32[1,128]{1,0:T(1,128)} %bitcast.14, s32[1,512]{1,0:T(1,128)S(1)} %get-tuple-element.18.target_ref), custom_call_target="tpu_custom_call" | custom-call | flops 1409286144 | bytes 9500000 | tf_op jit(solution)/shard_map/project_keys/pallas_call | solution.py:157
  57.3 0.0 copy-start.3
  57.3 3.1 %collective-permute-start.10 = (bf16[512,256]{1,0:T(8,128)(2,1)S(1)}, bf16[512,256]{1,0:T(8,128)(2,1)S(1)}, u32[]{:S(2)}, u32[]{:S(2)}) collective-permute-start(bf16[512,256]{1,0:T(8,128)(2,1)S(1)} %get-tuple-element.20.kv2), channel_id=1, source_target_pairs={{0,8},{8,16},{16,24},{24,32},{32,40},{40,48},{48,56},{56,64},{64,7... | collective-permute-start | bytes 786440 | tf_op jit(solution)/shard_map/ppermute | solution.py:352
  60.5 7.1 %collective-permute-start.9 = (bf16[512,256]{1,0:T(8,128)(2,1)S(1)}, bf16[512,256]{1,0:T(8,128)(2,1)S(1)}, u32[]{:S(2)}, u32[]{:S(2)}) collective-permute-start(bf16[512,256]{1,0:T(8,128)(2,1)S(1)} %get-tuple-element.20.kv2), channel_id=1, source_target_pairs={{0,16},{8,24},{16,32},{24,40},{32,48},{40,56},{48,64},{56,72},{64,... | collective-permute-start | bytes 786440 | tf_op jit(solution)/shard_map/ppermute | solution.py:352
  67.5 4.5 %project_queries.1.q_ref = f32[512,256]{1,0:T(8,128)S(1)} custom-call(bf16[512,5376]{1,0:T(8,128)(2,1)} %x_ref.3, bf16[5376,256]{1,0:T(8,128)(2,1)} %wq_ref.1), custom_call_target="tpu_custom_call" | custom-call | flops 1409286144 | bytes 8800000 | tf_op jit(solution)/shard_map/project_queries/pallas_call | solution.py:196
  72.1 10.0 %collective-permute-done.9.kv0 = bf16[512,256]{1,0:T(8,128)(2,1)S(1)} collective-permute-done((bf16[512,256]{1,0:T(8,128)(2,1)S(1)}, bf16[512,256]{1,0:T(8,128)(2,1)S(1)}, u32[]{:S(2)}, u32[]{:S(2)}) %collective-permute-start.9) | collective-permute-done | bytes 262176 | tf_op jit(solution)/shard_map/ppermute | solution.py:352
  82.1 4.3 %attend.1 = bf16[512,256]{1,0:T(8,128)(2,1)} custom-call(bf16[1024,256]{1,0:T(8,128)(2,1)S(1)} %bitcast.9, f32[512,256]{1,0:T(8,128)S(1)} %project_queries.1.q_ref, f32[512,384]{1,0:T(8,128)S(1)} %get-tuple-element.19.side_ref, bf16[512,256]{1,0:T(8,128)(2,1)S(1)} %collective-permute-done.9.kv0, bf16[512,256]{1,0:T(8,128)(2,1)S(1)} %collective-permute-done.10.kv1, ...), custom_call_target="tpu_custom_call" | custom-call | flops 671088640 | bytes 4000000 | tf_op jit(solution)/shard_map/attend/pallas_call | solution.py:295
  (9 shorter events, 0.0 us)
Async XLA Ops:
  1.3 22.0 %collective-permute-start.3 = (bf16[64,1024]{1,0:T(8,128)(2,1)S(1)}, bf16[64,1024]{1,0:T(8,128)(2,1)S(1)}, u32[]{:S(2)}, u32[]{:S(2)}) collective-permute-start(bf16[64,1024]{1,0:T(8,128)(2,1)S(1)} %pad_select_fusion), channel_id=1, source_target_pairs={{0,0},{1,8},{2,16},{3,24},{4,32},{5,40},{6,48},{7,56},{8,9},{9,17}... | collective-permute-start | bytes 393224 | tf_op jit(solution)/shard_map/ppermute | solution.py:330
  3.2 23.0 %collective-permute-start.4 = (bf16[64,1024]{1,0:T(8,128)(2,1)S(1)}, bf16[64,1024]{1,0:T(8,128)(2,1)S(1)}, u32[]{:S(2)}, u32[]{:S(2)}) collective-permute-start(bf16[64,1024]{1,0:T(8,128)(2,1)S(1)} %pad_select_fusion), channel_id=1, source_target_pairs={{0,32},{1,40},{2,48},{3,56},{4,0},{5,8},{6,16},{7,24},{8,41},{9,49... | collective-permute-start | bytes 393224 | tf_op jit(solution)/shard_map/ppermute | solution.py:330
  14.2 0.7 copy-start.2
  18.2 2.4 %copy-start = (bf16[7,512,768]{2,1,0:T(8,128)(2,1)}, bf16[7,512,768]{2,1,0:T(8,128)(2,1)S(1)}, u32[]{:S(2)}) copy-start(bf16[7,512,768]{2,1,0:T(8,128)(2,1)S(1)} %get-tuple-element.17.x_held) | copy-start | bytes 16515076
  20.6 13.3 %collective-permute-start = (bf16[32,5376]{1,0:T(8,128)(2,1)S(1)}, bf16[32,5376]{1,0:T(8,128)(2,1)S(1)}, u32[]{:S(2)}, u32[]{:S(2)}) collective-permute-start(bf16[32,5376]{1,0:T(8,128)(2,1)S(1)} %get-tuple-element.14), channel_id=1, source_target_pairs={{0,64},{64,128},{128,192},{192,0},{1,65},{65,129},{129,193},{193,1... | collective-permute-start | bytes 1032200 | tf_op jit(solution)/shard_map/ppermute | solution.py:343
  22.1 12.5 %collective-permute-start.1 = (bf16[32,5376]{1,0:T(8,128)(2,1)S(1)}, bf16[32,5376]{1,0:T(8,128)(2,1)S(1)}, u32[]{:S(2)}, u32[]{:S(2)}) collective-permute-start(bf16[32,5376]{1,0:T(8,128)(2,1)S(1)} %get-tuple-element.15), channel_id=1, source_target_pairs={{0,128},{64,192},{128,0},{192,64},{1,129},{65,193},{129,1},{193,65... | collective-permute-start | bytes 1032200 | tf_op jit(solution)/shard_map/ppermute | solution.py:343
  23.2 6.5 %collective-permute-start.7 = (bf16[64,1024]{1,0:T(8,128)(2,1)S(1)}, bf16[64,1024]{1,0:T(8,128)(2,1)S(1)}, u32[]{:S(2)}, u32[]{:S(2)}) collective-permute-start(bf16[64,1024]{1,0:T(8,128)(2,1)S(1)} %collective-permute-done.3), channel_id=1, source_target_pairs={{16,0},{24,8},{32,16},{40,24},{48,32},{56,40},{0,48},{8,56},{17,1}... | collective-permute-start | bytes 393224 | tf_op jit(solution)/shard_map/ppermute | solution.py:337
  23.4 10.5 %collective-permute-start.8 = (bf16[64,1024]{1,0:T(8,128)(2,1)S(1)}, bf16[64,1024]{1,0:T(8,128)(2,1)S(1)}, u32[]{:S(2)}, u32[]{:S(2)}) collective-permute-start(bf16[64,1024]{1,0:T(8,128)(2,1)S(1)} %collective-permute-done.3), channel_id=1, source_target_pairs={{48,0},{56,8},{0,16},{8,24},{16,32},{24,40},{32,48},{40,56},{49,1}... | collective-permute-start | bytes 393224 | tf_op jit(solution)/shard_map/ppermute | solution.py:337
  26.2 14.6 %collective-permute-start.2 = (bf16[32,5376]{1,0:T(8,128)(2,1)S(1)}, bf16[32,5376]{1,0:T(8,128)(2,1)S(1)}, u32[]{:S(2)}, u32[]{:S(2)}) collective-permute-start(bf16[32,5376]{1,0:T(8,128)(2,1)S(1)} %get-tuple-element.16), channel_id=1, source_target_pairs={{0,192},{64,0},{128,64},{192,128},{1,193},{65,1},{129,65},{193,129... | collective-permute-start | bytes 1032200 | tf_op jit(solution)/shard_map/ppermute | solution.py:343
  29.7 11.0 %collective-permute-start.5 = (bf16[128,1024]{1,0:T(8,128)(2,1)S(1)}, bf16[128,1024]{1,0:T(8,128)(2,1)S(1)}, u32[]{:S(2)}, u32[]{:S(2)}) collective-permute-start(bf16[128,1024]{1,0:T(8,128)(2,1)S(1)} %constant_dynamic-update-slice_fusion.refs_4_), channel_id=1, source_target_pairs={{8,0},{16,8},{24,16},{32,24},{40,32},{48,40},{56,48},{0,56},{9,1},... | collective-permute-start | bytes 786440 | tf_op jit(solution)/shard_map/ppermute | solution.py:337
  33.9 7.7 %collective-permute-start.6 = (bf16[128,1024]{1,0:T(8,128)(2,1)S(1)}, bf16[128,1024]{1,0:T(8,128)(2,1)S(1)}, u32[]{:S(2)}, u32[]{:S(2)}) collective-permute-start(bf16[128,1024]{1,0:T(8,128)(2,1)S(1)} %constant_dynamic-update-slice_fusion.refs_4_), channel_id=1, source_target_pairs={{56,0},{0,8},{8,16},{16,24},{24,32},{32,40},{40,48},{48,56},{57,1}... | collective-permute-start | bytes 786440 | tf_op jit(solution)/shard_map/ppermute | solution.py:337
  43.6 38.4 %all-to-all-start = ((bf16[32,32,256]{2,1,0:T(8,128)(2,1)}), bf16[32,32,256]{2,1,0:T(8,128)(2,1)S(1)}, u32[]{:S(2)}, u32[]{:S(2)}) async-start(bf16[32,32,256]{2,1,0:T(8,128)(2,1)} %bitcast.5), calls=%async_computation | async-start | bytes 1048576 | tf_op jit(solution)/shard_map/all_to_all | solution.py:357
  49.4 2.6 %copy-start.1 = (bf16[7,512,768]{2,1,0:T(8,128)(2,1)S(1)}, bf16[7,512,768]{2,1,0:T(8,128)(2,1)}, u32[]{:S(2)}) copy-start(bf16[7,512,768]{2,1,0:T(8,128)(2,1)} %copy-done) | copy-start | bytes 16515076
  57.3 24.7 %copy-start.3 = (f32[128]{0:T(128)S(1)}, f32[128]{0:T(128)}, u32[]{:S(2)}) copy-start(f32[128]{0:T(128)} %param.14) | copy-start | bytes 1540
  57.3 14.7 %collective-permute-start.10 = (bf16[512,256]{1,0:T(8,128)(2,1)S(1)}, bf16[512,256]{1,0:T(8,128)(2,1)S(1)}, u32[]{:S(2)}, u32[]{:S(2)}) collective-permute-start(bf16[512,256]{1,0:T(8,128)(2,1)S(1)} %get-tuple-element.20.kv2), channel_id=1, source_target_pairs={{0,8},{8,16},{16,24},{24,32},{32,40},{40,48},{48,56},{56,64},{64,7... | collective-permute-start | bytes 786440 | tf_op jit(solution)/shard_map/ppermute | solution.py:352
  60.5 21.6 %collective-permute-start.9 = (bf16[512,256]{1,0:T(8,128)(2,1)S(1)}, bf16[512,256]{1,0:T(8,128)(2,1)S(1)}, u32[]{:S(2)}, u32[]{:S(2)}) collective-permute-start(bf16[512,256]{1,0:T(8,128)(2,1)S(1)} %get-tuple-element.20.kv2), channel_id=1, source_target_pairs={{0,16},{8,24},{16,32},{24,40},{32,48},{40,56},{48,64},{56,72},{64,... | collective-permute-start | bytes 786440 | tf_op jit(solution)/shard_map/ppermute | solution.py:352
